TPU v7x, 32 devices: a whole 2x2x4 slice. The times are simulated.
32 devices in a mesh: fsdp: 4 (over y, x), ctx: 8 (over z, core).
Axes of the slice: x: 2, y: 2, z: 4, core: 2. Of those that a mesh axis runs over, the one named last changes fastest.
Arguments:
- block_input: bfloat16 [8, 1024, 768], P('fsdp', 'ctx'), may hold values from -6 to 6
- attn_gain: bfloat16 [768], P('fsdp'), may hold values from 0.5 to 1.5
- w_qkv: bfloat16 [768, 2304], P('fsdp'), may hold values from -0.21875 to 0.21875
- w_out: bfloat16 [768, 768], P('fsdp'), may hold values from -0.875 to 0.875
- ffn_gain: bfloat16 [768], P('fsdp'), may hold values from 0.5 to 1.5
- w_router: bfloat16 [768, 8], P('fsdp'), may hold values from -0.21875 to 0.21875
- w_gate: bfloat16 [768, 4, 2048], P('fsdp'), may hold values from -0.21875 to 0.21875
- w_up: bfloat16 [768, 4, 2048], P('fsdp'), may hold values from -0.21875 to 0.21875
- w_down: bfloat16 [768, 4, 2048], P('fsdp'), may hold values from -0.5 to 0.5
- const_mix: bfloat16 [768, 4], P('fsdp'), may hold values from -0.21875 to 0.21875
- const_vec: bfloat16 [768, 2], P('fsdp'), may hold values from -8 to 8
- prev_logits: float32 [8, 1024, 8], P('fsdp', 'ctx'), may hold values from -8 to 8
- routes: int32 [8, 1024, 2], P('fsdp', 'ctx'), may hold values from 0 to 7, all different within a row; in each aligned block of 128 rows (0 to 127, 128 to 255, ..., all dimensions but the last counted through in order) at most 48 rows name the same one
- doc_ids: int32 [8, 1024], P('fsdp'), may hold values from 0 to 3, never falling along the last dimension, each value on 1 to 512 neighbouring positions
- d_out: bfloat16 [8, 1024, 768], P('fsdp', 'ctx'), may hold values from -6 to 6
Outputs:
- out_block: bfloat16 [8, 1024, 768], P('fsdp', 'ctx')
- grad_x: float32 [8, 1024, 768], P('fsdp', 'ctx')
- grad_prev_logits: float32 [8, 1024, 8], P('fsdp', 'ctx')
- grad_attn_gain: float32 [768], P('fsdp')
- grad_w_qkv: float32 [768, 2304], P('fsdp')
- grad_w_out: float32 [768, 768], P('fsdp')
- grad_ffn_gain: float32 [768], P('fsdp')
- grad_w_router: float32 [768, 8], P('fsdp')
- grad_w_gate: float32 [768, 4, 2048], P('fsdp')
- grad_w_up: float32 [768, 4, 2048], P('fsdp')
- grad_w_down: float32 [768, 4, 2048], P('fsdp')
- grad_const_mix: float32 [768, 4], P('fsdp')
- grad_const_vec: float32 [768, 2], P('fsdp')
Inputs may be any that keep to these rules, and one draw needn't show every extreme that they name: `routes`: each token names two different experts. Within each aligned block of 128 positions of a sequence, no expert is named by more than 48 of the block's pairs, a bound that some block reaches. `doc_ids`: along each sequence the document number never falls, all 4 documents occur, and each spans at most 512 positions.
All inputs are finite; a program needn't handle non-finite values.
Results may differ from a plain program's by a relative error of at most 0.022.
Values may be sent and summed in bfloat16 or wider, within the bound.
No kernel may reach another device: no remote copies, remote signals or barrier semaphores. Data moves between devices by JAX's collectives and lax.ppermute only.
A program may use at most 384 MiB of HBM per device.

v0:
```python
import functools
import math

import jax
import jax.numpy as jnp
from jax import lax
from jax.experimental import pallas as pl
from jax.experimental.pallas import tpu as pltpu
from jax.sharding import PartitionSpec as P


H = 12
HD = 64
NF = 4
NC = 2
NE = 8
TOP = 2
MOST = 48
BF = jnp.bfloat16
F32 = jnp.float32


def dot(a, b, dims):
    return lax.dot_general(a, b, (dims, ((), ())), preferred_element_type=F32)


def mm(a, b):
    return dot(a, b, ((1,), (0,)))


def mm_nt(a, b):
    return dot(a, b, ((1,), (1,)))


def mm_tn(a, b):
    return dot(a, b, ((0,), (0,)))


def halves_swapped(t):
    half = t.shape[-1] // 2
    return jnp.concatenate([t[:, half:], t[:, :half]], axis=-1)


VMEM = pl.BlockSpec(memory_space=pltpu.VMEM)
SMEM = pl.BlockSpec(memory_space=pltpu.SMEM)


GRANTS = {
    "pack": 3,
    "grad_rows": 3,
    "order": 8,
    "attend": 14,
    "dispatch": 6,
    "experts0": 24,
    "experts": 14,
    "combine": 16,
    "expert_grads": 18,
    "attend_back": 20,
    "pair": 3,
    "input_grad": 6,
    "place": 13,
    "qkv_grad": 5,
}


def params(name, long=False):
    return pltpu.CompilerParams(vmem_limit_bytes=(56 if long else GRANTS[name]) << 20)


def norm_of(tile):
    return lax.rsqrt(jnp.mean(tile * tile, axis=-1, keepdims=True) + 1e-05)


def split(t):
    high = t.astype(BF)
    return high, (t - high.astype(F32)).astype(BF)


def pack_kernel(dims, meta, w_qkv, gain_a, gain_f, router, mix, vec, first):
    F, D, G, hpd = dims
    hw = hpd * HD
    d_local = D // F
    group = lax.rem(meta[3], G)
    for g in range(G):
        width = max(0, min(hw, H * HD - g * hw))

        @pl.when(group == g)
        def _():
            for part in range(3):
                if width:
                    first[:d_local, part * hw : part * hw + width] = w_qkv[
                        :, part * H * HD + g * hw : part * H * HD + g * hw + width
                    ]
                if width < hw:
                    first[:d_local, part * hw + width : (part + 1) * hw] = jnp.zeros(
                        (d_local, hw - width), BF
                    )

    rows = [t[...].astype(F32) for t in (gain_a, gain_f, router, mix, vec)]
    first[d_local:, :d_local] = jnp.concatenate(rows, axis=0).astype(BF)
    if d_local < 3 * hw:
        first[d_local:, d_local:] = jnp.zeros((16, 3 * hw - d_local), BF)


def grad_rows_kernel(dims, meta, grad, routes, slots, *outs):
    F, S, R, _, expert_of = dims
    table = outs[-1]
    below = lax.broadcasted_iota(jnp.int32, (R, R), 0)
    earlier = (below < lax.broadcasted_iota(jnp.int32, (R, R), 1)).astype(F32).astype(BF)
    expert = lax.broadcasted_iota(jnp.int32, (8, R), 0)
    for s in range(S):
        named = [routes[2 * s + w : 2 * s + w + 1, :] for w in range(TOP)]
        hots = [(expert == t).astype(F32) for t in named]
        counts = mm((hots[0] + hots[1]).astype(BF), earlier)
        lines = []
        for w in range(TOP):
            rank = jnp.sum(hots[w] * counts, axis=0, keepdims=True).astype(jnp.int32)
            line = jnp.where(named[w] < NF, named[w] * MOST + rank, -1)
            slots[2 * s + w : 2 * s + w + 1, :] = line
            lines.append(line)
        slot = lax.broadcasted_iota(jnp.int32, (NF * MOST, R), 0)
        picks = (slot == lines[0]) | (slot == lines[1])
        moved = mm(picks.astype(F32).astype(BF), grad[s]).astype(BF)
        for e in range(NF):
            table[e, s * MOST : (s + 1) * MOST, :] = moved[e * MOST : (e + 1) * MOST, :]
    for k in range(F):
        outs[k][...] = table[expert_of(lax.rem(meta[2] + k, F))]


def order_kernel(dims, meta, *refs):
    F = dims
    for k in range(F):
        e = lax.rem(meta[2] + k, F)
        for i in range(3):
            refs[3 + k][i] = refs[i][e]


def attend_kernel(dims, meta, start, cos, sin, *refs):
    Z, F, R, D, L, hpd, block = dims
    hw = hpd * HD
    xs, refs = refs[: 2 * Z], refs[2 * Z :]
    ws, refs = refs[:F], refs[F:]
    normed, weight, small_out, q_out, k_out, v_out, o_out, lse_out = refs[:8]
    pieces, small_s, att_s = refs[8 : 8 + Z], refs[8 + Z], refs[9 + Z]
    z, core, f = meta[0], meta[1], meta[2]
    d_local = D // F
    for k in range(F):
        row = pl.multiple_of(lax.rem(f - k + F, F) * d_local, d_local)
        weight[pl.ds(row, d_local), :] = ws[k][:d_local, :]
        small_s[k] = ws[k][d_local:, :d_local].astype(F32)
    small = jnp.concatenate([small_s[lax.rem(f - i + F, F)] for i in range(F)], axis=1)
    small_out[...] = small
    gain_row = small[0:1, :]
    for k in range(Z):
        for side in range(2):
            at = lax.rem(z - k + Z, Z) * 2 + (core if side == 0 else 1 - core)
            tile = xs[side * Z + k][...].astype(F32)
            row = pl.multiple_of(at * R, R)
            normed[pl.ds(row, R), :] = (tile * norm_of(tile) * gain_row).astype(BF)

    def project(step, carry):
        rows = pl.ds(pl.multiple_of(step * block, block), block)
        mixed = mm(normed[rows, :], weight[...])
        cosine, sine = cos[rows, :], sin[rows, :]
        for h in range(hpd):
            q = mixed[:, h * HD : (h + 1) * HD]
            k = mixed[:, hw + h * HD : hw + (h + 1) * HD]
            v = mixed[:, 2 * hw + h * HD : 2 * hw + (h + 1) * HD]
            q = (q * cosine + halves_swapped(q) * sine).astype(BF)
            q_out[h, rows, :] = (q.astype(F32) * HD ** (-0.5)).astype(BF)
            k_out[h, rows, :] = (k * cosine + halves_swapped(k) * sine).astype(BF)
            v_out[h, rows, :] = v.astype(BF)
        return carry

    lax.fori_loop(0, L // block, project, 0)

    def query_step(qb, carry):
        rows = pl.ds(pl.multiple_of(qb * block, block), block)
        first = start[rows, :]
        q_pos = qb * block + lax.broadcasted_iota(jnp.int32, (block, block), 0)
        column = lax.broadcasted_iota(jnp.int32, (block, block), 1)
        queries = [q_out[h, rows, :] for h in range(hpd)]

        def key_step(kb, state):
            keys = pl.ds(pl.multiple_of(kb * block, block), block)
            k_pos = kb * block + column
            allowed = (k_pos <= q_pos) & (k_pos >= first)
            new = []
            for h in range(hpd):
                high, total, acc = state[h]
                scores = mm_nt(queries[h], k_out[h, keys, :])
                scores = jnp.where(allowed, scores, -1e30)
                top = jnp.maximum(high, jnp.max(scores, axis=-1, keepdims=True))
                scale = jnp.exp(high - top)
                weights = jnp.where(allowed, jnp.exp(scores - top), 0.0)
                total = total * scale + jnp.sum(weights, axis=-1, keepdims=True)
                acc = acc * scale + mm(weights.astype(BF), v_out[h, keys, :])
                new.append((top, total, acc))
            return tuple(new)

        begin = tuple(
            (
                jnp.full((block, 1), -1e30, F32),
                jnp.zeros((block, 1), F32),
                jnp.zeros((block, HD), F32),
            )
            for _ in range(hpd)
        )
        state = lax.fori_loop(meta[4 + qb], qb + 1, key_step, begin)
        outs = []
        for h in range(hpd):
            high, total, acc = state[h]
            out = acc / total
            o_out[h, rows, :] = out
            lse_out[h, rows, :] = high + jnp.log(total)
            outs.append(out.astype(BF))
        whole = jnp.concatenate(outs, axis=-1)
        for part in range(block // R):
            att_s[qb * (block // R) + part] = whole[part * R : (part + 1) * R, :]
        return carry

    lax.fori_loop(0, L // block, query_step, 0)
    for k in range(Z):
        chip = lax.rem(z + k, Z) * 2
        pieces[k][0] = att_s[chip + core]
        pieces[k][1] = att_s[chip + 1 - core]


def piece_at(dims, meta, k, side):
    Z, G = dims
    chip = lax.rem(meta[0] - k + Z, Z)
    group = lax.rem(2 * chip + (meta[1] if side == 0 else 1 - meta[1]), G)
    return lax.div(2 * chip, G), group


def columns_of(prev, routes, s):
    width = prev.shape[2]
    gap = jnp.zeros((2, width), F32)
    tall = jnp.concatenate([gap, prev[s], jnp.zeros((6, width), F32)], axis=0)
    named = routes[2 * s : 2 * s + 2, :].astype(F32)
    named = jnp.concatenate([named, jnp.zeros((6, width), F32)], axis=0)
    return tall.T, named.T.astype(jnp.int32)


def router_parts(logits, prev, routes):
    lane = lax.broadcasted_iota(jnp.int32, logits.shape, 1)
    inside = (lane >= 2) & (lane < 2 + NE)
    shown = jnp.where(inside, logits + prev, -1e30)
    weights = jnp.exp(shown - jnp.max(shown, axis=-1, keepdims=True))
    weights = jnp.where(inside, weights, 0.0)
    router = weights / jnp.sum(weights, axis=-1, keepdims=True)
    hots = [lane == routes[:, w : w + 1] + 2 for w in range(TOP)]
    gates = [jnp.sum(jnp.where(hot, router, 0.0), axis=-1, keepdims=True) for hot in hots]
    return lane, router, hots, gates


def dispatch_kernel(dims, meta, x, small, prev, routes, slots, *refs):
    Z, F, S, R, D, G, hw, expert_of = dims
    atts, refs = refs[: 2 * Z], refs[2 * Z :]
    ws, refs = refs[:F], refs[F:]
    hidden, w_full, toks, table = refs[0], refs[1], refs[2:-1], refs[-1]

    def att(k, side):
        return atts[k][0] if side == 0 else atts[Z + k][...]

    f = meta[2]
    d_local = D // F
    if G * hw > D:
        w_full[D:, :] = jnp.zeros((G * hw - D, D), BF)
    for k in range(F):
        row = pl.multiple_of(lax.rem(f - k + F, F) * d_local, d_local)
        w_full[pl.ds(row, d_local), :] = ws[k][...]
    for s in range(S):
        hidden[s * R : (s + 1) * R, :] = x[s].astype(F32)
    for k in range(Z):
        for side in range(2):
            seq, group = piece_at((Z, G), meta, k, side)
            rows = pl.ds(pl.multiple_of(seq * R, R), R)
            heads = pl.ds(pl.multiple_of(group * hw, hw), hw)
            hidden[rows, :] += mm(att(k, side), w_full[heads, :])
    gain = small[1:2, :]
    small_low = small[...].astype(BF)
    for s in range(S):
        at = slice(s * R, (s + 1) * R)
        tile = hidden[at, :]
        unit_low = (tile * norm_of(tile) * gain).astype(BF)
        logits = mm_nt(unit_low, small_low)
        _, _, _, gates = router_parts(logits, *columns_of(prev, routes, s))
        slot = lax.broadcasted_iota(jnp.int32, (NF * MOST, R), 0)
        picks = [
            (slot == slots[2 * s + w : 2 * s + w + 1, :]).astype(F32).astype(BF)
            for w in range(TOP)
        ]
        packed = mm(picks[0] + picks[1], unit_low).astype(BF)
        wide = lax.broadcasted_iota(jnp.int32, (R, 128), 1)
        columns = jnp.zeros((NF * MOST, 128), F32)
        for w in range(TOP):
            high, low = split(gates[w])
            both = jnp.where(
                wide == 0, high.astype(F32), jnp.where(wide == 1, low.astype(F32), 0.0)
            )
            columns = columns + mm(picks[w], both.astype(BF))
        for e in range(NF):
            to = slice(s * MOST, (s + 1) * MOST)
            table[e, to, :D] = packed[e * MOST : (e + 1) * MOST, :]
            table[e, to, D:] = columns[e * MOST : (e + 1) * MOST, :].astype(BF)
    for k in range(F):
        toks[k][...] = table[expert_of(lax.rem(f + k, F))]


def ffn_kernel(dims, own, meta, rows_a, rows_b, g_a, g_b, *refs):
    F, D = dims
    n = rows_a.shape[0]
    ws, refs = refs[:F], refs[F:]
    (inner_out, gate_out, up_out, xt_out, drt_out), refs = refs[:5], refs[5:]
    if own:
        mine_out, theirs_out, x_s, dr_s, w_s, acc = refs
    else:
        x_s, dr_s, w_s = refs
    step = pl.program_id(0)
    d_local = D // F

    @pl.when(step == 0)
    def _():
        for i, (rows, g) in enumerate(((rows_a, g_a), (rows_b, g_b))):
            at = slice(i * n, (i + 1) * n)
            x_s[at, :] = rows[:, :D]
            xt_out[:, at] = rows[:, :D].T
            gate = rows[:, D : D + 1].astype(F32) + rows[:, D + 1 : D + 2].astype(F32)
            dr = (gate * g[...].astype(F32)).astype(BF)
            dr_s[at, :] = dr
            drt_out[:, at] = dr.T

    for k in range(F):
        at = pl.ds(pl.multiple_of(lax.rem(meta[2] - k + F, F) * d_local, d_local), d_local)
        for i in range(3):
            w_s[i, at, :] = ws[k][i]
    piece = n // 2
    for r in range(4):
        rows = slice(r * piece, (r + 1) * piece)
        gate_act = mm(x_s[rows, :], w_s[0])
        up_act = mm(x_s[rows, :], w_s[1])
        inner_grad = mm(dr_s[rows, :], w_s[2])
        sig = 0.5 * jnp.tanh(0.5 * gate_act) + 0.5
        act = gate_act * sig
        inner_out[rows, :] = (act * up_act).astype(BF)
        gate_out[rows, :] = (inner_grad * up_act * (sig + act * (1.0 - sig))).astype(BF)
        up_out[rows, :] = (inner_grad * act).astype(BF)
    if own:
        result = mm_nt(inner_out[...], w_s[2])
        packed = mm_nt(gate_out[...], w_s[0]) + mm_nt(up_out[...], w_s[1])

        @pl.when(step == 0)
        def _():
            acc[0] = result
            acc[1] = packed

        @pl.when(step > 0)
        def _():
            acc[0] += result
            acc[1] += packed

        @pl.when(step == pl.num_programs(0) - 1)
        def _():
            mine_out[...] = acc[:, :n, :]
            theirs_out[...] = acc[:, n:, :].astype(BF)


def weight_kernel(dims, meta, *refs):
    F, D, Z = dims
    planes, refs = [refs[5 * p : 5 * p + 5] for p in range(Z)], refs[5 * Z :]
    outs, (acc,) = refs[:F], refs[F:]
    d_local = D // F
    for i, (left, right) in enumerate(((3, 1), (3, 2), (4, 0))):
        total = mm(planes[0][left][...], planes[0][right][...])
        for p in range(1, Z):
            total = total + mm(planes[p][left][...], planes[p][right][...])
        acc[i] = total.astype(BF)
    for k in range(F):
        at = pl.ds(pl.multiple_of(lax.rem(meta[2] + k, F) * d_local, d_local), d_local)
        for i in range(3):
            outs[k][i] = acc[i, at, :]


def combine_kernel(dims, meta, hidden, grad, small, prev, routes, slots, *refs):
    Z, F, S, R, D, G, hw, per, _ = dims
    rets, refs = refs[:F], refs[F:]
    atts, refs = refs[: 2 * Z], refs[2 * Z :]
    w_full, refs = refs[0], refs[1:]
    out_block, dh_out, prev_out, refs = refs[0], refs[1], refs[2], refs[3:]
    das, refs = refs[:Z], refs[Z:]
    payloads, refs = refs[:F], refs[F:]
    back_s, gw_s, dproj_s, rows_s = refs

    def att(k, side):
        return atts[k][0] if side == 0 else atts[Z + k][...]

    f = meta[2]
    d_local = D // F
    for k in range(F):
        back_s[lax.rem(f + k, F)] = rets[k][...]
    gain = small[1:2, :]
    small_all = small[...]
    small_low = small_all.astype(BF)
    small_grads = jnp.zeros((16, D), F32)
    gain_grad = jnp.zeros((1, D), F32)
    for s in range(S):
        at = slice(s * R, (s + 1) * R)
        tile = hidden[at, :]
        factor = norm_of(tile)
        normal = tile * factor
        unit = normal * gain
        unit_low = unit.astype(BF)
        logits = mm_nt(unit_low, small_low)
        before, route = columns_of(prev, routes, s)
        lane, router, hots, gates = router_parts(logits, before, route)
        g_low = grad[s]
        g = g_low.astype(F32)

        def column(t, index):
            return jnp.sum(jnp.where(lane == index, t, 0.0), axis=-1, keepdims=True)

        shares = []
        for i in range(NC):
            a, b = column(logits, 10 + 2 * i), column(logits, 11 + 2 * i)
            top = jnp.maximum(a, b)
            ea, eb = jnp.exp(a - top), jnp.exp(b - top)
            shares.append((ea / (ea + eb), eb / (ea + eb)))
        back = []
        for part in range(2):
            experts = []
            for e in range(NF):
                to = slice(s * MOST, (s + 1) * MOST)
                total = back_s[e * per, part, to, :]
                for j in range(1, per):
                    total = total.astype(F32) + back_s[e * per + j, part, to, :].astype(F32)
                experts.append(total.astype(BF))
            back.append(jnp.concatenate(experts, axis=0))
        slot = lax.broadcasted_iota(jnp.int32, (NF * MOST, R), 0)
        picks = [
            (slot == slots[2 * s + w : 2 * s + w + 1, :]).astype(F32).astype(BF)
            for w in range(TOP)
        ]
        values = [mm_tn(picks[w], back[0]) for w in range(TOP)]
        unit_grad = mm_tn(picks[0] + picks[1], back[1])
        ug = jnp.sum(unit * g, axis=-1, keepdims=True)
        vg_all = mm_nt(g_low, small_low)
        vg = [column(vg_all, 14 + i) for i in range(NC)]

        def named(w, e):
            return (route[:, w : w + 1] == e).astype(F32)

        gate_grads = []
        coef_unit = jnp.zeros((R, 1), F32)
        for w in range(TOP):
            total = jnp.sum(g * values[w], axis=-1, keepdims=True) + named(w, NF + 1) * ug
            coef_unit = coef_unit + gates[w] * named(w, NF + 1)
            for i in range(NC):
                here = named(w, NF + 2 + i)
                total = total + here * (shares[i][0] * ug + shares[i][1] * vg[i])
                coef_unit = coef_unit + gates[w] * here * shares[i][0]
            gate_grads.append(total)
        mixture = gates[0] * values[0] + gates[1] * values[1] + coef_unit * unit
        prob_grad = sum(jnp.where(hots[w], gate_grads[w], 0.0) for w in range(TOP))
        prev_grad = router * (prob_grad - jnp.sum(router * prob_grad, axis=-1, keepdims=True))
        prev_out[s] = prev_grad.T[2 : 2 + NE, :]
        left = prev_grad
        right = jnp.zeros_like(prev_grad)
        for i in range(NC):
            amount = sum(gates[w] * named(w, NF + 2 + i) for w in range(TOP))
            s0, s1 = shares[i]
            mixture = mixture + amount * s1 * small_all[14 + i : 15 + i, :]
            d0, d1 = amount * ug, amount * vg[i]
            inner = s0 * d0 + s1 * d1
            left = left + jnp.where(lane == 10 + 2 * i, s0 * (d0 - inner), 0.0)
            left = left + jnp.where(lane == 11 + 2 * i, s1 * (d1 - inner), 0.0)
            right = right + jnp.where(lane == 14 + i, amount * s1, 0.0)
        out_block[s] = (tile + mixture).astype(BF)
        left_high, left_low = split(left)
        right_high, right_low = split(right)
        unit_grad = unit_grad + mm(left_high, small_low) + mm(left_low, small_low)
        unit_grad = unit_grad + coef_unit * g
        small_grads = small_grads + mm_tn(left_high, unit_low) + mm_tn(left_low, unit_low)
        small_grads = small_grads + mm_tn(right_high, g_low) + mm_tn(right_low, g_low)
        gain_grad = gain_grad + jnp.sum(unit_grad * normal, axis=0, keepdims=True)
        scaled = unit_grad * gain
        dh = g + factor * (scaled - normal * jnp.mean(scaled * normal, axis=-1, keepdims=True))
        dh_out[at, :] = dh
        dproj_s[at, :] = dh.astype(BF)
    row = lax.broadcasted_iota(jnp.int32, (16, D), 0)
    small_grads = jnp.where(row == 1, gain_grad, small_grads).astype(BF)
    for i in range(F):
        rows_s[i] = small_grads[:, i * d_local : (i + 1) * d_local]
    gw_s[...] = jnp.zeros_like(gw_s)
    for k in range(Z):
        for side in range(2):
            seq, group = piece_at((Z, G), meta, k, side)
            dproj = dproj_s[pl.ds(pl.multiple_of(seq * R, R), R), :]
            heads = pl.ds(pl.multiple_of(group * hw, hw), hw)
            das[k][side] = mm_nt(dproj, w_full[heads, :]).astype(BF)
            gw_s[heads, :] += mm_tn(att(k, side), dproj)
    for k in range(F):
        ff = lax.rem(f + k, F)
        at = pl.ds(pl.multiple_of(ff * d_local, d_local), d_local)
        payloads[k][:d_local, :] = gw_s[at, :].astype(BF)
        payloads[k][d_local:, :d_local] = rows_s[ff]
        payloads[k][d_local:, d_local:] = jnp.zeros((16, D - d_local), BF)


def back_kernel(dims, meta, start, cos, sin, small, *refs):
    Z, F, R, D, L, hpd, block = dims
    hw = hpd * HD
    xs, refs = refs[: 2 * Z], refs[2 * Z :]
    dos, refs = refs[: 2 * Z], refs[2 * Z :]
    (normed, weight, q_in, k_in, v_in, o_in, lse_in), refs = refs[:7], refs[7:]
    payloads, refs = refs[:F], refs[F:]
    (mine_out, theirs_out), refs = refs[:2], refs[2:]
    do_s, dq_s, dk_s, dv_s, mixed_s, gw_s, rows_s = refs
    z, core, f = meta[0], meta[1], meta[2]
    d_local = D // F
    for k in range(Z):
        for side in range(2):
            at = lax.rem(z + k, Z) * 2 + (core if side == 0 else 1 - core)
            row = pl.multiple_of(at * R, R)
            tile = dos[k][0] if side == 0 else dos[Z + k][...]
            for h in range(hpd):
                do_s[h, pl.ds(row, R), :] = tile[:, h * HD : (h + 1) * HD]
    dk_s[...] = jnp.zeros_like(dk_s)
    dv_s[...] = jnp.zeros_like(dv_s)

    def query_step(qb, carry):
        rows = pl.ds(pl.multiple_of(qb * block, block), block)
        first = start[rows, :]
        q_pos = qb * block + lax.broadcasted_iota(jnp.int32, (block, block), 0)
        column = lax.broadcasted_iota(jnp.int32, (block, block), 1)
        queries = [q_in[h, rows, :] for h in range(hpd)]
        upstream = [do_s[h, rows, :] for h in range(hpd)]
        lses = [lse_in[h, rows, :] for h in range(hpd)]
        deltas = [
            jnp.sum(upstream[h].astype(F32) * o_in[h, rows, :], axis=-1, keepdims=True)
            for h in range(hpd)
        ]

        def key_step(kb, state):
            keys = pl.ds(pl.multiple_of(kb * block, block), block)
            k_pos = kb * block + column
            allowed = (k_pos <= q_pos) & (k_pos >= first)
            new = []
            for h in range(hpd):
                key, value = k_in[h, keys, :], v_in[h, keys, :]
                scores = mm_nt(queries[h], key)
                weights = jnp.where(allowed, jnp.exp(scores - lses[h]), 0.0)
                dp = mm_nt(upstream[h], value)
                ds = (weights * (dp - deltas[h])).astype(BF)
                dv_s[h, keys, :] += mm_tn(weights.astype(BF), upstream[h])
                dk_s[h, keys, :] += mm_tn(ds, queries[h])
                new.append(state[h] + mm(ds, key))
            return tuple(new)

        begin = tuple(jnp.zeros((block, HD), F32) for _ in range(hpd))
        state = lax.fori_loop(meta[4 + qb], qb + 1, key_step, begin)
        for h in range(hpd):
            dq_s[h, rows, :] = state[h]
        return carry

    lax.fori_loop(0, L // block, query_step, 0)

    def unrotate(step, carry):
        rows = pl.ds(pl.multiple_of(step * block, block), block)
        cosine, sine = cos[rows, :], sin[rows, :]
        parts = [[], [], []]
        for h in range(hpd):
            dq = dq_s[h, rows, :] * HD ** (-0.5)
            dk = dk_s[h, rows, :]
            parts[0].append((dq * cosine - halves_swapped(dq) * sine).astype(BF))
            parts[1].append((dk * cosine - halves_swapped(dk) * sine).astype(BF))
            parts[2].append(dv_s[h, rows, :].astype(BF))
        mixed_s[rows, :] = jnp.concatenate(parts[0] + parts[1] + parts[2], axis=-1)
        return carry

    lax.fori_loop(0, L // block, unrotate, 0)
    gw_s[...] = mm_tn(normed[...], mixed_s[...]).astype(BF)
    total = jnp.zeros((1, D), F32)
    for k in range(Z):
        for side in range(2):
            chip = lax.rem(z - k + Z, Z)
            at = chip * 2 + (core if side == 0 else 1 - core)
            tile = xs[side * Z + k][...].astype(F32)
            row = pl.multiple_of(at * R, R)
            dn = mm_nt(mixed_s[pl.ds(row, R), :], weight[...])
            total = total + jnp.sum(dn * (tile * norm_of(tile)), axis=0, keepdims=True)
            if side == 0:
                mine_out[chip] = dn.astype(BF)
            else:
                theirs_out[chip] = dn.astype(BF)
    total = jnp.broadcast_to(total, (16, D)).astype(BF)
    for i in range(F):
        rows_s[i] = total[:, i * d_local : (i + 1) * d_local]
    for k in range(F):
        ff = lax.rem(f + k, F)
        at = pl.ds(pl.multiple_of(ff * d_local, d_local), d_local)
        payloads[k][:d_local, :] = gw_s[at, :]
        payloads[k][d_local:, :d_local] = rows_s[ff]
        if d_local < 3 * hw:
            payloads[k][d_local:, d_local:] = jnp.zeros((16, 3 * hw - d_local), BF)


def pair_kernel(Z, meta, mine, theirs, *outs):
    for k in range(Z):
        chip = lax.rem(meta[0] + k, Z)
        outs[k][...] = (mine[chip].astype(F32) + theirs[chip].astype(F32)).astype(BF)


def last_kernel(dims, meta, x, dh, small, *refs):
    Z, S, R, _, G = dims
    dns, out, acc = refs[:Z], refs[Z], refs[Z + 1]
    acc[...] = jnp.zeros_like(acc)
    for k in range(Z):
        seq, _ = piece_at((Z, G), meta, k, 0)
        acc[seq] += dns[k][...].astype(F32)
    gain = small[0:1, :]
    for s in range(S):
        tile = x[s].astype(F32)
        factor = norm_of(tile)
        normal = tile * factor
        scaled = acc[s] * gain
        out[s] = dh[s * R : (s + 1) * R, :] + factor * (
            scaled - normal * jnp.mean(scaled * normal, axis=-1, keepdims=True)
        )


def place_kernel(dims, ks, part, meta, *refs):
    F, per, CW, width = dims
    n = len(ks)
    ours, theirs, refs = refs[:n], refs[n : 2 * n], refs[2 * n :]
    outs, (buf, sems) = refs[-5:-2], refs[-2:]
    copies = []
    for side in range(2):
        for j, k in enumerate(ks):
            dev = lax.rem(meta[2] - k + F, F)
            core = meta[1] if side == 0 else 1 - meta[1]
            e = lax.div(dev, per)
            lane = (lax.rem(dev, per) * 2 + core) * CW + part * width
            lanes = pl.ds(pl.multiple_of(lane, 128), width)
            for i in range(3):
                at = (side * n + j) * 3 + i
                buf[at] = (ours if side == 0 else theirs)[j][i].astype(F32)
                copy = pltpu.make_async_copy(buf.at[at], outs[i].at[:, e, lanes], sems.at[at])
                copy.start()
                copies.append(copy)
    for copy in copies:
        copy.wait()


def qkv_grad_kernel(dims, meta, *refs):
    G, D, d_local, hw = dims
    pieces, (out, gain_out, table) = refs[:-3], refs[-3:]
    group = lax.rem(meta[3], G)
    at = 0
    for piece in pieces:
        for j in range(piece.shape[0]):
            table[at] = piece[j]
            at += 1
    gain = jnp.zeros((1, d_local), F32)
    for i in range(G):
        tile = table[jnp.bitwise_xor(group, i)].astype(F32)
        gain = gain + tile[d_local : d_local + 1, :d_local]
        width = max(0, min(hw, D - i * hw))
        if width:
            for part in range(3):
                out[:, part * D + i * hw : part * D + i * hw + width] = tile[
                    :d_local, part * hw : part * hw + width
                ]
    gain_out[...] = gain


def body(
    block_input,
    attn_gain,
    w_qkv,
    w_out,
    ffn_gain,
    w_router,
    w_gate,
    w_up,
    w_down,
    const_mix,
    const_vec,
    prev_logits,
    routes,
    doc_ids,
    d_out,
    *,
    F,
    C,
):
    S, R, D = block_input.shape
    L = doc_ids.shape[1]
    Z = C // 2
    G = C // S
    hpd = -(-H // G)
    hw = hpd * HD
    FF = w_gate.shape[2]
    per = F // NF
    CW = FF // (2 * per)
    d_local = D // F
    T = S * R
    block = min(256, L)
    shaped = jax.ShapeDtypeStruct
    f = lax.axis_index("fsdp")
    c = lax.axis_index("ctx")
    core = c % 2
    z = c // 2

    def fs(t, k):
        return lax.ppermute(t, "fsdp", [(i, (i + k) % F) for i in range(F)])

    def zs(t, k):
        return lax.ppermute(
            t, "ctx", [(2 * i + j, 2 * ((i + k) % Z) + j) for i in range(Z) for j in range(2)]
        )

    def cx(t):
        return lax.ppermute(t, "ctx", [(i, i ^ 1) for i in range(C)])

    def pick(t, index, axis=0):
        return lax.dynamic_index_in_dim(t, index, axis, keepdims=False)

    def seq_of(chip):
        return chip // (Z // S)

    def expert_of(dev):
        return lax.div(dev, per)

    def chunk_of(dev):
        return (dev % per) * 2 + core

    def call(kernel, name, out_shape, args, scratch=(), smem=1, **kw):
        return pl.pallas_call(
            kernel,
            out_shape=out_shape,
            in_specs=[SMEM] * smem + [VMEM] * (len(args) - smem),
            out_specs=tuple([VMEM] * len(out_shape)),
            scratch_shapes=list(scratch),
            compiler_params=params(name, L > 2048),
            **kw,
        )(*args)

    x_mine = [pick(block_input, seq_of(z))] + [
        zs(pick(block_input, seq_of((z + k) % Z)), k) for k in range(1, Z)
    ]
    x_theirs = [cx(t) for t in x_mine]

    my_docs = pick(doc_ids, c // G)
    start = jnp.sum((my_docs[None, :] < my_docs[:, None]).astype(jnp.int32), axis=1)
    first_block = start.reshape(L // block, block)[:, 0] // block
    meta = jnp.concatenate([jnp.stack([z, core, f, c]).astype(jnp.int32), first_block])
    route_rows = routes.transpose(0, 2, 1).reshape(S * TOP, R)
    prev = prev_logits.transpose(0, 2, 1)

    (first,) = call(
        functools.partial(pack_kernel, (F, D, G, hpd)),
        "pack",
        (shaped((d_local + 16, 3 * hw), BF),),
        (
            meta,
            w_qkv,
            attn_gain[None],
            ffn_gain[None],
            w_router.T,
            const_mix.T,
            const_vec.T,
        ),
    )
    w_pieces = [first] + [fs(first, k) for k in range(1, F)]
    slot_rows, *g_outs = call(
        functools.partial(grad_rows_kernel, (F, S, R, D, expert_of)),
        "grad_rows",
        (shaped((S * TOP, R), jnp.int32),) + (shaped((S * MOST, D), BF),) * F,
        (meta, d_out, route_rows),
        [pltpu.VMEM((NF, S * MOST, D), BF)],
    )
    g_mine = jnp.concatenate([g_outs[0]] + [fs(g_outs[k], k) for k in range(1, F)], axis=0)
    o_pieces = [w_out] + [fs(w_out, k) for k in range(1, F)]

    def expert_slices():
        if per == 1:
            cut = [
                lax.dynamic_slice_in_dim(w, core * CW, CW, 2).transpose(1, 0, 2)
                for w in (w_gate, w_up, w_down)
            ]
            cut = lax.optimization_barrier(cut)
            return call(
                functools.partial(order_kernel, F),
                "order",
                (shaped((3, d_local, CW), BF),) * F,
                (meta, *cut),
            )
        out = []
        for k in range(F):
            dev = (f + k) % F
            out.append(
                jnp.stack(
                    [
                        pick(
                            lax.dynamic_slice_in_dim(w, chunk_of(dev) * CW, CW, 2),
                            expert_of(dev),
                            1,
                        )
                        for w in (w_gate, w_up, w_down)
                    ]
                )
            )
        return out

    slices = expert_slices()
    e_pieces = [slices[0]] + [fs(slices[k], k) for k in range(1, F)]

    frequency = jnp.exp(jnp.arange(HD // 2, dtype=F32) * (-2.0 * math.log(10000.0) / HD))
    angles = jnp.arange(L).astype(F32)[:, None] * frequency[None, :]
    cosine, sine = jnp.cos(angles), jnp.sin(angles)
    cosine = jnp.concatenate([cosine, cosine], axis=1)
    sine = jnp.concatenate([-sine, sine], axis=1)
    dims = (Z, F, R, D, L, hpd, block)
    normed, qkv_w, small, q, k_, v, o, lse, *att_pieces = call(
        functools.partial(attend_kernel, dims),
        "attend",
        (
            shaped((L, D), BF),
            shaped((D, 3 * hw), BF),
            shaped((16, D), F32),
            shaped((hpd, L, HD), BF),
            shaped((hpd, L, HD), BF),
            shaped((hpd, L, HD), BF),
            shaped((hpd, L, HD), F32),
            shaped((hpd, L, 1), F32),
        )
        + (shaped((2, R, hw), BF),) * Z,
        (meta, start[:, None], cosine, sine, *x_mine, *x_theirs, *w_pieces),
        [pltpu.VMEM((F, 16, d_local), F32), pltpu.VMEM((C, R, hw), BF)],
    )

    g_planes = [(g_mine, cx(g_mine))] + [zs(g_mine, k) for k in range(1, Z)]

    pieces = [att_pieces[0]] + [zs(att_pieces[k], k) for k in range(1, Z)]
    atts = pieces + [cx(t[1]) for t in pieces]
    outs = call(
        functools.partial(dispatch_kernel, (Z, F, S, R, D, G, hw, expert_of)),
        "dispatch",
        (shaped((T, D), F32), shaped((G * hw, D), BF))
        + (shaped((S * MOST, D + 128), BF),) * F,
        (meta, block_input, small, prev, route_rows, slot_rows, *atts, *o_pieces),
        [pltpu.VMEM((NF, S * MOST, D + 128), BF)],
    )
    hidden, out_w, toks = outs[0], outs[1], outs[2:]
    own = [toks[0]] + [fs(toks[k], k) for k in range(1, F)]
    own = jnp.concatenate(own, axis=0)
    n = own.shape[0]

    steps = 4 if CW % 512 == 0 else 2
    cut = CW // steps
    e_spec = pl.BlockSpec((3, d_local, cut), lambda i: (0, 0, i))
    act_spec = pl.BlockSpec((2 * n, cut), lambda i: (0, i))
    both_spec = pl.BlockSpec((D, 2 * n), lambda i: (0, 0))

    def ffn(at, rows, theirs, g_rows):
        own_plane = at == 0
        shapes = (shaped((2 * n, CW), BF),) * 3 + (shaped((D, 2 * n), BF),) * 2
        specs = (act_spec,) * 3 + (both_spec,) * 2
        scratch = [pltpu.VMEM((2 * n, D), BF), pltpu.VMEM((2 * n, D), BF)]
        scratch.append(pltpu.VMEM((3, D, cut), BF))
        if own_plane:
            shapes += (shaped((2, n, D), F32), shaped((2, n, D), BF))
            specs += (pl.BlockSpec((2, n, D), lambda i: (0, 0, 0)),) * 2
            scratch.append(pltpu.VMEM((2, 2 * n, D), F32))
        row_spec = pl.BlockSpec((n, D + 128), lambda i: (0, 0))
        g_spec = pl.BlockSpec((n, D), lambda i: (0, 0))
        return pl.pallas_call(
            functools.partial(ffn_kernel, (F, D), own_plane),
            out_shape=shapes,
            grid=(steps,),
            in_specs=[SMEM, row_spec, row_spec, g_spec, g_spec] + [e_spec] * F,
            out_specs=specs,
            scratch_shapes=scratch,
            compiler_params=params("experts" if at else "experts0", L > 2048),
        )(meta, rows, theirs, *g_rows, *e_pieces)

    *plane, back_mine, back_theirs = ffn(0, own, cx(own), g_planes[0])
    planes = [plane]
    back = (back_mine + cx(back_theirs).astype(F32)).astype(BF).reshape(2, F, S * MOST, D)
    rets = [back[:, 0]] + [fs(back[:, k], -k) for k in range(1, F)]
    ring = [own]
    for _ in range(1, Z):
        ring.append(zs(ring[-1], 1))

    def far(k, after):
        rows, g_rows, _ = lax.optimization_barrier((ring[k], g_planes[k], after))
        planes.append(ffn(k, rows, cx(rows), (g_rows, cx(g_rows))))

    far(1, back_mine)
    outs = call(
        functools.partial(combine_kernel, (Z, F, S, R, D, G, hw, per, expert_of)),
        "combine",
        (shaped((S, R, D), BF), shaped((T, D), F32), shaped((S, NE, R), F32))
        + (shaped((2, R, hw), BF),) * Z
        + (shaped((d_local + 16, D), BF),) * F,
        (meta, hidden, d_out, small, prev, route_rows, slot_rows, *rets, *atts, out_w),
        [
            pltpu.VMEM((F, 2, S * MOST, D), BF),
            pltpu.VMEM((G * hw, D), F32),
            pltpu.VMEM((T, D), BF),
            pltpu.VMEM((F, 16, d_local), BF),
        ],
    )
    out_block, hidden_grad, prev_grad = outs[:3]
    das, o_payloads = outs[3 : 3 + Z], outs[3 + Z :]
    grad_prev = prev_grad.transpose(0, 2, 1)

    do_pieces = [das[0]] + [zs(das[k], -k) for k in range(1, Z)]
    dos = do_pieces + [cx(t[1]) for t in do_pieces]

    for k in range(2, Z):
        far(k, hidden_grad)
    parts = 2
    width = CW // parts
    wide = min(256, width)
    flat = [t for plane in planes for t in plane]
    e_grads = []
    for part in range(parts):
        first_block_at = part * (width // wide)
        if Z > 4:
            lanes = slice(part * width, (part + 1) * width)
            trio = [
                sum(mm(plane[left], plane[right][:, lanes]) for plane in planes).astype(BF)
                for left, right in ((3, 1), (3, 2), (4, 0))
            ]
            trio = jnp.stack(trio).reshape(3, F, d_local, width)
            e_grads.append([pick(trio, (f + k) % F, 1) for k in range(F)])
            continue
        acts = pl.BlockSpec((2 * n, wide), lambda i, b=first_block_at: (0, b + i))
        e_grads.append(
            pl.pallas_call(
                functools.partial(weight_kernel, (F, D, Z)),
                out_shape=(shaped((3, d_local, width), BF),) * F,
                grid=(width // wide,),
                in_specs=[SMEM] + [acts, acts, acts, both_spec, both_spec] * Z,
                out_specs=(pl.BlockSpec((3, d_local, wide), lambda i: (0, 0, i)),) * F,
                scratch_shapes=[pltpu.VMEM((3, D, wide), BF)],
                compiler_params=params("expert_grads", L > 2048),
            )(meta, *flat)
        )
    dos[0], *_ = lax.optimization_barrier((dos[0], e_grads[-1][0]))
    outs = call(
        functools.partial(back_kernel, dims),
        "attend_back",
        (shaped((d_local + 16, 3 * hw), BF),) * F + (shaped((Z, R, D), BF),) * 2,
        (
            meta,
            start[:, None],
            cosine,
            sine,
            small,
            *x_mine,
            *x_theirs,
            *dos,
            normed,
            qkv_w,
            q,
            k_,
            v,
            o,
            lse,
        ),
        [
            pltpu.VMEM((hpd, L, HD), BF),
            pltpu.VMEM((hpd, L, HD), F32),
            pltpu.VMEM((hpd, L, HD), F32),
            pltpu.VMEM((hpd, L, HD), F32),
            pltpu.VMEM((L, 3 * hw), BF),
            pltpu.VMEM((D, 3 * hw), BF),
            pltpu.VMEM((F, 16, d_local), BF),
        ],
    )
    q_payloads, dn_mine, dn_theirs = outs[:F], outs[F], outs[F + 1]
    dns = call(
        functools.partial(pair_kernel, Z),
        "pair",
        (shaped((R, D), BF),) * Z,
        (meta, dn_mine, cx(dn_theirs)),
    )
    paired = dns[0]
    dns = [dns[0]] + [zs(dns[k], k) for k in range(1, Z)]
    (grad_x,) = call(
        functools.partial(last_kernel, (Z, S, R, D, G)),
        "input_grad",
        (shaped((S, R, D), F32),),
        (meta, block_input, hidden_grad, small, *dns),
        [pltpu.VMEM((S, R, D), F32)],
    )

    def moved_rows(parts):
        return [parts[0]] + [fs(parts[k], k) for k in range(1, F)]

    def summed_rows(parts):
        return sum(p.astype(F32) for p in parts).astype(BF)

    def over_ctx(t):
        step = 1
        while step < C:
            moved = lax.ppermute(t, "ctx", [(i, i ^ step) for i in range(C)])
            t = (t.astype(F32) + moved.astype(F32)).astype(BF)
            step *= 2
        return t

    payload = summed_rows(moved_rows(q_payloads))
    summed = payload.astype(F32)
    for j in range(1, S):
        moved = lax.ppermute(payload, "ctx", [(i, (i + j * G) % C) for i in range(C)])
        summed = summed + moved.astype(F32)
    payload = summed.astype(BF)[None]
    gathered = [payload]
    step = 1
    while step < G:
        gathered.append(lax.ppermute(payload, "ctx", [(i, i ^ step) for i in range(C)]))
        step *= 2
        if step < G:
            payload = jnp.concatenate([payload, gathered[-1]], axis=0)
    grad_qkv, grad_gain_one = call(
        functools.partial(qkv_grad_kernel, (G, D, d_local, hw)),
        "qkv_grad",
        (shaped((d_local, 3 * D), F32), shaped((1, d_local), F32)),
        (meta, *gathered),
        [pltpu.VMEM((G, d_local + 16, 3 * hw), BF)],
    )
    grad_gain_one = grad_gain_one[0]

    moved = moved_rows(o_payloads)
    moved, _ = lax.optimization_barrier((moved, paired))
    payload = over_ctx(summed_rows(moved)).astype(F32)
    grad_w_out = payload[:d_local]
    smalls = payload[d_local:, :d_local]

    ANY = pl.BlockSpec(memory_space=pl.ANY)
    placed = ()
    for part in range(parts):
        ours = [e_grads[part][0]] + [fs(e_grads[part][k], k) for k in range(1, F)]
        theirs = [cx(t) for t in ours]
        groups = [list(range(F))] if part < parts - 1 else [list(range(F - 1)), [F - 1]]
        for ks in groups:
            args = (meta, *[ours[k] for k in ks], *[theirs[k] for k in ks], *placed)
            at = 1 + 2 * len(ks)
            placed = pl.pallas_call(
                functools.partial(place_kernel, (F, per, CW, width), ks, part),
                out_shape=(shaped((d_local, NF, FF), F32),) * 3,
                in_specs=[SMEM] + [VMEM] * (2 * len(ks)) + [ANY] * len(placed),
                out_specs=(ANY,) * 3,
                input_output_aliases={at + i: i for i in range(len(placed))},
                scratch_shapes=[
                    pltpu.VMEM((6 * len(ks), d_local, width), F32),
                    pltpu.SemaphoreType.DMA((6 * len(ks),)),
                ],
                compiler_params=params("place", L > 2048),
            )(*args)
    grad_gate, grad_up, grad_down = placed
    return (
        out_block,
        grad_x,
        grad_prev,
        grad_gain_one,
        grad_qkv,
        grad_w_out,
        smalls[1],
        smalls[2:10].T,
        grad_gate,
        grad_up,
        grad_down,
        smalls[10:14].T,
        smalls[14:16].T,
    )


def solution(mesh):
    F, Z = mesh.shape["fsdp"], mesh.shape["ctx"] // 2

    def layer(*args):
        return body(*args, F=F, C=2 * Z)

    return jax.shard_map(
        layer,
        mesh=mesh,
        in_specs=(
            P("fsdp", "ctx", None),
            P("fsdp"),
            P("fsdp", None),
            P("fsdp", None),
            P("fsdp"),
            P("fsdp", None),
            P("fsdp", None, None),
            P("fsdp", None, None),
            P("fsdp", None, None),
            P("fsdp", None),
            P("fsdp", None),
            P("fsdp", "ctx", None),
            P("fsdp", "ctx", None),
            P("fsdp", None),
            P("fsdp", "ctx", None),
        ),
        out_specs=(
            P("fsdp", "ctx", None),
            P("fsdp", "ctx", None),
            P("fsdp", "ctx", None),
            P("fsdp"),
            P("fsdp", None),
            P("fsdp", None),
            P("fsdp"),
            P("fsdp", None),
            P("fsdp", None, None),
            P("fsdp", None, None),
            P("fsdp", None, None),
            P("fsdp", None),
            P("fsdp", None),
        ),
        check_vma=False,
    )
```

profile of v0, /device:TPU:0, one launch (start us, length us, event | category | flops | bytes accessed | tf_op | source)
XLA Modules:
  0.0 477.0 jit_solution(10640136532143830456)
XLA Ops:
  0.9 2.2 dynamic-slice_bitcast_fusion
  3.1 3.1 collective-permute-start
  6.1 2.6 collective-permute-start.1
  8.7 1.3 collective-permute-start.2
  12.1 1.4 shard_map.246.refs_8_
  13.5 1.5 collective-permute-start.7
  15.0 3.2 fusion.2
  18.2 1.9 constant_dynamic-slice_fusion.2
  22.5 4.3 constant_dynamic-slice_fusion
  26.8 1.5 collective-permute-start.8
  28.4 1.4 collective-permute-start.9
  30.7 2.1 copy.86
  36.6 6.5 %collective-permute-start.17 = (bf16[192,768]{1,0:T(8,128)(2,1)S(1)}, bf16[192,768]{1,0:T(8,128)(2,1)S(1)}, u32[]{:S(2)}, u32[]{:S(2)}) collective-permute-start(bf16[192,768]{1,0:T(8,128)(2,1)S(1)} %copy-done.44), channel_id=1, source_target_pairs={{0,8},{8,16},{16,24},{24,0},{1,9},{9,17},{17,25},{25,1},{2,10},{10... | collective-permute-start | bytes 884744 | tf_op jit(solution)/shard_map/ppermute | solution.py:716
  45.8 14.9 %shard_map.247 = (bf16[1024,768]{1,0:T(8,128)(2,1)S(1)}, bf16[768,576]{1,0:T(8,128)(2,1)S(1)}, f32[16,768]{1,0:T(8,128)S(1)}, bf16[3,1024,64]{2,1,0:T(8,128)(2,1...) custom-call(s32[8]{0:T(128)S(1)} %concatenate.18.meta, ...), custom_call_target="tpu_custom_call" | custom-call | tf_op jit(solution)/shard_map/pallas_call | solution.py:739
  66.3 6.8 %collective-permute-done.10.refs_1_.refs_5_ = bf16[2,128,192]{2,1,0:T(8,128)(2,1)S(1)} collective-permute-done((bf16[2,128,192]{2,1,0:T(8,128)(2,1)S(1)}, bf16[2,128,192]{2,1,0:T(8,128)(2,1)S(1)}, u32[]{:S(2)}, u32[]{:S(2)}) %collective-permute-start.10) | collective-permute-done | bytes 98336 | tf_op jit(solution)/shard_map/ppermute | solution.py:719
  73.1 6.4 %collective-permute-done.11.refs_2_.refs_6_ = bf16[2,128,192]{2,1,0:T(8,128)(2,1)S(1)} collective-permute-done((bf16[2,128,192]{2,1,0:T(8,128)(2,1)S(1)}, bf16[2,128,192]{2,1,0:T(8,128)(2,1)S(1)}, u32[]{:S(2)}, u32[]{:S(2)}) %collective-permute-start.11) | collective-permute-done | bytes 98336 | tf_op jit(solution)/shard_map/ppermute | solution.py:719
  79.5 5.0 %collective-permute-done.12.refs_3_.refs_7_ = bf16[2,128,192]{2,1,0:T(8,128)(2,1)S(1)} collective-permute-done((bf16[2,128,192]{2,1,0:T(8,128)(2,1)S(1)}, bf16[2,128,192]{2,1,0:T(8,128)(2,1)S(1)}, u32[]{:S(2)}, u32[]{:S(2)}) %collective-permute-start.12) | collective-permute-done | bytes 98336 | tf_op jit(solution)/shard_map/ppermute | solution.py:719
  84.4 1.5 collective-permute-start.25
  88.8 2.3 collective-permute-start.30
  91.1 2.5 shard_map.249
  93.8 1.5 collective-permute-start.21
  95.3 50.0 %collective-permute-done.20 = bf16[96,896]{1,0:T(8,128)(2,1)S(1)} collective-permute-done((bf16[96,896]{1,0:T(8,128)(2,1)S(1)}, bf16[96,896]{1,0:T(8,128)(2,1)S(1)}, u32[]{:S(2)}, u32[]{:S(2)}) %collective-permute-start.20) | collective-permute-done | bytes 172064 | tf_op jit(solution)/shard_map/ppermute | solution.py:716
  145.4 3.0 collective-permute-done.21
  148.4 2.9 collective-permute-done.22
  151.4 2.6 collective-permute-done.26
  154.1 2.0 collective-permute-done.27.g_b
  156.1 13.8 %shard_map.251 = (bf16[768,1024]{1,0:T(8,128)(2,1)S(1)}, bf16[768,1024]{1,0:T(8,128)(2,1)S(1)}, bf16[768,1024]{1,0:T(8,128)(2,1)S(1)}, bf16[768,768]{1,0:T(8,128...) custom-call(s32[8]{0:T(128)S(1)} %concatenate.18.meta, ...), custom_call_target="tpu_custom_call" | custom-call | tf_op jit(solution)/shard_map/pallas_call | solution.py:878
  170.4 19.9 %collective-permute-done.35.rows_a = bf16[384,896]{1,0:T(8,128)(2,1)S(1)} collective-permute-done((bf16[384,896]{1,0:T(8,128)(2,1)S(1)}, bf16[384,896]{1,0:T(8,128)(2,1)S(1)}, u32[]{:S(2)}, u32[]{:S(2)}) %collective-permute-start.35) | collective-permute-done | bytes 688160 | tf_op jit(solution)/shard_map/ppermute | solution.py:719
  193.6 9.4 %collective-permute-done.36.g_a = bf16[384,768]{1,0:T(8,128)(2,1)S(1)} collective-permute-done((bf16[384,768]{1,0:T(8,128)(2,1)S(1)}, bf16[384,768]{1,0:T(8,128)(2,1)S(1)}, u32[]{:S(2)}, u32[]{:S(2)}) %collective-permute-start.36) | collective-permute-done | bytes 589856 | tf_op jit(solution)/shard_map/ppermute | solution.py:719
  202.9 14.8 %collective-permute-done.39.rows_a = bf16[384,896]{1,0:T(8,128)(2,1)S(1)} collective-permute-done((bf16[384,896]{1,0:T(8,128)(2,1)S(1)}, bf16[384,896]{1,0:T(8,128)(2,1)S(1)}, u32[]{:S(2)}, u32[]{:S(2)}) %collective-permute-start.39) | collective-permute-done | bytes 688160 | tf_op jit(solution)/shard_map/ppermute | solution.py:719
  220.3 7.1 %shard_map.252 = (bf16[2,128,768]{2,1,0:T(8,128)(2,1)}, f32[256,768]{1,0:T(8,128)S(1)}, f32[2,8,128]{2,1,0:T(8,128)}, bf16[2,128,192]{2,1,0:T(8,128)(2,1)S(1)}, ...) custom-call(s32[8]{0:T(128)S(1)} %concatenate.18.meta, ...), custom_call_target="tpu_custom_call" | custom-call | tf_op jit(solution)/shard_map/pallas_call | solution.py:739
  228.3 14.8 %collective-permute-done.40.g_a = bf16[384,768]{1,0:T(8,128)(2,1)S(1)} collective-permute-done((bf16[384,768]{1,0:T(8,128)(2,1)S(1)}, bf16[384,768]{1,0:T(8,128)(2,1)S(1)}, u32[]{:S(2)}, u32[]{:S(2)}) %collective-permute-start.40) | collective-permute-done | bytes 589856 | tf_op jit(solution)/shard_map/ppermute | solution.py:719
  243.1 16.1 %collective-permute-done.44.g_a = bf16[384,768]{1,0:T(8,128)(2,1)S(1)} collective-permute-done((bf16[384,768]{1,0:T(8,128)(2,1)S(1)}, bf16[384,768]{1,0:T(8,128)(2,1)S(1)}, u32[]{:S(2)}, u32[]{:S(2)}) %collective-permute-start.44) | collective-permute-done | bytes 589856 | tf_op jit(solution)/shard_map/ppermute | solution.py:719
  260.7 13.4 %collective-permute-done.47.refs_9_ = bf16[2,128,192]{2,1,0:T(8,128)(2,1)S(1)} collective-permute-done((bf16[2,128,192]{2,1,0:T(8,128)(2,1)S(1)}, bf16[2,128,192]{2,1,0:T(8,128)(2,1)S(1)}, u32[]{:S(2)}, u32[]{:S(2)}) %collective-permute-start.47) | collective-permute-done | bytes 98336 | tf_op jit(solution)/shard_map/ppermute | solution.py:719
  274.8 7.8 %collective-permute-done.48.refs_10_ = bf16[2,128,192]{2,1,0:T(8,128)(2,1)S(1)} collective-permute-done((bf16[2,128,192]{2,1,0:T(8,128)(2,1)S(1)}, bf16[2,128,192]{2,1,0:T(8,128)(2,1)S(1)}, u32[]{:S(2)}, u32[]{:S(2)}) %collective-permute-start.48) | collective-permute-done | bytes 98336 | tf_op jit(solution)/shard_map/ppermute | solution.py:719
  282.6 6.8 %collective-permute-done.49.refs_11_ = bf16[2,128,192]{2,1,0:T(8,128)(2,1)S(1)} collective-permute-done((bf16[2,128,192]{2,1,0:T(8,128)(2,1)S(1)}, bf16[2,128,192]{2,1,0:T(8,128)(2,1)S(1)}, u32[]{:S(2)}, u32[]{:S(2)}) %collective-permute-start.49) | collective-permute-done | bytes 98336 | tf_op jit(solution)/shard_map/ppermute | solution.py:719
  291.8 8.2 %shard_map.253 = (bf16[768,1024]{1,0:T(8,128)(2,1)S(1)}, bf16[768,1024]{1,0:T(8,128)(2,1)S(1)}, bf16[768,1024]{1,0:T(8,128)(2,1)S(1)}, bf16[768,768]{1,0:T(8,128)(2,1)S(1)}, bf16[768,768]{1,0:T(8,128)(2,1)S(1)}) custom-call(s32[8]{0:T(128)S(1)} %concatenate.18.meta, bf16[384,896]{1,0:T(8,128)(2,1)S(1)} %collective-permute-done.35.rows_a, ...), custom_call_target="tpu_custom_call" | custom-call | tf_op jit(solution)/shard_map/pallas_call | solution.py:878
  300.0 8.0 %shard_map.254 = (bf16[768,1024]{1,0:T(8,128)(2,1)S(1)}, bf16[768,1024]{1,0:T(8,128)(2,1)S(1)}, bf16[768,1024]{1,0:T(8,128)(2,1)S(1)}, bf16[768,768]{1,0:T(8,128)(2,1)S(1)}, bf16[768,768]{1,0:T(8,128)(2,1)S(1)}) custom-call(s32[8]{0:T(128)S(1)} %concatenate.18.meta, bf16[384,896]{1,0:T(8,128)(2,1)S(1)} %collective-permute-done.39.rows_a, ...), custom_call_target="tpu_custom_call" | custom-call | tf_op jit(solution)/shard_map/pallas_call | solution.py:878
  308.0 8.0 %shard_map.255 = (bf16[768,1024]{1,0:T(8,128)(2,1)S(1)}, bf16[768,1024]{1,0:T(8,128)(2,1)S(1)}, bf16[768,1024]{1,0:T(8,128)(2,1)S(1)}, bf16[768,768]{1,0:T(8,128)(2,1)S(1)}, bf16[768,768]{1,0:T(8,128)(2,1)S(1)}) custom-call(s32[8]{0:T(128)S(1)} %concatenate.18.meta, bf16[384,896]{1,0:T(8,128)(2,1)S(1)} %collective-permute-done.43.rows_a, ...), custom_call_target="tpu_custom_call" | custom-call | tf_op jit(solution)/shard_map/pallas_call | solution.py:878
  316.2 10.3 %shard_map.256 = (bf16[3,192,512]{2,1,0:T(8,128)(2,1)S(1)}, bf16[3,192,512]{2,1,0:T(8,128)(2,1)}, bf16[3,192,512]{2,1,0:T(8,128)(2,1)}, bf16[3,192,512]{2,1,0:T(8,128)(2,1)}) custom-call(s32[8]{0:T(128)S(1)} %concatenate.18.meta, bf16[768,1024]{1,0:T(8,128)(2,1)S(1)} %get-tuple-element.144.refs_0_, bf16[768,1024]{1,0:T(8,128)(2,1)S(1)} %get-tuple-element.145.refs_1_, ...), custom_call_target="tpu_custom_call" | custom-call | tf_op jit(solution)/shard_map/pallas_call | solution.py:942
  326.6 1.4 copy-done.16
  331.5 20.7 %shard_map.257 = (bf16[208,576]{1,0:T(8,128)(2,1)S(1)}, bf16[208,576]{1,0:T(8,128)(2,1)S(1)}, bf16[208,576]{1,0:T(8,128)(2,1)S(1)}, bf16[208,576]{1,0:T(8,128)(2...) custom-call(s32[8]{0:T(128)S(1)} %concatenate.18.meta, s32[1024,1]{1,0:T(8,128)S(1)} %copy-done.4, ...), custom_call_target="tpu_custom_call" | custom-call | tf_op jit(solution)/shard_map/pallas_call | solution.py:739
  352.2 3.2 collective-permute-start.59
  355.4 2.9 collective-permute-start.66
  358.3 3.1 collective-permute-done.60
  362.4 5.4 %collective-permute-done.59 = bf16[208,576]{1,0:T(8,128)(2,1)S(1)} collective-permute-done((bf16[208,576]{1,0:T(8,128)(2,1)S(1)}, bf16[208,576]{1,0:T(8,128)(2,1)S(1)}, u32[]{:S(2)}, u32[]{:S(2)}) %collective-permute-start.59) | collective-permute-done | bytes 239648 | tf_op jit(solution)/shard_map/ppermute | solution.py:716
  369.7 4.4 collective-permute-done.66
  374.1 11.6 %collective-permute-done.61 = bf16[208,576]{1,0:T(8,128)(2,1)S(1)} collective-permute-done((bf16[208,576]{1,0:T(8,128)(2,1)S(1)}, bf16[208,576]{1,0:T(8,128)(2,1)S(1)}, u32[]{:S(2)}, u32[]{:S(2)}) %collective-permute-start.61) | collective-permute-done | bytes 239648 | tf_op jit(solution)/shard_map/ppermute | solution.py:1018
  385.7 9.5 %shard_map.261 = (bf16[3,192,512]{2,1,0:T(8,128)(2,1)S(1)}, bf16[3,192,512]{2,1,0:T(8,128)(2,1)S(1)}, bf16[3,192,512]{2,1,0:T(8,128)(2,1)S(1)}, bf16[3,192,512]{2,1,0:T(8,128)(2,1)S(1)}) custom-call(s32[8]{0:T(128)S(1)} %concatenate.18.meta, bf16[768,1024]{1,0:T(8,128)(2,1)S(1)} %get-tuple-element.144.refs_0_, ...), custom_call_target="tpu_custom_call" | custom-call | tf_op jit(solution)/shard_map/pallas_call | solution.py:942
  395.2 2.7 collective-permute-start.77
  399.0 3.0 collective-permute-start.79
  403.9 8.5 %collective-permute-done.77.refs_1_ = bf16[3,192,512]{2,1,0:T(8,128)(2,1)S(1)} collective-permute-done((bf16[3,192,512]{2,1,0:T(8,128)(2,1)S(1)}, bf16[3,192,512]{2,1,0:T(8,128)(2,1)S(1)}, u32[]{:S(2)}, u32[]{:S(2)}) %collective-permute-start.77) | collective-permute-done | bytes 589856 | tf_op jit(solution)/shard_map/ppermute | solution.py:716
  412.4 12.1 %collective-permute-done.78.refs_2_ = bf16[3,192,512]{2,1,0:T(8,128)(2,1)S(1)} collective-permute-done((bf16[3,192,512]{2,1,0:T(8,128)(2,1)S(1)}, bf16[3,192,512]{2,1,0:T(8,128)(2,1)S(1)}, u32[]{:S(2)}, u32[]{:S(2)}) %collective-permute-start.78) | collective-permute-done | bytes 589856 | tf_op jit(solution)/shard_map/ppermute | solution.py:716
  425.2 8.0 %collective-permute-done.55.refs_1_ = bf16[128,768]{1,0:T(8,128)(2,1)S(1)} collective-permute-done((bf16[128,768]{1,0:T(8,128)(2,1)S(1)}, bf16[128,768]{1,0:T(8,128)(2,1)S(1)}, u32[]{:S(2)}, u32[]{:S(2)}) %collective-permute-start.55) | collective-permute-done | bytes 196640 | tf_op jit(solution)/shard_map/ppermute | solution.py:719
  434.3 8.4 %collective-permute-done.56.refs_2_ = bf16[128,768]{1,0:T(8,128)(2,1)S(1)} collective-permute-done((bf16[128,768]{1,0:T(8,128)(2,1)S(1)}, bf16[128,768]{1,0:T(8,128)(2,1)S(1)}, u32[]{:S(2)}, u32[]{:S(2)}) %collective-permute-start.56) | collective-permute-done | bytes 196640 | tf_op jit(solution)/shard_map/ppermute | solution.py:719
  442.7 2.5 collective-permute-start.68
  445.9 6.0 %collective-permute-done.68 = bf16[208,768]{1,0:T(8,128)(2,1)S(1)} collective-permute-done((bf16[208,768]{1,0:T(8,128)(2,1)S(1)}, bf16[208,768]{1,0:T(8,128)(2,1)S(1)}, u32[]{:S(2)}, u32[]{:S(2)}) %collective-permute-start.68) | collective-permute-done | bytes 319520 | tf_op jit(solution)/shard_map/ppermute | solution.py:1010
  453.0 3.6 collective-permute-start.69
  456.6 2.0 shard_map.259
  458.6 4.4 shard_map.262
  463.0 3.6 shard_map.263
  466.6 2.0 shard_map.264
  468.6 2.6 collective-permute-done.63.refs_2_
  471.2 2.1 shard_map.260
  (306 shorter events, 48.4 us)
Async XLA Ops:
  3.1 23.8 %collective-permute-start = (bf16[128,768]{1,0:T(8,128)(2,1)}, bf16[128,768]{1,0:T(8,128)(2,1)}, u32[]{:S(2)}, u32[]{:S(2)}) collective-permute-start(bf16[128,768]{1,0:T(8,128)(2,1)} %get-tuple-element.225), channel_id=1, source_target_pairs={{0,2},{1,3},{2,4},{3,5},{4,6},{5,7},{6,0},{7,1},{8,10},{9,11},{10,... | collective-permute-start | bytes 589832 | tf_op jit(solution)/shard_map/ppermute | solution.py:719
  6.1 22.2 %collective-permute-start.1 = (bf16[128,768]{1,0:T(8,128)(2,1)}, bf16[128,768]{1,0:T(8,128)(2,1)}, u32[]{:S(2)}, u32[]{:S(2)}) collective-permute-start(bf16[128,768]{1,0:T(8,128)(2,1)} %get-tuple-element.224), channel_id=1, source_target_pairs={{0,4},{1,5},{2,6},{3,7},{4,0},{5,1},{6,2},{7,3},{8,12},{9,13},{10,... | collective-permute-start | bytes 589832 | tf_op jit(solution)/shard_map/ppermute | solution.py:719
  8.7 21.1 %collective-permute-start.2 = (bf16[128,768]{1,0:T(8,128)(2,1)}, bf16[128,768]{1,0:T(8,128)(2,1)}, u32[]{:S(2)}, u32[]{:S(2)}) collective-permute-start(bf16[128,768]{1,0:T(8,128)(2,1)} %get-tuple-element.223), channel_id=1, source_target_pairs={{0,6},{1,7},{2,0},{3,1},{4,2},{5,3},{6,4},{7,5},{8,14},{9,15},{10,... | collective-permute-start | bytes 589832 | tf_op jit(solution)/shard_map/ppermute | solution.py:719
  10.1 19.8 %collective-permute-start.3 = (bf16[128,768]{1,0:T(8,128)(2,1)S(1)}, bf16[128,768]{1,0:T(8,128)(2,1)}, u32[]{:S(2)}, u32[]{:S(2)}) collective-permute-start(bf16[128,768]{1,0:T(8,128)(2,1)S(1)} %get-tuple-element.226.refs_0_), channel_id=1, source_target_pairs={{0,1},{1,0},{2,3},{3,2},{4,5},{5,4},{6,7},{7,6},{8,9},{9,8},{10,11... | collective-permute-start | bytes 589832 | tf_op jit(solution)/shard_map/ppermute | solution.py:724
  13.5 16.9 %collective-permute-start.7 = (bf16[208,576]{1,0:T(8,128)(2,1)}, bf16[208,576]{1,0:T(8,128)(2,1)}, u32[]{:S(2)}, u32[]{:S(2)}) collective-permute-start(bf16[208,576]{1,0:T(8,128)(2,1)} %shard_map.246.refs_8_), channel_id=1, source_target_pairs={{0,8},{8,16},{16,24},{24,0},{1,9},{9,17},{17,25},{25,1},{2,10},{10... | collective-permute-start | bytes 718856 | tf_op jit(solution)/shard_map/ppermute | solution.py:716
  28.4 14.8 %collective-permute-start.9 = (bf16[208,576]{1,0:T(8,128)(2,1)}, bf16[208,576]{1,0:T(8,128)(2,1)}, u32[]{:S(2)}, u32[]{:S(2)}) collective-permute-start(bf16[208,576]{1,0:T(8,128)(2,1)} %shard_map.246.refs_8_), channel_id=1, source_target_pairs={{0,24},{8,0},{16,8},{24,16},{1,25},{9,1},{17,9},{25,17},{2,26},{10... | collective-permute-start | bytes 718856 | tf_op jit(solution)/shard_map/ppermute | solution.py:716
  29.8 13.9 %collective-permute-start.4 = (bf16[128,768]{1,0:T(8,128)(2,1)}, bf16[128,768]{1,0:T(8,128)(2,1)S(1)}, u32[]{:S(2)}, u32[]{:S(2)}) collective-permute-start(bf16[128,768]{1,0:T(8,128)(2,1)} %collective-permute-done.refs_1_), channel_id=1, source_target_pairs={{0,1},{1,0},{2,3},{3,2},{4,5},{5,4},{6,7},{7,6},{8,9},{9,8},{10,11... | collective-permute-start | bytes 589832 | tf_op jit(solution)/shard_map/ppermute | solution.py:724
  29.9 14.8 %collective-permute-start.5 = (bf16[128,768]{1,0:T(8,128)(2,1)}, bf16[128,768]{1,0:T(8,128)(2,1)S(1)}, u32[]{:S(2)}, u32[]{:S(2)}) collective-permute-start(bf16[128,768]{1,0:T(8,128)(2,1)} %collective-permute-done.1.refs_2_), channel_id=1, source_target_pairs={{0,1},{1,0},{2,3},{3,2},{4,5},{5,4},{6,7},{7,6},{8,9},{9,8},{10,11... | collective-permute-start | bytes 589832 | tf_op jit(solution)/shard_map/ppermute | solution.py:724
  30.3 15.4 %collective-permute-start.6 = (bf16[128,768]{1,0:T(8,128)(2,1)}, bf16[128,768]{1,0:T(8,128)(2,1)S(1)}, u32[]{:S(2)}, u32[]{:S(2)}) collective-permute-start(bf16[128,768]{1,0:T(8,128)(2,1)} %collective-permute-done.2.refs_3_), channel_id=1, source_target_pairs={{0,1},{1,0},{2,3},{3,2},{4,5},{5,4},{6,7},{7,6},{8,9},{9,8},{10,11... | collective-permute-start | bytes 589832 | tf_op jit(solution)/shard_map/ppermute | solution.py:724
  36.6 49.4 %collective-permute-start.17 = (bf16[192,768]{1,0:T(8,128)(2,1)S(1)}, bf16[192,768]{1,0:T(8,128)(2,1)S(1)}, u32[]{:S(2)}, u32[]{:S(2)}) collective-permute-start(bf16[192,768]{1,0:T(8,128)(2,1)S(1)} %copy-done.44), channel_id=1, source_target_pairs={{0,8},{8,16},{16,24},{24,0},{1,9},{9,17},{17,25},{25,1},{2,10},{10... | collective-permute-start | bytes 884744 | tf_op jit(solution)/shard_map/ppermute | solution.py:716
  43.2 43.4 %collective-permute-start.18 = (bf16[192,768]{1,0:T(8,128)(2,1)S(1)}, bf16[192,768]{1,0:T(8,128)(2,1)S(1)}, u32[]{:S(2)}, u32[]{:S(2)}) collective-permute-start(bf16[192,768]{1,0:T(8,128)(2,1)S(1)} %copy-done.44), channel_id=1, source_target_pairs={{0,16},{8,24},{16,0},{24,8},{1,17},{9,25},{17,1},{25,9},{2,18},{10... | collective-permute-start | bytes 884744 | tf_op jit(solution)/shard_map/ppermute | solution.py:716
  43.7 43.0 %collective-permute-start.19 = (bf16[192,768]{1,0:T(8,128)(2,1)S(1)}, bf16[192,768]{1,0:T(8,128)(2,1)S(1)}, u32[]{:S(2)}, u32[]{:S(2)}) collective-permute-start(bf16[192,768]{1,0:T(8,128)(2,1)S(1)} %copy-done.44), channel_id=1, source_target_pairs={{0,24},{8,0},{16,8},{24,16},{1,25},{9,1},{17,9},{25,17},{2,26},{10... | collective-permute-start | bytes 884744 | tf_op jit(solution)/shard_map/ppermute | solution.py:716
  44.7 41.3 %collective-permute-start.24 = (bf16[96,768]{1,0:T(8,128)(2,1)S(1)}, bf16[96,768]{1,0:T(8,128)(2,1)S(1)}, u32[]{:S(2)}, u32[]{:S(2)}) collective-permute-start(bf16[96,768]{1,0:T(8,128)(2,1)S(1)} %copy-done.57), channel_id=1, source_target_pairs={{0,8},{8,16},{16,24},{24,0},{1,9},{9,17},{17,25},{25,1},{2,10},{10... | collective-permute-start | bytes 442376 | tf_op jit(solution)/shard_map/ppermute | solution.py:716
  87.3 68.8 %collective-permute-start.28 = (bf16[3,192,1024]{2,1,0:T(8,128)(2,1)S(1)}, bf16[3,192,1024]{2,1,0:T(8,128)(2,1)S(1)}, u32[]{:S(2)}, u32[]{:S(2)}) collective-permute-start(bf16[3,192,1024]{2,1,0:T(8,128)(2,1)S(1)} %get-tuple-element.135), channel_id=1, source_target_pairs={{0,8},{8,16},{16,24},{24,0},{1,9},{9,17},{17,25},{25,1},{2,10},{10... | collective-permute-start | bytes 3538952 | tf_op jit(solution)/shard_map/ppermute | solution.py:716
  87.4 68.7 %collective-permute-start.29 = (bf16[3,192,1024]{2,1,0:T(8,128)(2,1)S(1)}, bf16[3,192,1024]{2,1,0:T(8,128)(2,1)S(1)}, u32[]{:S(2)}, u32[]{:S(2)}) collective-permute-start(bf16[3,192,1024]{2,1,0:T(8,128)(2,1)S(1)} %get-tuple-element.136), channel_id=1, source_target_pairs={{0,16},{8,24},{16,0},{24,8},{1,17},{9,25},{17,1},{25,9},{2,18},{10... | collective-permute-start | bytes 3538952 | tf_op jit(solution)/shard_map/ppermute | solution.py:716
  88.8 67.3 %collective-permute-start.30 = (bf16[3,192,1024]{2,1,0:T(8,128)(2,1)S(1)}, bf16[3,192,1024]{2,1,0:T(8,128)(2,1)S(1)}, u32[]{:S(2)}, u32[]{:S(2)}) collective-permute-start(bf16[3,192,1024]{2,1,0:T(8,128)(2,1)S(1)} %get-tuple-element.137), channel_id=1, source_target_pairs={{0,24},{8,0},{16,8},{24,16},{1,25},{9,1},{17,9},{25,17},{2,26},{10... | collective-permute-start | bytes 3538952 | tf_op jit(solution)/shard_map/ppermute | solution.py:716
  93.6 51.7 %collective-permute-start.20 = (bf16[96,896]{1,0:T(8,128)(2,1)S(1)}, bf16[96,896]{1,0:T(8,128)(2,1)S(1)}, u32[]{:S(2)}, u32[]{:S(2)}) collective-permute-start(bf16[96,896]{1,0:T(8,128)(2,1)S(1)} %get-tuple-element.124), channel_id=1, source_target_pairs={{0,8},{8,16},{16,24},{24,0},{1,9},{9,17},{17,25},{25,1},{2,10},{10... | collective-permute-start | bytes 516104 | tf_op jit(solution)/shard_map/ppermute | solution.py:716
  93.8 54.5 %collective-permute-start.21 = (bf16[96,896]{1,0:T(8,128)(2,1)S(1)}, bf16[96,896]{1,0:T(8,128)(2,1)S(1)}, u32[]{:S(2)}, u32[]{:S(2)}) collective-permute-start(bf16[96,896]{1,0:T(8,128)(2,1)S(1)} %get-tuple-element.125), channel_id=1, source_target_pairs={{0,16},{8,24},{16,0},{24,8},{1,17},{9,25},{17,1},{25,9},{2,18},{10... | collective-permute-start | bytes 516104 | tf_op jit(solution)/shard_map/ppermute | solution.py:716
  170.0 20.3 %collective-permute-start.31 = (bf16[2,384,768]{2,1,0:T(8,128)(2,1)S(1)}, bf16[2,384,768]{2,1,0:T(8,128)(2,1)S(1)}, u32[]{:S(2)}, u32[]{:S(2)}) collective-permute-start(bf16[2,384,768]{2,1,0:T(8,128)(2,1)S(1)} %get-tuple-element.139), channel_id=1, source_target_pairs={{0,1},{1,0},{2,3},{3,2},{4,5},{5,4},{6,7},{7,6},{8,9},{9,8},{10,11... | collective-permute-start | bytes 3538952 | tf_op jit(solution)/shard_map/ppermute | solution.py:724
  170.2 20.1 %collective-permute-start.35 = (bf16[384,896]{1,0:T(8,128)(2,1)S(1)}, bf16[384,896]{1,0:T(8,128)(2,1)S(1)}, u32[]{:S(2)}, u32[]{:S(2)}) collective-permute-start(bf16[384,896]{1,0:T(8,128)(2,1)S(1)} %constant_dynamic-update-slice_fusion.rows_a), channel_id=1, source_target_pairs={{0,2},{1,3},{2,4},{3,5},{4,6},{5,7},{6,0},{7,1},{8,10},{9,11},{10,... | collective-permute-start | bytes 2064392 | tf_op jit(solution)/shard_map/ppermute | solution.py:719
  170.2 32.7 %collective-permute-start.36 = (bf16[384,768]{1,0:T(8,128)(2,1)S(1)}, bf16[384,768]{1,0:T(8,128)(2,1)S(1)}, u32[]{:S(2)}, u32[]{:S(2)}) collective-permute-start(bf16[384,768]{1,0:T(8,128)(2,1)S(1)} %constant_dynamic-update-slice_fusion.4.g_a), channel_id=1, source_target_pairs={{0,2},{1,3},{2,4},{3,5},{4,6},{5,7},{6,0},{7,1},{8,10},{9,11},{10,... | collective-permute-start | bytes 1769480 | tf_op jit(solution)/shard_map/ppermute | solution.py:719
  190.3 27.5 %collective-permute-start.39 = (bf16[384,896]{1,0:T(8,128)(2,1)S(1)}, bf16[384,896]{1,0:T(8,128)(2,1)S(1)}, u32[]{:S(2)}, u32[]{:S(2)}) collective-permute-start(bf16[384,896]{1,0:T(8,128)(2,1)S(1)} %collective-permute-done.35.rows_a), channel_id=1, source_target_pairs={{0,2},{1,3},{2,4},{3,5},{4,6},{5,7},{6,0},{7,1},{8,10},{9,11},{10,... | collective-permute-start | bytes 2064392 | tf_op jit(solution)/shard_map/ppermute | solution.py:719
  190.7 28.0 %collective-permute-start.32 = (bf16[2,96,768]{2,1,0:T(8,128)(2,1)S(1)}, bf16[2,96,768]{2,1,0:T(8,128)(2,1)S(1)}, u32[]{:S(2)}, u32[]{:S(2)}) collective-permute-start(bf16[2,96,768]{2,1,0:T(8,128)(2,1)S(1)} %get-tuple-element.221), channel_id=1, source_target_pairs={{0,24},{8,0},{16,8},{24,16},{1,25},{9,1},{17,9},{25,17},{2,26},{10... | collective-permute-start | bytes 884744 | tf_op jit(solution)/shard_map/ppermute | solution.py:716
  192.0 27.8 %collective-permute-start.33 = (bf16[2,96,768]{2,1,0:T(8,128)(2,1)S(1)}, bf16[2,96,768]{2,1,0:T(8,128)(2,1)S(1)}, u32[]{:S(2)}, u32[]{:S(2)}) collective-permute-start(bf16[2,96,768]{2,1,0:T(8,128)(2,1)S(1)} %get-tuple-element.220), channel_id=1, source_target_pairs={{0,16},{8,24},{16,0},{24,8},{1,17},{9,25},{17,1},{25,9},{2,18},{10... | collective-permute-start | bytes 884744 | tf_op jit(solution)/shard_map/ppermute | solution.py:716
  192.8 27.0 %collective-permute-start.34 = (bf16[2,96,768]{2,1,0:T(8,128)(2,1)S(1)}, bf16[2,96,768]{2,1,0:T(8,128)(2,1)S(1)}, u32[]{:S(2)}, u32[]{:S(2)}) collective-permute-start(bf16[2,96,768]{2,1,0:T(8,128)(2,1)S(1)} %get-tuple-element.219), channel_id=1, source_target_pairs={{0,8},{8,16},{16,24},{24,0},{1,9},{9,17},{17,25},{25,1},{2,10},{10... | collective-permute-start | bytes 884744 | tf_op jit(solution)/shard_map/ppermute | solution.py:716
  202.9 40.2 %collective-permute-start.40 = (bf16[384,768]{1,0:T(8,128)(2,1)S(1)}, bf16[384,768]{1,0:T(8,128)(2,1)S(1)}, u32[]{:S(2)}, u32[]{:S(2)}) collective-permute-start(bf16[384,768]{1,0:T(8,128)(2,1)S(1)} %constant_dynamic-update-slice_fusion.4.g_a), channel_id=1, source_target_pairs={{0,4},{1,5},{2,6},{3,7},{4,0},{5,1},{6,2},{7,3},{8,12},{9,13},{10,... | collective-permute-start | bytes 1769480 | tf_op jit(solution)/shard_map/ppermute | solution.py:719
  217.8 41.4 %collective-permute-start.44 = (bf16[384,768]{1,0:T(8,128)(2,1)S(1)}, bf16[384,768]{1,0:T(8,128)(2,1)S(1)}, u32[]{:S(2)}, u32[]{:S(2)}) collective-permute-start(bf16[384,768]{1,0:T(8,128)(2,1)S(1)} %constant_dynamic-update-slice_fusion.4.g_a), channel_id=1, source_target_pairs={{0,6},{1,7},{2,0},{3,1},{4,2},{5,3},{6,4},{7,5},{8,14},{9,15},{10,... | collective-permute-start | bytes 1769480 | tf_op jit(solution)/shard_map/ppermute | solution.py:719
  218.7 40.4 %collective-permute-start.43 = (bf16[384,896]{1,0:T(8,128)(2,1)S(1)}, bf16[384,896]{1,0:T(8,128)(2,1)S(1)}, u32[]{:S(2)}, u32[]{:S(2)}) collective-permute-start(bf16[384,896]{1,0:T(8,128)(2,1)S(1)} %collective-permute-done.39.rows_a), channel_id=1, source_target_pairs={{0,2},{1,3},{2,4},{3,5},{4,6},{5,7},{6,0},{7,1},{8,10},{9,11},{10,... | collective-permute-start | bytes 2064392 | tf_op jit(solution)/shard_map/ppermute | solution.py:719
  219.8 40.0 %collective-permute-start.37 = (bf16[384,896]{1,0:T(8,128)(2,1)S(1)}, bf16[384,896]{1,0:T(8,128)(2,1)S(1)}, u32[]{:S(2)}, u32[]{:S(2)}) collective-permute-start(bf16[384,896]{1,0:T(8,128)(2,1)S(1)} %collective-permute-done.35.rows_a), channel_id=1, source_target_pairs={{0,1},{1,0},{2,3},{3,2},{4,5},{5,4},{6,7},{7,6},{8,9},{9,8},{10,11... | collective-permute-start | bytes 2064392 | tf_op jit(solution)/shard_map/ppermute | solution.py:724
  219.8 39.5 %collective-permute-start.38 = (bf16[384,768]{1,0:T(8,128)(2,1)S(1)}, bf16[384,768]{1,0:T(8,128)(2,1)S(1)}, u32[]{:S(2)}, u32[]{:S(2)}) collective-permute-start(bf16[384,768]{1,0:T(8,128)(2,1)S(1)} %collective-permute-done.36.g_a), channel_id=1, source_target_pairs={{0,1},{1,0},{2,3},{3,2},{4,5},{5,4},{6,7},{7,6},{8,9},{9,8},{10,11... | collective-permute-start | bytes 1769480 | tf_op jit(solution)/shard_map/ppermute | solution.py:724
  243.1 46.8 %collective-permute-start.42 = (bf16[384,768]{1,0:T(8,128)(2,1)S(1)}, bf16[384,768]{1,0:T(8,128)(2,1)S(1)}, u32[]{:S(2)}, u32[]{:S(2)}) collective-permute-start(bf16[384,768]{1,0:T(8,128)(2,1)S(1)} %collective-permute-done.40.g_a), channel_id=1, source_target_pairs={{0,1},{1,0},{2,3},{3,2},{4,5},{5,4},{6,7},{7,6},{8,9},{9,8},{10,11... | collective-permute-start | bytes 1769480 | tf_op jit(solution)/shard_map/ppermute | solution.py:724
  259.2 14.9 %collective-permute-start.47 = (bf16[2,128,192]{2,1,0:T(8,128)(2,1)S(1)}, bf16[2,128,192]{2,1,0:T(8,128)(2,1)S(1)}, u32[]{:S(2)}, u32[]{:S(2)}) collective-permute-start(bf16[2,128,192]{2,1,0:T(8,128)(2,1)S(1)} %get-tuple-element.172), channel_id=1, source_target_pairs={{0,6},{1,7},{2,0},{3,1},{4,2},{5,3},{6,4},{7,5},{8,14},{9,15},{10,... | collective-permute-start | bytes 294920 | tf_op jit(solution)/shard_map/ppermute | solution.py:719
  259.3 31.9 %collective-permute-start.41 = (bf16[384,896]{1,0:T(8,128)(2,1)S(1)}, bf16[384,896]{1,0:T(8,128)(2,1)S(1)}, u32[]{:S(2)}, u32[]{:S(2)}) collective-permute-start(bf16[384,896]{1,0:T(8,128)(2,1)S(1)} %collective-permute-done.39.rows_a), channel_id=1, source_target_pairs={{0,1},{1,0},{2,3},{3,2},{4,5},{5,4},{6,7},{7,6},{8,9},{9,8},{10,11... | collective-permute-start | bytes 2064392 | tf_op jit(solution)/shard_map/ppermute | solution.py:724
  259.8 31.9 %collective-permute-start.45 = (bf16[384,896]{1,0:T(8,128)(2,1)S(1)}, bf16[384,896]{1,0:T(8,128)(2,1)S(1)}, u32[]{:S(2)}, u32[]{:S(2)}) collective-permute-start(bf16[384,896]{1,0:T(8,128)(2,1)S(1)} %collective-permute-done.43.rows_a), channel_id=1, source_target_pairs={{0,1},{1,0},{2,3},{3,2},{4,5},{5,4},{6,7},{7,6},{8,9},{9,8},{10,11... | collective-permute-start | bytes 2064392 | tf_op jit(solution)/shard_map/ppermute | solution.py:724
  260.5 30.6 %collective-permute-start.46 = (bf16[384,768]{1,0:T(8,128)(2,1)S(1)}, bf16[384,768]{1,0:T(8,128)(2,1)S(1)}, u32[]{:S(2)}, u32[]{:S(2)}) collective-permute-start(bf16[384,768]{1,0:T(8,128)(2,1)S(1)} %collective-permute-done.44.g_a), channel_id=1, source_target_pairs={{0,1},{1,0},{2,3},{3,2},{4,5},{5,4},{6,7},{7,6},{8,9},{9,8},{10,11... | collective-permute-start | bytes 1769480 | tf_op jit(solution)/shard_map/ppermute | solution.py:724
  289.4 66.0 %collective-permute-start.64 = (bf16[208,768]{1,0:T(8,128)(2,1)}, bf16[208,768]{1,0:T(8,128)(2,1)}, u32[]{:S(2)}, u32[]{:S(2)}) collective-permute-start(bf16[208,768]{1,0:T(8,128)(2,1)} %get-tuple-element.196), channel_id=1, source_target_pairs={{0,8},{8,16},{16,24},{24,0},{1,9},{9,17},{17,25},{25,1},{2,10},{10... | collective-permute-start | bytes 958472 | tf_op jit(solution)/shard_map/ppermute | solution.py:716
  289.9 68.4 %collective-permute-start.65 = (bf16[208,768]{1,0:T(8,128)(2,1)}, bf16[208,768]{1,0:T(8,128)(2,1)}, u32[]{:S(2)}, u32[]{:S(2)}) collective-permute-start(bf16[208,768]{1,0:T(8,128)(2,1)} %get-tuple-element.197), channel_id=1, source_target_pairs={{0,16},{8,24},{16,0},{24,8},{1,17},{9,25},{17,1},{25,9},{2,18},{10... | collective-permute-start | bytes 958472 | tf_op jit(solution)/shard_map/ppermute | solution.py:716
  291.1 35.4 %collective-permute-start.51 = (bf16[128,192]{1,0:T(8,128)(2,1)S(1)}, bf16[128,192]{1,0:T(8,128)(2,1)S(1)}, u32[]{:S(2)}, u32[]{:S(2)}) collective-permute-start(bf16[128,192]{1,0:T(8,128)(2,1)S(1)} %slice_bitcast_fusion.6), channel_id=1, source_target_pairs={{0,1},{1,0},{2,3},{3,2},{4,5},{5,4},{6,7},{7,6},{8,9},{9,8},{10,11... | collective-permute-start | bytes 147464 | tf_op jit(solution)/shard_map/ppermute | solution.py:724
  291.2 35.3 %collective-permute-start.52 = (bf16[128,192]{1,0:T(8,128)(2,1)S(1)}, bf16[128,192]{1,0:T(8,128)(2,1)S(1)}, u32[]{:S(2)}, u32[]{:S(2)}) collective-permute-start(bf16[128,192]{1,0:T(8,128)(2,1)S(1)} %slice_bitcast_fusion.5), channel_id=1, source_target_pairs={{0,1},{1,0},{2,3},{3,2},{4,5},{5,4},{6,7},{7,6},{8,9},{9,8},{10,11... | collective-permute-start | bytes 147464 | tf_op jit(solution)/shard_map/ppermute | solution.py:724
  291.7 34.8 %collective-permute-start.53 = (bf16[128,192]{1,0:T(8,128)(2,1)S(1)}, bf16[128,192]{1,0:T(8,128)(2,1)S(1)}, u32[]{:S(2)}, u32[]{:S(2)}) collective-permute-start(bf16[128,192]{1,0:T(8,128)(2,1)S(1)} %slice_bitcast_fusion.4), channel_id=1, source_target_pairs={{0,1},{1,0},{2,3},{3,2},{4,5},{5,4},{6,7},{7,6},{8,9},{9,8},{10,11... | collective-permute-start | bytes 147464 | tf_op jit(solution)/shard_map/ppermute | solution.py:724
  352.2 15.6 %collective-permute-start.59 = (bf16[208,576]{1,0:T(8,128)(2,1)S(1)}, bf16[208,576]{1,0:T(8,128)(2,1)S(1)}, u32[]{:S(2)}, u32[]{:S(2)}) collective-permute-start(bf16[208,576]{1,0:T(8,128)(2,1)S(1)} %get-tuple-element.191), channel_id=1, source_target_pairs={{0,16},{8,24},{16,0},{24,8},{1,17},{9,25},{17,1},{25,9},{2,18},{10... | collective-permute-start | bytes 718856 | tf_op jit(solution)/shard_map/ppermute | solution.py:716
  355.4 13.0 %collective-permute-start.58 = (bf16[208,576]{1,0:T(8,128)(2,1)S(1)}, bf16[208,576]{1,0:T(8,128)(2,1)S(1)}, u32[]{:S(2)}, u32[]{:S(2)}) collective-permute-start(bf16[208,576]{1,0:T(8,128)(2,1)S(1)} %get-tuple-element.190), channel_id=1, source_target_pairs={{0,8},{8,16},{16,24},{24,0},{1,9},{9,17},{17,25},{25,1},{2,10},{10... | collective-permute-start | bytes 718856 | tf_op jit(solution)/shard_map/ppermute | solution.py:716
  355.4 18.7 %collective-permute-start.66 = (bf16[208,768]{1,0:T(8,128)(2,1)S(1)}, bf16[208,768]{1,0:T(8,128)(2,1)S(1)}, u32[]{:S(2)}, u32[]{:S(2)}) collective-permute-start(bf16[208,768]{1,0:T(8,128)(2,1)S(1)} %copy-done.51), channel_id=1, source_target_pairs={{0,24},{8,0},{16,8},{24,16},{1,25},{9,1},{17,9},{25,17},{2,26},{10... | collective-permute-start | bytes 958472 | tf_op jit(solution)/shard_map/ppermute | solution.py:716
  358.3 39.6 %collective-permute-start.54 = (bf16[4,128,768]{2,1,0:T(8,128)(2,1)}, bf16[4,128,768]{2,1,0:T(8,128)(2,1)S(1)}, u32[]{:S(2)}, u32[]{:S(2)}) collective-permute-start(bf16[4,128,768]{2,1,0:T(8,128)(2,1)} %get-tuple-element.183), channel_id=1, source_target_pairs={{0,1},{1,0},{2,3},{3,2},{4,5},{5,4},{6,7},{7,6},{8,9},{9,8},{10,11... | collective-permute-start | bytes 2359304 | tf_op jit(solution)/shard_map/ppermute | solution.py:724
  361.5 33.7 %collective-permute-start.70 = (bf16[3,192,512]{2,1,0:T(8,128)(2,1)}, bf16[3,192,512]{2,1,0:T(8,128)(2,1)S(1)}, u32[]{:S(2)}, u32[]{:S(2)}) collective-permute-start(bf16[3,192,512]{2,1,0:T(8,128)(2,1)} %get-tuple-element.203), channel_id=1, source_target_pairs={{0,24},{8,0},{16,8},{24,16},{1,25},{9,1},{17,9},{25,17},{2,26},{10... | collective-permute-start | bytes 1769480 | tf_op jit(solution)/shard_map/ppermute | solution.py:716
  367.8 31.2 %collective-permute-start.72 = (bf16[3,192,512]{2,1,0:T(8,128)(2,1)}, bf16[3,192,512]{2,1,0:T(8,128)(2,1)S(1)}, u32[]{:S(2)}, u32[]{:S(2)}) collective-permute-start(bf16[3,192,512]{2,1,0:T(8,128)(2,1)} %get-tuple-element.204), channel_id=1, source_target_pairs={{0,8},{8,16},{16,24},{24,0},{1,9},{9,17},{17,25},{25,1},{2,10},{10... | collective-permute-start | bytes 1769480 | tf_op jit(solution)/shard_map/ppermute | solution.py:716
  368.4 33.6 %collective-permute-start.73 = (bf16[3,192,512]{2,1,0:T(8,128)(2,1)}, bf16[3,192,512]{2,1,0:T(8,128)(2,1)S(1)}, u32[]{:S(2)}, u32[]{:S(2)}) collective-permute-start(bf16[3,192,512]{2,1,0:T(8,128)(2,1)} %get-tuple-element.205), channel_id=1, source_target_pairs={{0,16},{8,24},{16,0},{24,8},{1,17},{9,25},{17,1},{25,9},{2,18},{10... | collective-permute-start | bytes 1769480 | tf_op jit(solution)/shard_map/ppermute | solution.py:716
  374.1 11.6 %collective-permute-start.61 = (bf16[208,576]{1,0:T(8,128)(2,1)S(1)}, bf16[208,576]{1,0:T(8,128)(2,1)S(1)}, u32[]{:S(2)}, u32[]{:S(2)}) collective-permute-start(bf16[208,576]{1,0:T(8,128)(2,1)S(1)} %add_convert_fusion.6), channel_id=1, source_target_pairs={{0,4},{1,5},{2,6},{3,7},{4,0},{5,1},{6,2},{7,3},{8,12},{9,13},{10,... | collective-permute-start | bytes 718856 | tf_op jit(solution)/shard_map/ppermute | solution.py:1018
  385.6 17.7 %collective-permute-start.74 = (bf16[3,192,512]{2,1,0:T(8,128)(2,1)S(1)}, bf16[3,192,512]{2,1,0:T(8,128)(2,1)S(1)}, u32[]{:S(2)}, u32[]{:S(2)}) collective-permute-start(bf16[3,192,512]{2,1,0:T(8,128)(2,1)S(1)} %get-tuple-element.170.refs_0_), channel_id=1, source_target_pairs={{0,1},{1,0},{2,3},{3,2},{4,5},{5,4},{6,7},{7,6},{8,9},{9,8},{10,11... | collective-permute-start | bytes 1769480 | tf_op jit(solution)/shard_map/ppermute | solution.py:724
  395.2 17.2 %collective-permute-start.77 = (bf16[3,192,512]{2,1,0:T(8,128)(2,1)S(1)}, bf16[3,192,512]{2,1,0:T(8,128)(2,1)S(1)}, u32[]{:S(2)}, u32[]{:S(2)}) collective-permute-start(bf16[3,192,512]{2,1,0:T(8,128)(2,1)S(1)} %get-tuple-element.207), channel_id=1, source_target_pairs={{0,8},{8,16},{16,24},{24,0},{1,9},{9,17},{17,25},{25,1},{2,10},{10... | collective-permute-start | bytes 1769480 | tf_op jit(solution)/shard_map/ppermute | solution.py:716
  397.9 26.6 %collective-permute-start.78 = (bf16[3,192,512]{2,1,0:T(8,128)(2,1)S(1)}, bf16[3,192,512]{2,1,0:T(8,128)(2,1)S(1)}, u32[]{:S(2)}, u32[]{:S(2)}) collective-permute-start(bf16[3,192,512]{2,1,0:T(8,128)(2,1)S(1)} %get-tuple-element.208), channel_id=1, source_target_pairs={{0,16},{8,24},{16,0},{24,8},{1,17},{9,25},{17,1},{25,9},{2,18},{10... | collective-permute-start | bytes 1769480 | tf_op jit(solution)/shard_map/ppermute | solution.py:716
  399.0 25.6 %collective-permute-start.79 = (bf16[3,192,512]{2,1,0:T(8,128)(2,1)S(1)}, bf16[3,192,512]{2,1,0:T(8,128)(2,1)S(1)}, u32[]{:S(2)}, u32[]{:S(2)}) collective-permute-start(bf16[3,192,512]{2,1,0:T(8,128)(2,1)S(1)} %get-tuple-element.209), channel_id=1, source_target_pairs={{0,24},{8,0},{16,8},{24,16},{1,25},{9,1},{17,9},{25,17},{2,26},{10... | collective-permute-start | bytes 1769480 | tf_op jit(solution)/shard_map/ppermute | solution.py:716
  402.0 22.6 %collective-permute-start.80 = (bf16[3,192,512]{2,1,0:T(8,128)(2,1)S(1)}, bf16[3,192,512]{2,1,0:T(8,128)(2,1)S(1)}, u32[]{:S(2)}, u32[]{:S(2)}) collective-permute-start(bf16[3,192,512]{2,1,0:T(8,128)(2,1)S(1)} %get-tuple-element.206.refs_0_), channel_id=1, source_target_pairs={{0,1},{1,0},{2,3},{3,2},{4,5},{5,4},{6,7},{7,6},{8,9},{9,8},{10,11... | collective-permute-start | bytes 1769480 | tf_op jit(solution)/shard_map/ppermute | solution.py:724
  403.3 29.9 %collective-permute-start.67 = (bf16[208,768]{1,0:T(8,128)(2,1)S(1)}, bf16[208,768]{1,0:T(8,128)(2,1)S(1)}, u32[]{:S(2)}, u32[]{:S(2)}) collective-permute-start(bf16[208,768]{1,0:T(8,128)(2,1)S(1)} %add_convert_fusion.4), channel_id=1, source_target_pairs={{0,1},{1,0},{2,3},{3,2},{4,5},{5,4},{6,7},{7,6},{8,9},{9,8},{10,11... | collective-permute-start | bytes 958472 | tf_op jit(solution)/shard_map/ppermute | solution.py:1010
  412.4 12.7 %collective-permute-start.62 = (bf16[1,208,576]{2,1,0:T(8,128)(2,1)S(1)}, bf16[1,208,576]{2,1,0:T(8,128)(2,1)S(1)}, u32[]{:S(2)}, u32[]{:S(2)}) collective-permute-start(bf16[1,208,576]{2,1,0:T(8,128)(2,1)S(1)} %fusion.1.refs_0_), channel_id=1, source_target_pairs={{0,1},{1,0},{2,3},{3,2},{4,5},{5,4},{6,7},{7,6},{8,9},{9,8},{10,11... | collective-permute-start | bytes 718856 | tf_op jit(solution)/shard_map/ppermute | solution.py:1024
  424.6 20.6 %collective-permute-start.81 = (bf16[3,192,512]{2,1,0:T(8,128)(2,1)S(1)}, bf16[3,192,512]{2,1,0:T(8,128)(2,1)S(1)}, u32[]{:S(2)}, u32[]{:S(2)}) collective-permute-start(bf16[3,192,512]{2,1,0:T(8,128)(2,1)S(1)} %collective-permute-done.77.refs_1_), channel_id=1, source_target_pairs={{0,1},{1,0},{2,3},{3,2},{4,5},{5,4},{6,7},{7,6},{8,9},{9,8},{10,11... | collective-permute-start | bytes 1769480 | tf_op jit(solution)/shard_map/ppermute | solution.py:724
  424.6 21.1 %collective-permute-start.82 = (bf16[3,192,512]{2,1,0:T(8,128)(2,1)S(1)}, bf16[3,192,512]{2,1,0:T(8,128)(2,1)S(1)}, u32[]{:S(2)}, u32[]{:S(2)}) collective-permute-start(bf16[3,192,512]{2,1,0:T(8,128)(2,1)S(1)} %collective-permute-done.78.refs_2_), channel_id=1, source_target_pairs={{0,1},{1,0},{2,3},{3,2},{4,5},{5,4},{6,7},{7,6},{8,9},{9,8},{10,11... | collective-permute-start | bytes 1769480 | tf_op jit(solution)/shard_map/ppermute | solution.py:724
  425.1 27.9 %collective-permute-start.83 = (bf16[3,192,512]{2,1,0:T(8,128)(2,1)S(1)}, bf16[3,192,512]{2,1,0:T(8,128)(2,1)S(1)}, u32[]{:S(2)}, u32[]{:S(2)}) collective-permute-start(bf16[3,192,512]{2,1,0:T(8,128)(2,1)S(1)} %collective-permute-done.79.refs_3_), channel_id=1, source_target_pairs={{0,1},{1,0},{2,3},{3,2},{4,5},{5,4},{6,7},{7,6},{8,9},{9,8},{10,11... | collective-permute-start | bytes 1769480 | tf_op jit(solution)/shard_map/ppermute | solution.py:724
  433.2 12.0 %collective-permute-start.57 = (bf16[128,768]{1,0:T(8,128)(2,1)S(1)}, bf16[128,768]{1,0:T(8,128)(2,1)S(1)}, u32[]{:S(2)}, u32[]{:S(2)}) collective-permute-start(bf16[128,768]{1,0:T(8,128)(2,1)S(1)} %get-tuple-element.187), channel_id=1, source_target_pairs={{0,6},{1,7},{2,0},{3,1},{4,2},{5,3},{6,4},{7,5},{8,14},{9,15},{10,... | collective-permute-start | bytes 589832 | tf_op jit(solution)/shard_map/ppermute | solution.py:719
  445.2 21.3 %collective-permute-start.71 = (bf16[3,192,512]{2,1,0:T(8,128)(2,1)S(1)}, bf16[3,192,512]{2,1,0:T(8,128)(2,1)S(1)}, u32[]{:S(2)}, u32[]{:S(2)}) collective-permute-start(bf16[3,192,512]{2,1,0:T(8,128)(2,1)S(1)} %collective-permute-done.70.refs_0_), channel_id=1, source_target_pairs={{0,1},{1,0},{2,3},{3,2},{4,5},{5,4},{6,7},{7,6},{8,9},{9,8},{10,11... | collective-permute-start | bytes 1769480 | tf_op jit(solution)/shard_map/ppermute | solution.py:724
  445.2 17.7 %collective-permute-start.75 = (bf16[3,192,512]{2,1,0:T(8,128)(2,1)S(1)}, bf16[3,192,512]{2,1,0:T(8,128)(2,1)S(1)}, u32[]{:S(2)}, u32[]{:S(2)}) collective-permute-start(bf16[3,192,512]{2,1,0:T(8,128)(2,1)S(1)} %collective-permute-done.72.refs_1_), channel_id=1, source_target_pairs={{0,1},{1,0},{2,3},{3,2},{4,5},{5,4},{6,7},{7,6},{8,9},{9,8},{10,11... | collective-permute-start | bytes 1769480 | tf_op jit(solution)/shard_map/ppermute | solution.py:724
  445.8 17.2 %collective-permute-start.76 = (bf16[3,192,512]{2,1,0:T(8,128)(2,1)S(1)}, bf16[3,192,512]{2,1,0:T(8,128)(2,1)S(1)}, u32[]{:S(2)}, u32[]{:S(2)}) collective-permute-start(bf16[3,192,512]{2,1,0:T(8,128)(2,1)S(1)} %collective-permute-done.73.refs_2_), channel_id=1, source_target_pairs={{0,1},{1,0},{2,3},{3,2},{4,5},{5,4},{6,7},{7,6},{8,9},{9,8},{10,11... | collective-permute-start | bytes 1769480 | tf_op jit(solution)/shard_map/ppermute | solution.py:724
  451.9 19.3 %collective-permute-start.63 = (bf16[2,208,576]{2,1,0:T(8,128)(2,1)S(1)}, bf16[2,208,576]{2,1,0:T(8,128)(2,1)S(1)}, u32[]{:S(2)}, u32[]{:S(2)}) collective-permute-start(bf16[2,208,576]{2,1,0:T(8,128)(2,1)S(1)} %pad_maximum_fusion), channel_id=1, source_target_pairs={{0,2},{1,3},{2,0},{3,1},{4,6},{5,7},{6,4},{7,5},{8,10},{9,11},{10,... | collective-permute-start | bytes 1437704 | tf_op jit(solution)/shard_map/ppermute | solution.py:1024
  453.0 20.3 %collective-permute-start.69 = (bf16[208,768]{1,0:T(8,128)(2,1)S(1)}, bf16[208,768]{1,0:T(8,128)(2,1)S(1)}, u32[]{:S(2)}, u32[]{:S(2)}) collective-permute-start(bf16[208,768]{1,0:T(8,128)(2,1)S(1)} %add_convert_fusion.2), channel_id=1, source_target_pairs={{0,4},{1,5},{2,6},{3,7},{4,0},{5,1},{6,2},{7,3},{8,12},{9,13},{10,... | collective-permute-start | bytes 958472 | tf_op jit(solution)/shard_map/ppermute | solution.py:1010
  (87 other events, 1546.1 us)
where the time goes:
time: 486 us; the launch traced here: 477 us
  waiting for transfers between devices  253 us (52%)
  Pallas kernels  121 us (25%)
  starting transfers between devices  64 us (13%)
  local copies, waits for them, and re-layouts  30.2 us (6%)
  other arithmetic  6.2 us (1%)
    ppermute x18, waiting for transfers between devices, zs(): lax.ppermute(t, 'ctx', [(2 * i + j, 2 * ((i + k) % Z) + j) for i in range...  137 us
    ppermute x30, waiting for transfers between devices, fs(): return lax.ppermute(t, 'fsdp', [(i, (i + k) % F) for i in range(F)])  92.5 us
    pallas_call x10, Pallas kernels, call(): pl.pallas_call(kernel, out_shape=out_shape, in_specs=[SMEM] * smem + [VME...  53.3 us
    ppermute x30, starting transfers between devices, fs(): return lax.ppermute(t, 'fsdp', [(i, (i + k) % F) for i in range(F)])  39.5 us
    pallas_call x4, Pallas kernels, ffn(): pl.pallas_call(functools.partial(ffn_kernel, (F, D), own_plane), out_shap...  38 us
    pallas_call x2, Pallas kernels, body(): pl.pallas_call(functools.partial(weight_kernel, (F, D, Z)), out_shape=(sh...  19.8 us
    unnamed x143, local copies, waits for them, and re-layouts  18 us
    ppermute x18, starting transfers between devices, zs(): lax.ppermute(t, 'ctx', [(2 * i + j, 2 * ((i + k) % Z) + j) for i in range...  11.7 us
  transfers between devices with their start and end apart: 84, of which 31 were waited for; matrix products, arithmetic and copies ran while one was open for 3% of the time, Pallas kernels for 23%

commit v1 on v0

--- a/solution.py
+++ b/solution.py
@@ -46,25 +46,31 @@
 
 
 GRANTS = {
-    "pack": 3,
-    "grad_rows": 3,
-    "order": 8,
-    "attend": 14,
-    "dispatch": 6,
-    "experts0": 24,
-    "experts": 14,
-    "combine": 16,
-    "expert_grads": 18,
-    "attend_back": 20,
-    "pair": 3,
-    "input_grad": 6,
-    "place": 13,
-    "qkv_grad": 5,
+    "pack": 4,
+    "stack": 2,
+    "order": 4,
+    "attend": 10,
+    "dispatch": 4,
+    "experts0": 20,
+    "experts": 11,
+    "combine": 12,
+    "expert_grads": 14,
+    "attend_back": 16,
+    "normed_grad": 3,
+    "pair": 2,
+    "input_grad": 4,
+    "place": 18,
+    "qkv_grad": 4,
 }
 
 
 def params(name, long=False):
     return pltpu.CompilerParams(vmem_limit_bytes=(56 if long else GRANTS[name]) << 20)
+
+
+def place_of():
+    c = lax.axis_index("ctx")
+    return lax.div(c, 2), lax.rem(c, 2), lax.axis_index("fsdp"), c
 
 
 def norm_of(tile):
@@ -76,11 +82,15 @@
     return high, (t - high.astype(F32)).astype(BF)
 
 
-def pack_kernel(dims, meta, w_qkv, gain_a, gain_f, router, mix, vec, first):
-    F, D, G, hpd = dims
+def pack_kernel(dims, grad, routes, w_qkv, gains, router, mix, vec, slots, *outs):
+    F, S, R, D, G, hpd, expert_of = dims
     hw = hpd * HD
+    _, _, f, c = place_of()
     d_local = D // F
-    group = lax.rem(meta[3], G)
+    top = S * MOST
+    outs, table = outs[:F], outs[F]
+    group = lax.rem(c, G)
+    own = outs[0]
     for g in range(G):
         width = max(0, min(hw, H * HD - g * hw))
 
@@ -88,23 +98,20 @@
         def _():
             for part in range(3):
                 if width:
-                    first[:d_local, part * hw : part * hw + width] = w_qkv[
+                    own[top : top + d_local, part * hw : part * hw + width] = w_qkv[
                         :, part * H * HD + g * hw : part * H * HD + g * hw + width
                     ]
                 if width < hw:
-                    first[:d_local, part * hw + width : (part + 1) * hw] = jnp.zeros(
+                    own[top : top + d_local, part * hw + width : (part + 1) * hw] = jnp.zeros(
                         (d_local, hw - width), BF
                     )
 
-    rows = [t[...].astype(F32) for t in (gain_a, gain_f, router, mix, vec)]
-    first[d_local:, :d_local] = jnp.concatenate(rows, axis=0).astype(BF)
-    if d_local < 3 * hw:
-        first[d_local:, d_local:] = jnp.zeros((16, 3 * hw - d_local), BF)
-
-
-def grad_rows_kernel(dims, meta, grad, routes, slots, *outs):
-    F, S, R, _, expert_of = dims
-    table = outs[-1]
+    rows = [t[...].astype(F32) for t in (gains, router, mix, vec)]
+    own[top + d_local :, :d_local] = jnp.concatenate(rows, axis=0).astype(BF)
+    own[top + d_local :, d_local:] = jnp.zeros((16, D - d_local), BF)
+    own[top : top + d_local, 3 * hw :] = jnp.zeros((d_local, D - 3 * hw), BF)
+    for k in range(1, F):
+        outs[k][top:, :] = own[top:, :]
     below = lax.broadcasted_iota(jnp.int32, (R, R), 0)
     earlier = (below < lax.broadcasted_iota(jnp.int32, (R, R), 1)).astype(F32).astype(BF)
     expert = lax.broadcasted_iota(jnp.int32, (8, R), 0)
@@ -124,10 +131,17 @@
         for e in range(NF):
             table[e, s * MOST : (s + 1) * MOST, :] = moved[e * MOST : (e + 1) * MOST, :]
     for k in range(F):
-        outs[k][...] = table[expert_of(lax.rem(meta[2] + k, F))]
-
-
-def order_kernel(dims, meta, *refs):
+        outs[k][:top, :] = table[expert_of(lax.rem(f + k, F))]
+
+
+def stack_kernel(n, *refs):
+    out = refs[-1]
+    for i, ref in enumerate(refs[:-1]):
+        out[i * n : (i + 1) * n, :] = ref[:n, :]
+
+
+def order_kernel(dims, *refs):
+    meta = place_of()
     F = dims
     for k in range(F):
         e = lax.rem(meta[2] + k, F)
@@ -135,19 +149,36 @@
             refs[3 + k][i] = refs[i][e]
 
 
-def attend_kernel(dims, meta, start, cos, sin, *refs):
+def turn_tables(cos_low, sin_low, cos_high, sin_high, cosine, sine, L):
+    low = cos_low.shape[0]
+    for step in range(L // low):
+        a, b = cos_high[step : step + 1, :], sin_high[step : step + 1, :]
+        at = slice(step * low, (step + 1) * low)
+        cosine[at, :] = a * cos_low[...] - b * sin_low[...]
+        sine[at, :] = b * cos_low[...] + a * sin_low[...]
+
+
+def signed(sine):
+    lane = lax.broadcasted_iota(jnp.int32, sine.shape, 1)
+    return jnp.where(lane < HD // 2, -sine, sine)
+
+
+def attend_kernel(dims, blocks, start, cos_low, sin_low, cos_high, sin_high, *refs):
     Z, F, R, D, L, hpd, block = dims
     hw = hpd * HD
     xs, refs = refs[: 2 * Z], refs[2 * Z :]
     ws, refs = refs[:F], refs[F:]
-    normed, weight, small_out, q_out, k_out, v_out, o_out, lse_out = refs[:8]
-    pieces, small_s, att_s = refs[8 : 8 + Z], refs[8 + Z], refs[9 + Z]
-    z, core, f = meta[0], meta[1], meta[2]
+    normed, weight, small_out, cos, sin, q_out, k_out, v_out, kt_out, ot_out, lse_out = refs[:11]
+    refs = refs[11:]
+    pieces, (small_s, vt_s, att_s) = refs[:Z], refs[Z:]
+    z, core, f, _ = place_of()
     d_local = D // F
+    top = ws[0].shape[0] - d_local - 16
+    turn_tables(cos_low, sin_low, cos_high, sin_high, cos, sin, L)
     for k in range(F):
         row = pl.multiple_of(lax.rem(f - k + F, F) * d_local, d_local)
-        weight[pl.ds(row, d_local), :] = ws[k][:d_local, :]
-        small_s[k] = ws[k][d_local:, :d_local].astype(F32)
+        weight[pl.ds(row, d_local), :] = ws[k][top : top + d_local, : 3 * hw]
+        small_s[k] = ws[k][top + d_local :, :d_local].astype(F32)
     small = jnp.concatenate([small_s[lax.rem(f - i + F, F)] for i in range(F)], axis=1)
     small_out[...] = small
     gain_row = small[0:1, :]
@@ -161,60 +192,63 @@
     def project(step, carry):
         rows = pl.ds(pl.multiple_of(step * block, block), block)
         mixed = mm(normed[rows, :], weight[...])
-        cosine, sine = cos[rows, :], sin[rows, :]
+        cosine, sine = cos[rows, :], signed(sin[rows, :])
         for h in range(hpd):
             q = mixed[:, h * HD : (h + 1) * HD]
             k = mixed[:, hw + h * HD : hw + (h + 1) * HD]
             v = mixed[:, 2 * hw + h * HD : 2 * hw + (h + 1) * HD]
             q = (q * cosine + halves_swapped(q) * sine).astype(BF)
             q_out[h, rows, :] = (q.astype(F32) * HD ** (-0.5)).astype(BF)
-            k_out[h, rows, :] = (k * cosine + halves_swapped(k) * sine).astype(BF)
+            k = k * cosine + halves_swapped(k) * sine
+            k_out[h, rows, :] = k.astype(BF)
+            kt_out[h, :, rows] = k.T.astype(BF)
             v_out[h, rows, :] = v.astype(BF)
+            vt_s[h, :, rows] = v.T.astype(BF)
         return carry
 
     lax.fori_loop(0, L // block, project, 0)
 
     def query_step(qb, carry):
         rows = pl.ds(pl.multiple_of(qb * block, block), block)
-        first = start[rows, :]
-        q_pos = qb * block + lax.broadcasted_iota(jnp.int32, (block, block), 0)
-        column = lax.broadcasted_iota(jnp.int32, (block, block), 1)
+        first = start[:, rows]
+        q_pos = qb * block + lax.broadcasted_iota(jnp.int32, (block, block), 1)
+        down = lax.broadcasted_iota(jnp.int32, (block, block), 0)
         queries = [q_out[h, rows, :] for h in range(hpd)]
 
         def key_step(kb, state):
             keys = pl.ds(pl.multiple_of(kb * block, block), block)
-            k_pos = kb * block + column
+            k_pos = kb * block + down
             allowed = (k_pos <= q_pos) & (k_pos >= first)
             new = []
             for h in range(hpd):
                 high, total, acc = state[h]
-                scores = mm_nt(queries[h], k_out[h, keys, :])
+                scores = mm_nt(k_out[h, keys, :], queries[h])
                 scores = jnp.where(allowed, scores, -1e30)
-                top = jnp.maximum(high, jnp.max(scores, axis=-1, keepdims=True))
+                top = jnp.maximum(high, jnp.max(scores, axis=0, keepdims=True))
                 scale = jnp.exp(high - top)
                 weights = jnp.where(allowed, jnp.exp(scores - top), 0.0)
-                total = total * scale + jnp.sum(weights, axis=-1, keepdims=True)
-                acc = acc * scale + mm(weights.astype(BF), v_out[h, keys, :])
+                total = total * scale + jnp.sum(weights, axis=0, keepdims=True)
+                acc = acc * scale + mm(vt_s[h, :, keys], weights.astype(BF))
                 new.append((top, total, acc))
             return tuple(new)
 
         begin = tuple(
             (
-                jnp.full((block, 1), -1e30, F32),
-                jnp.zeros((block, 1), F32),
-                jnp.zeros((block, HD), F32),
+                jnp.full((1, block), -1e30, F32),
+                jnp.zeros((1, block), F32),
+                jnp.zeros((HD, block), F32),
             )
             for _ in range(hpd)
         )
-        state = lax.fori_loop(meta[4 + qb], qb + 1, key_step, begin)
+        state = lax.fori_loop(blocks[qb], qb + 1, key_step, begin)
         outs = []
         for h in range(hpd):
             high, total, acc = state[h]
             out = acc / total
-            o_out[h, rows, :] = out
-            lse_out[h, rows, :] = high + jnp.log(total)
-            outs.append(out.astype(BF))
-        whole = jnp.concatenate(outs, axis=-1)
+            ot_out[h, :, rows] = out
+            lse_out[h, :, rows] = high + jnp.log(total)
+            outs.append(out)
+        whole = jnp.concatenate(outs, axis=0).T.astype(BF)
         for part in range(block // R):
             att_s[qb * (block // R) + part] = whole[part * R : (part + 1) * R, :]
         return carry
@@ -254,7 +288,8 @@
     return lane, router, hots, gates
 
 
-def dispatch_kernel(dims, meta, x, small, prev, routes, slots, *refs):
+def dispatch_kernel(dims, x, small, prev, routes, slots, *refs):
+    meta = place_of()
     Z, F, S, R, D, G, hw, expert_of = dims
     atts, refs = refs[: 2 * Z], refs[2 * Z :]
     ws, refs = refs[:F], refs[F:]
@@ -308,15 +343,18 @@
         toks[k][...] = table[expert_of(lax.rem(f + k, F))]
 
 
-def ffn_kernel(dims, own, meta, rows_a, rows_b, g_a, g_b, *refs):
+def ffn_kernel(dims, own, rows_a, rows_b, g_a, g_b, *refs):
+    meta = place_of()
     F, D = dims
     n = rows_a.shape[0]
-    ws, refs = refs[:F], refs[F:]
+    ws, refs = (refs[:F], refs[F:]) if own else ((), refs)
+    if not own:
+        w_s, refs = refs[0], refs[1:]
     (inner_out, gate_out, up_out, xt_out, drt_out), refs = refs[:5], refs[5:]
     if own:
-        mine_out, theirs_out, x_s, dr_s, w_s, acc = refs
+        mine_out, theirs_out, w_s, x_s, dr_s, acc = refs
     else:
-        x_s, dr_s, w_s = refs
+        x_s, dr_s = refs
     step = pl.program_id(0)
     d_local = D // F
 
@@ -331,10 +369,10 @@
             dr_s[at, :] = dr
             drt_out[:, at] = dr.T
 
-    for k in range(F):
+    for k, piece in enumerate(ws):
         at = pl.ds(pl.multiple_of(lax.rem(meta[2] - k + F, F) * d_local, d_local), d_local)
         for i in range(3):
-            w_s[i, at, :] = ws[k][i]
+            w_s[i, at, :] = piece[i]
     piece = n // 2
     for r in range(4):
         rows = slice(r * piece, (r + 1) * piece)
@@ -366,7 +404,8 @@
             theirs_out[...] = acc[:, n:, :].astype(BF)
 
 
-def weight_kernel(dims, meta, *refs):
+def weight_kernel(dims, *refs):
+    meta = place_of()
     F, D, Z = dims
     planes, refs = [refs[5 * p : 5 * p + 5] for p in range(Z)], refs[5 * Z :]
     outs, (acc,) = refs[:F], refs[F:]
@@ -382,7 +421,8 @@
             outs[k][i] = acc[i, at, :]
 
 
-def combine_kernel(dims, meta, hidden, grad, small, prev, routes, slots, *refs):
+def combine_kernel(dims, hidden, grad, small, prev, routes, slots, *refs):
+    meta = place_of()
     Z, F, S, R, D, G, hw, per, _ = dims
     rets, refs = refs[:F], refs[F:]
     atts, refs = refs[: 2 * Z], refs[2 * Z :]
@@ -507,70 +547,69 @@
         payloads[k][d_local:, d_local:] = jnp.zeros((16, D - d_local), BF)
 
 
-def back_kernel(dims, meta, start, cos, sin, small, *refs):
+def back_kernel(dims, blocks, start, cos, sin, small, *refs):
     Z, F, R, D, L, hpd, block = dims
     hw = hpd * HD
-    xs, refs = refs[: 2 * Z], refs[2 * Z :]
     dos, refs = refs[: 2 * Z], refs[2 * Z :]
-    (normed, weight, q_in, k_in, v_in, o_in, lse_in), refs = refs[:7], refs[7:]
+    (normed, weight, q_in, k_in, v_in, kt_in, ot_in, lse_in), refs = refs[:8], refs[8:]
     payloads, refs = refs[:F], refs[F:]
-    (mine_out, theirs_out), refs = refs[:2], refs[2:]
-    do_s, dq_s, dk_s, dv_s, mixed_s, gw_s, rows_s = refs
-    z, core, f = meta[0], meta[1], meta[2]
+    mixed_s, do_s, delta_s, dq_s, dk_s, dv_s, gw_s, rows_s = refs
+    z, core, f, _ = place_of()
     d_local = D // F
     for k in range(Z):
         for side in range(2):
             at = lax.rem(z + k, Z) * 2 + (core if side == 0 else 1 - core)
-            row = pl.multiple_of(at * R, R)
+            rows = pl.ds(pl.multiple_of(at * R, R), R)
             tile = dos[k][0] if side == 0 else dos[Z + k][...]
+            turned = tile.astype(F32).T
             for h in range(hpd):
-                do_s[h, pl.ds(row, R), :] = tile[:, h * HD : (h + 1) * HD]
+                heads = slice(h * HD, (h + 1) * HD)
+                do_s[h, rows, :] = tile[:, heads]
+                delta_s[h, :, rows] = jnp.sum(
+                    turned[heads, :] * ot_in[h, :, rows], axis=0, keepdims=True
+                )
     dk_s[...] = jnp.zeros_like(dk_s)
     dv_s[...] = jnp.zeros_like(dv_s)
 
     def query_step(qb, carry):
         rows = pl.ds(pl.multiple_of(qb * block, block), block)
-        first = start[rows, :]
-        q_pos = qb * block + lax.broadcasted_iota(jnp.int32, (block, block), 0)
-        column = lax.broadcasted_iota(jnp.int32, (block, block), 1)
+        first = start[:, rows]
+        q_pos = qb * block + lax.broadcasted_iota(jnp.int32, (block, block), 1)
+        down = lax.broadcasted_iota(jnp.int32, (block, block), 0)
         queries = [q_in[h, rows, :] for h in range(hpd)]
         upstream = [do_s[h, rows, :] for h in range(hpd)]
-        lses = [lse_in[h, rows, :] for h in range(hpd)]
-        deltas = [
-            jnp.sum(upstream[h].astype(F32) * o_in[h, rows, :], axis=-1, keepdims=True)
-            for h in range(hpd)
-        ]
+        lses = [lse_in[h, :, rows] for h in range(hpd)]
+        deltas = [delta_s[h, :, rows] for h in range(hpd)]
 
         def key_step(kb, state):
             keys = pl.ds(pl.multiple_of(kb * block, block), block)
-            k_pos = kb * block + column
+            k_pos = kb * block + down
             allowed = (k_pos <= q_pos) & (k_pos >= first)
             new = []
             for h in range(hpd):
-                key, value = k_in[h, keys, :], v_in[h, keys, :]
-                scores = mm_nt(queries[h], key)
+                scores = mm_nt(k_in[h, keys, :], queries[h])
                 weights = jnp.where(allowed, jnp.exp(scores - lses[h]), 0.0)
-                dp = mm_nt(upstream[h], value)
+                dp = mm_nt(v_in[h, keys, :], upstream[h])
                 ds = (weights * (dp - deltas[h])).astype(BF)
-                dv_s[h, keys, :] += mm_tn(weights.astype(BF), upstream[h])
-                dk_s[h, keys, :] += mm_tn(ds, queries[h])
-                new.append(state[h] + mm(ds, key))
+                dv_s[h, keys, :] += mm(weights.astype(BF), upstream[h])
+                dk_s[h, keys, :] += mm(ds, queries[h])
+                new.append(state[h] + mm(kt_in[h, :, keys], ds))
             return tuple(new)
 
-        begin = tuple(jnp.zeros((block, HD), F32) for _ in range(hpd))
-        state = lax.fori_loop(meta[4 + qb], qb + 1, key_step, begin)
+        begin = tuple(jnp.zeros((HD, block), F32) for _ in range(hpd))
+        state = lax.fori_loop(blocks[qb], qb + 1, key_step, begin)
         for h in range(hpd):
-            dq_s[h, rows, :] = state[h]
+            dq_s[h, rows, :] = state[h].T * HD ** (-0.5)
         return carry
 
     lax.fori_loop(0, L // block, query_step, 0)
 
     def unrotate(step, carry):
         rows = pl.ds(pl.multiple_of(step * block, block), block)
-        cosine, sine = cos[rows, :], sin[rows, :]
+        cosine, sine = cos[rows, :], signed(sin[rows, :])
         parts = [[], [], []]
         for h in range(hpd):
-            dq = dq_s[h, rows, :] * HD ** (-0.5)
+            dq = dq_s[h, rows, :]
             dk = dk_s[h, rows, :]
             parts[0].append((dq * cosine - halves_swapped(dq) * sine).astype(BF))
             parts[1].append((dk * cosine - halves_swapped(dk) * sine).astype(BF))
@@ -579,21 +618,11 @@
         return carry
 
     lax.fori_loop(0, L // block, unrotate, 0)
-    gw_s[...] = mm_tn(normed[...], mixed_s[...]).astype(BF)
-    total = jnp.zeros((1, D), F32)
-    for k in range(Z):
-        for side in range(2):
-            chip = lax.rem(z - k + Z, Z)
-            at = chip * 2 + (core if side == 0 else 1 - core)
-            tile = xs[side * Z + k][...].astype(F32)
-            row = pl.multiple_of(at * R, R)
-            dn = mm_nt(mixed_s[pl.ds(row, R), :], weight[...])
-            total = total + jnp.sum(dn * (tile * norm_of(tile)), axis=0, keepdims=True)
-            if side == 0:
-                mine_out[chip] = dn.astype(BF)
-            else:
-                theirs_out[chip] = dn.astype(BF)
-    total = jnp.broadcast_to(total, (16, D)).astype(BF)
+    gw = mm_tn(normed[...], mixed_s[...])
+    gw_s[...] = gw.astype(BF)
+    high, low = split(gw * weight[...].astype(F32))
+    ones = jnp.ones((16, 3 * hw), BF)
+    total = ((mm_nt(ones, high) + mm_nt(ones, low)) / small[0:1, :]).astype(BF)
     for i in range(F):
         rows_s[i] = total[:, i * d_local : (i + 1) * d_local]
     for k in range(F):
@@ -605,13 +634,32 @@
             payloads[k][d_local:, d_local:] = jnp.zeros((16, 3 * hw - d_local), BF)
 
 
-def pair_kernel(Z, meta, mine, theirs, *outs):
+def normed_grad_kernel(dims, mixed, weight, mine, theirs):
+    Z, R = dims
+    core = place_of()[1]
+    for chip in range(Z):
+        for parity in range(2):
+            row = (2 * chip + parity) * R
+            part = mm_nt(mixed[row : row + R, :], weight[...]).astype(BF)
+
+            @pl.when(core == parity)
+            def _():
+                mine[chip] = part
+
+            @pl.when(core != parity)
+            def _():
+                theirs[chip] = part
+
+
+def pair_kernel(Z, mine, theirs, *outs):
+    meta = place_of()
     for k in range(Z):
         chip = lax.rem(meta[0] + k, Z)
         outs[k][...] = (mine[chip].astype(F32) + theirs[chip].astype(F32)).astype(BF)
 
 
-def last_kernel(dims, meta, x, dh, small, *refs):
+def last_kernel(dims, x, dh, small, *refs):
+    meta = place_of()
     Z, S, R, _, G = dims
     dns, out, acc = refs[:Z], refs[Z], refs[Z + 1]
     acc[...] = jnp.zeros_like(acc)
@@ -629,7 +677,8 @@
         )
 
 
-def place_kernel(dims, ks, part, meta, *refs):
+def place_kernel(dims, ks, left, *refs):
+    meta = place_of()
     F, per, CW, width = dims
     n = len(ks)
     ours, theirs, refs = refs[:n], refs[n : 2 * n], refs[2 * n :]
@@ -640,7 +689,7 @@
             dev = lax.rem(meta[2] - k + F, F)
             core = meta[1] if side == 0 else 1 - meta[1]
             e = lax.div(dev, per)
-            lane = (lax.rem(dev, per) * 2 + core) * CW + part * width
+            lane = (lax.rem(dev, per) * 2 + core) * CW + left
             lanes = pl.ds(pl.multiple_of(lane, 128), width)
             for i in range(3):
                 at = (side * n + j) * 3 + i
@@ -652,7 +701,8 @@
         copy.wait()
 
 
-def qkv_grad_kernel(dims, meta, *refs):
+def qkv_grad_kernel(dims, *refs):
+    meta = place_of()
     G, D, d_local, hw = dims
     pieces, (out, gain_out, table) = refs[:-3], refs[-3:]
     group = lax.rem(meta[3], G)
@@ -705,7 +755,7 @@
     CW = FF // (2 * per)
     d_local = D // F
     T = S * R
-    block = min(256, L)
+    block = min(512, L)
     shaped = jax.ShapeDtypeStruct
     f = lax.axis_index("fsdp")
     c = lax.axis_index("ctx")
@@ -735,7 +785,7 @@
     def chunk_of(dev):
         return (dev % per) * 2 + core
 
-    def call(kernel, name, out_shape, args, scratch=(), smem=1, **kw):
+    def call(kernel, name, out_shape, args, scratch=(), smem=0, **kw):
         return pl.pallas_call(
             kernel,
             out_shape=out_shape,
@@ -754,33 +804,31 @@
     my_docs = pick(doc_ids, c // G)
     start = jnp.sum((my_docs[None, :] < my_docs[:, None]).astype(jnp.int32), axis=1)
     first_block = start.reshape(L // block, block)[:, 0] // block
-    meta = jnp.concatenate([jnp.stack([z, core, f, c]).astype(jnp.int32), first_block])
     route_rows = routes.transpose(0, 2, 1).reshape(S * TOP, R)
     prev = prev_logits.transpose(0, 2, 1)
 
-    (first,) = call(
-        functools.partial(pack_kernel, (F, D, G, hpd)),
+    slot_rows, *packs = call(
+        functools.partial(pack_kernel, (F, S, R, D, G, hpd, expert_of)),
         "pack",
-        (shaped((d_local + 16, 3 * hw), BF),),
+        (shaped((S * TOP, R), jnp.int32),) + (shaped((S * MOST + d_local + 16, D), BF),) * F,
         (
-            meta,
+            d_out,
+            route_rows,
             w_qkv,
-            attn_gain[None],
-            ffn_gain[None],
+            jnp.stack([attn_gain, ffn_gain]),
             w_router.T,
             const_mix.T,
             const_vec.T,
         ),
-    )
-    w_pieces = [first] + [fs(first, k) for k in range(1, F)]
-    slot_rows, *g_outs = call(
-        functools.partial(grad_rows_kernel, (F, S, R, D, expert_of)),
-        "grad_rows",
-        (shaped((S * TOP, R), jnp.int32),) + (shaped((S * MOST, D), BF),) * F,
-        (meta, d_out, route_rows),
         [pltpu.VMEM((NF, S * MOST, D), BF)],
     )
-    g_mine = jnp.concatenate([g_outs[0]] + [fs(g_outs[k], k) for k in range(1, F)], axis=0)
+    w_pieces = [packs[0]] + [fs(packs[k], k) for k in range(1, F)]
+    (g_mine,) = call(
+        functools.partial(stack_kernel, S * MOST),
+        "stack",
+        (shaped((F * S * MOST, D), BF),),
+        tuple(w_pieces),
+    )
     o_pieces = [w_out] + [fs(w_out, k) for k in range(1, F)]
 
     def expert_slices():
@@ -794,7 +842,7 @@
                 functools.partial(order_kernel, F),
                 "order",
                 (shaped((3, d_local, CW), BF),) * F,
-                (meta, *cut),
+                tuple(cut),
             )
         out = []
         for k in range(F):
@@ -817,27 +865,35 @@
     e_pieces = [slices[0]] + [fs(slices[k], k) for k in range(1, F)]
 
     frequency = jnp.exp(jnp.arange(HD // 2, dtype=F32) * (-2.0 * math.log(10000.0) / HD))
-    angles = jnp.arange(L).astype(F32)[:, None] * frequency[None, :]
-    cosine, sine = jnp.cos(angles), jnp.sin(angles)
-    cosine = jnp.concatenate([cosine, cosine], axis=1)
-    sine = jnp.concatenate([-sine, sine], axis=1)
+    frequency = jnp.concatenate([frequency, frequency])
+    low = jnp.arange(32).astype(F32)[:, None] * frequency[None, :]
+    high = (32 * jnp.arange(L // 32)).astype(F32)[:, None] * frequency[None, :]
+    tables = (jnp.cos(low), jnp.sin(low), jnp.cos(high), jnp.sin(high))
     dims = (Z, F, R, D, L, hpd, block)
-    normed, qkv_w, small, q, k_, v, o, lse, *att_pieces = call(
+    normed, qkv_w, small, cosine, sine, q, k_, v, kt, ot, lse, *att_pieces = call(
         functools.partial(attend_kernel, dims),
         "attend",
         (
             shaped((L, D), BF),
             shaped((D, 3 * hw), BF),
             shaped((16, D), F32),
+            shaped((L, HD), F32),
+            shaped((L, HD), F32),
             shaped((hpd, L, HD), BF),
             shaped((hpd, L, HD), BF),
             shaped((hpd, L, HD), BF),
-            shaped((hpd, L, HD), F32),
-            shaped((hpd, L, 1), F32),
+            shaped((hpd, HD, L), BF),
+            shaped((hpd, HD, L), F32),
+            shaped((hpd, 1, L), F32),
         )
         + (shaped((2, R, hw), BF),) * Z,
-        (meta, start[:, None], cosine, sine, *x_mine, *x_theirs, *w_pieces),
-        [pltpu.VMEM((F, 16, d_local), F32), pltpu.VMEM((C, R, hw), BF)],
+        (first_block, start[None], *tables, *x_mine, *x_theirs, *w_pieces),
+        [
+            pltpu.VMEM((F, 16, d_local), F32),
+            pltpu.VMEM((hpd, HD, L), BF),
+            pltpu.VMEM((C, R, hw), BF),
+        ],
+        smem=1,
     )
 
     g_planes = [(g_mine, cx(g_mine))] + [zs(g_mine, k) for k in range(1, Z)]
@@ -849,12 +905,17 @@
         "dispatch",
         (shaped((T, D), F32), shaped((G * hw, D), BF))
         + (shaped((S * MOST, D + 128), BF),) * F,
-        (meta, block_input, small, prev, route_rows, slot_rows, *atts, *o_pieces),
+        (block_input, small, prev, route_rows, slot_rows, *atts, *o_pieces),
         [pltpu.VMEM((NF, S * MOST, D + 128), BF)],
     )
     hidden, out_w, toks = outs[0], outs[1], outs[2:]
     own = [toks[0]] + [fs(toks[k], k) for k in range(1, F)]
-    own = jnp.concatenate(own, axis=0)
+    (own,) = call(
+        functools.partial(stack_kernel, S * MOST),
+        "stack",
+        (shaped((F * S * MOST, D + 128), BF),),
+        tuple(own),
+    )
     n = own.shape[0]
 
     steps = 4 if CW % 512 == 0 else 2
@@ -868,10 +929,10 @@
         shapes = (shaped((2 * n, CW), BF),) * 3 + (shaped((D, 2 * n), BF),) * 2
         specs = (act_spec,) * 3 + (both_spec,) * 2
         scratch = [pltpu.VMEM((2 * n, D), BF), pltpu.VMEM((2 * n, D), BF)]
-        scratch.append(pltpu.VMEM((3, D, cut), BF))
+        w_spec = pl.BlockSpec((3, D, cut), lambda i: (0, 0, i))
         if own_plane:
-            shapes += (shaped((2, n, D), F32), shaped((2, n, D), BF))
-            specs += (pl.BlockSpec((2, n, D), lambda i: (0, 0, 0)),) * 2
+            shapes += (shaped((2, n, D), F32), shaped((2, n, D), BF), shaped((3, D, CW), BF))
+            specs += (pl.BlockSpec((2, n, D), lambda i: (0, 0, 0)),) * 2 + (w_spec,)
             scratch.append(pltpu.VMEM((2, 2 * n, D), F32))
         row_spec = pl.BlockSpec((n, D + 128), lambda i: (0, 0))
         g_spec = pl.BlockSpec((n, D), lambda i: (0, 0))
@@ -879,13 +940,14 @@
             functools.partial(ffn_kernel, (F, D), own_plane),
             out_shape=shapes,
             grid=(steps,),
-            in_specs=[SMEM, row_spec, row_spec, g_spec, g_spec] + [e_spec] * F,
+            in_specs=[row_spec, row_spec, g_spec, g_spec]
+            + ([e_spec] * F if own_plane else [w_spec]),
             out_specs=specs,
             scratch_shapes=scratch,
             compiler_params=params("experts" if at else "experts0", L > 2048),
-        )(meta, rows, theirs, *g_rows, *e_pieces)
-
-    *plane, back_mine, back_theirs = ffn(0, own, cx(own), g_planes[0])
+        )(rows, theirs, *g_rows, *(e_pieces if own_plane else [weights]))
+
+    *plane, back_mine, back_theirs, weights = ffn(0, own, cx(own), g_planes[0])
     planes = [plane]
     back = (back_mine + cx(back_theirs).astype(F32)).astype(BF).reshape(2, F, S * MOST, D)
     rets = [back[:, 0]] + [fs(back[:, k], -k) for k in range(1, F)]
@@ -904,7 +966,7 @@
         (shaped((S, R, D), BF), shaped((T, D), F32), shaped((S, NE, R), F32))
         + (shaped((2, R, hw), BF),) * Z
         + (shaped((d_local + 16, D), BF),) * F,
-        (meta, hidden, d_out, small, prev, route_rows, slot_rows, *rets, *atts, out_w),
+        (hidden, d_out, small, prev, route_rows, slot_rows, *rets, *atts, out_w),
         [
             pltpu.VMEM((F, 2, S * MOST, D), BF),
             pltpu.VMEM((G * hw, D), F32),
@@ -921,80 +983,84 @@
 
     for k in range(2, Z):
         far(k, hidden_grad)
-    parts = 2
-    width = CW // parts
-    wide = min(256, width)
     flat = [t for plane in planes for t in plane]
+    wide = 256
+    widths = [CW - wide, wide]
     e_grads = []
-    for part in range(parts):
-        first_block_at = part * (width // wide)
+    for part, width in enumerate(widths):
+        left = sum(widths[:part])
         if Z > 4:
-            lanes = slice(part * width, (part + 1) * width)
+            lanes = slice(left, left + width)
             trio = [
-                sum(mm(plane[left], plane[right][:, lanes]) for plane in planes).astype(BF)
-                for left, right in ((3, 1), (3, 2), (4, 0))
+                sum(mm(plane[a], plane[b][:, lanes]) for plane in planes).astype(BF)
+                for a, b in ((3, 1), (3, 2), (4, 0))
             ]
             trio = jnp.stack(trio).reshape(3, F, d_local, width)
             e_grads.append([pick(trio, (f + k) % F, 1) for k in range(F)])
             continue
-        acts = pl.BlockSpec((2 * n, wide), lambda i, b=first_block_at: (0, b + i))
+        acts = pl.BlockSpec((2 * n, wide), lambda i, b=left // wide: (0, b + i))
         e_grads.append(
             pl.pallas_call(
                 functools.partial(weight_kernel, (F, D, Z)),
                 out_shape=(shaped((3, d_local, width), BF),) * F,
                 grid=(width // wide,),
-                in_specs=[SMEM] + [acts, acts, acts, both_spec, both_spec] * Z,
+                in_specs=[acts, acts, acts, both_spec, both_spec] * Z,
                 out_specs=(pl.BlockSpec((3, d_local, wide), lambda i: (0, 0, i)),) * F,
                 scratch_shapes=[pltpu.VMEM((3, D, wide), BF)],
                 compiler_params=params("expert_grads", L > 2048),
-            )(meta, *flat)
+            )(*flat)
         )
     dos[0], *_ = lax.optimization_barrier((dos[0], e_grads[-1][0]))
     outs = call(
         functools.partial(back_kernel, dims),
         "attend_back",
-        (shaped((d_local + 16, 3 * hw), BF),) * F + (shaped((Z, R, D), BF),) * 2,
+        (shaped((d_local + 16, 3 * hw), BF),) * F + (shaped((L, 3 * hw), BF),),
         (
-            meta,
-            start[:, None],
+            first_block,
+            start[None],
             cosine,
             sine,
             small,
-            *x_mine,
-            *x_theirs,
             *dos,
             normed,
             qkv_w,
             q,
             k_,
             v,
-            o,
+            kt,
+            ot,
             lse,
         ),
         [
             pltpu.VMEM((hpd, L, HD), BF),
+            pltpu.VMEM((hpd, 1, L), F32),
             pltpu.VMEM((hpd, L, HD), F32),
             pltpu.VMEM((hpd, L, HD), F32),
             pltpu.VMEM((hpd, L, HD), F32),
-            pltpu.VMEM((L, 3 * hw), BF),
             pltpu.VMEM((D, 3 * hw), BF),
             pltpu.VMEM((F, 16, d_local), BF),
         ],
-    )
-    q_payloads, dn_mine, dn_theirs = outs[:F], outs[F], outs[F + 1]
+        smem=1,
+    )
+    q_payloads, mixed_grad = outs[:F], outs[F]
+    dn_mine, dn_theirs = call(
+        functools.partial(normed_grad_kernel, (Z, R)),
+        "normed_grad",
+        (shaped((Z, R, D), BF),) * 2,
+        (mixed_grad, qkv_w),
+    )
     dns = call(
         functools.partial(pair_kernel, Z),
         "pair",
         (shaped((R, D), BF),) * Z,
-        (meta, dn_mine, cx(dn_theirs)),
-    )
-    paired = dns[0]
+        (dn_mine, cx(dn_theirs)),
+    )
     dns = [dns[0]] + [zs(dns[k], k) for k in range(1, Z)]
     (grad_x,) = call(
         functools.partial(last_kernel, (Z, S, R, D, G)),
         "input_grad",
         (shaped((S, R, D), F32),),
-        (meta, block_input, hidden_grad, small, *dns),
+        (block_input, hidden_grad, small, *dns),
         [pltpu.VMEM((S, R, D), F32)],
     )
 
@@ -1029,30 +1095,31 @@
         functools.partial(qkv_grad_kernel, (G, D, d_local, hw)),
         "qkv_grad",
         (shaped((d_local, 3 * D), F32), shaped((1, d_local), F32)),
-        (meta, *gathered),
+        tuple(gathered),
         [pltpu.VMEM((G, d_local + 16, 3 * hw), BF)],
     )
     grad_gain_one = grad_gain_one[0]
 
     moved = moved_rows(o_payloads)
-    moved, _ = lax.optimization_barrier((moved, paired))
     payload = over_ctx(summed_rows(moved)).astype(F32)
     grad_w_out = payload[:d_local]
     smalls = payload[d_local:, :d_local]
 
     ANY = pl.BlockSpec(memory_space=pl.ANY)
     placed = ()
-    for part in range(parts):
+    for part, width in enumerate(widths):
         ours = [e_grads[part][0]] + [fs(e_grads[part][k], k) for k in range(1, F)]
         theirs = [cx(t) for t in ours]
-        groups = [list(range(F))] if part < parts - 1 else [list(range(F - 1)), [F - 1]]
+        groups = [list(range(F))]
         for ks in groups:
-            args = (meta, *[ours[k] for k in ks], *[theirs[k] for k in ks], *placed)
-            at = 1 + 2 * len(ks)
+            args = (*[ours[k] for k in ks], *[theirs[k] for k in ks], *placed)
+            at = 2 * len(ks)
             placed = pl.pallas_call(
-                functools.partial(place_kernel, (F, per, CW, width), ks, part),
+                functools.partial(
+                    place_kernel, (F, per, CW, width), ks, sum(widths[:part])
+                ),
                 out_shape=(shaped((d_local, NF, FF), F32),) * 3,
-                in_specs=[SMEM] + [VMEM] * (2 * len(ks)) + [ANY] * len(placed),
+                in_specs=[VMEM] * (2 * len(ks)) + [ANY] * len(placed),
                 out_specs=(ANY,) * 3,
                 input_output_aliases={at + i: i for i in range(len(placed))},
                 scratch_shapes=[

time: 486 us -> 447 us (0.920)
  waiting for transfers between devices: 253 us -> 170 us
  starting transfers between devices: 64 us -> 140 us
  local copies, waits for them, and re-layouts: 30.2 us -> 16.3 us
  Pallas kernels: 121 us -> 109 us
    ppermute x18, waiting for transfers between devices: 137 us -> 71.1 us  [zs(): lax.ppermute(t, 'ctx', [(2 * i + j, 2 * ((i + k) % Z) + j) for i in range...]
    ppermute x30 -> x27, starting transfers between devices: 39.5 us -> 102 us  [fs(): return lax.ppermute(t, 'fsdp', [(i, (i + k) % F) for i in range(F)])]
    ppermute x30 -> x27, waiting for transfers between devices: 92.5 us -> 68.4 us  [fs(): return lax.ppermute(t, 'fsdp', [(i, (i + k) % F) for i in range(F)])]
    ppermute x18, starting transfers between devices: 11.7 us -> 27.5 us  [zs(): lax.ppermute(t, 'ctx', [(2 * i + j, 2 * ((i + k) % Z) + j) for i in range...]
    ppermute x1, waiting for transfers between devices: 11.6 us -> 25.4 us  [body(): lax.ppermute(payload, 'ctx', [(i, (i + j * G) % C) for i in range(C)])]
    unnamed x143 -> x71, local copies, waits for them, and re-layouts: 18 us -> 5.69 us
    pallas_call x10 -> x12, Pallas kernels: 53.3 us -> 46.7 us  [call(): pl.pallas_call(kernel, out_shape=out_shape, in_specs=[SMEM] * smem + [VME...]
    ppermute x3, starting transfers between devices: 6.67 us -> 0.36 us  [over_ctx(): moved = lax.ppermute(t, 'ctx', [(i, i ^ step) for i in range(C)])]
  transfers between devices with their start and end apart: 84 -> 81, of which waited for: 31 -> 29; matrix products, arithmetic and copies ran while one was open for 3% -> 3% of each run, Pallas kernels for 23% -> 21%
where the time goes in v1:
time: 447 us; the launch traced here: 439 us
  waiting for transfers between devices  170 us (38%)
  starting transfers between devices  140 us (31%)
  Pallas kernels  109 us (24%)
  local copies, waits for them, and re-layouts  16.3 us (4%)
    ppermute x27, starting transfers between devices, fs(): return lax.ppermute(t, 'fsdp', [(i, (i + k) % F) for i in range(F)])  102 us
    ppermute x18, waiting for transfers between devices, zs(): lax.ppermute(t, 'ctx', [(2 * i + j, 2 * ((i + k) % Z) + j) for i in range...  71.1 us
    ppermute x27, waiting for transfers between devices, fs(): return lax.ppermute(t, 'fsdp', [(i, (i + k) % F) for i in range(F)])  68.4 us
    pallas_call x12, Pallas kernels, call(): pl.pallas_call(kernel, out_shape=out_shape, in_specs=[SMEM] * smem + [VME...  46.7 us
    pallas_call x4, Pallas kernels, ffn(): pl.pallas_call(functools.partial(ffn_kernel, (F, D), own_plane), out_shap...  35.8 us
    ppermute x18, starting transfers between devices, zs(): lax.ppermute(t, 'ctx', [(2 * i + j, 2 * ((i + k) % Z) + j) for i in range...  27.5 us
    ppermute x1, waiting for transfers between devices, body(): lax.ppermute(payload, 'ctx', [(i, (i + j * G) % C) for i in range(C)])  25.4 us
    pallas_call x2, Pallas kernels, body(): pl.pallas_call(functools.partial(weight_kernel, (F, D, Z)), out_shape=(sh...  18.2 us
  transfers between devices with their start and end apart: 81, of which 29 were waited for; matrix products, arithmetic and copies ran while one was open for 3% of the time, Pallas kernels for 21%

profile of v1, /device:TPU:0, one launch (start us, length us, event | category | flops | bytes accessed | tf_op | source)
XLA Modules:
  0.0 438.6 jit_solution(15746229068859547766)
XLA Ops:
  0.9 2.3 dynamic-slice_bitcast_fusion
  3.2 5.1 %collective-permute-start.2 = (bf16[128,768]{1,0:T(8,128)(2,1)}, bf16[128,768]{1,0:T(8,128)(2,1)}, u32[]{:S(2)}, u32[]{:S(2)}) collective-permute-start(bf16[128,768]{1,0:T(8,128)(2,1)} %get-tuple-element.219), channel_id=1, source_target_pairs={{0,6},{1,7},{2,0},{3,1},{4,2},{5,3},{6,4},{7,5},{8,14},{9,15},{10,... | collective-permute-start | bytes 589832 | tf_op jit(solution)/shard_map/ppermute | solution.py:769
  9.4 1.7 shard_map.246
  12.6 1.5 collective-permute-start.7
  14.0 1.5 collective-permute-start.8
  19.4 2.9 constant_dynamic-slice_fusion
  22.3 1.5 collective-permute-start.9
  29.9 1.5 collective-permute-start.17
  32.8 4.5 %collective-permute-done.8.refs_10_.refs_2_ = bf16[304,768]{1,0:T(8,128)(2,1)} collective-permute-done((bf16[304,768]{1,0:T(8,128)(2,1)}, bf16[304,768]{1,0:T(8,128)(2,1)}, u32[]{:S(2)}, u32[]{:S(2)}) %collective-permute-start.8) | collective-permute-done | bytes 466976 | tf_op jit(solution)/shard_map/ppermute | solution.py:766
  37.3 12.6 %shard_map.247 = (bf16[1024,768]{1,0:T(8,128)(2,1)S(1)}, bf16[768,576]{1,0:T(8,128)(2,1)S(1)}, f32[16,768]{1,0:T(8,128)S(1)}, f32[1024,64]{1,0:T(8,128)S(1)}, f3...) custom-call(s32[2]{0:T(128)S(1)} %and_select_fusion.blocks, ...), custom_call_target="tpu_custom_call" | custom-call | tf_op jit(solution)/shard_map/pallas_call | solution.py:789
  50.0 2.5 collective-permute-start.10
  52.6 4.5 %collective-permute-done.10.refs_1_.refs_5_ = bf16[2,128,192]{2,1,0:T(8,128)(2,1)S(1)} collective-permute-done((bf16[2,128,192]{2,1,0:T(8,128)(2,1)S(1)}, bf16[2,128,192]{2,1,0:T(8,128)(2,1)S(1)}, u32[]{:S(2)}, u32[]{:S(2)}) %collective-permute-start.10) | collective-permute-done | bytes 98336 | tf_op jit(solution)/shard_map/ppermute | solution.py:769
  57.5 7.7 %collective-permute-done.11.refs_2_.refs_6_ = bf16[2,128,192]{2,1,0:T(8,128)(2,1)S(1)} collective-permute-done((bf16[2,128,192]{2,1,0:T(8,128)(2,1)S(1)}, bf16[2,128,192]{2,1,0:T(8,128)(2,1)S(1)}, u32[]{:S(2)}, u32[]{:S(2)}) %collective-permute-start.11) | collective-permute-done | bytes 98336 | tf_op jit(solution)/shard_map/ppermute | solution.py:769
  66.2 1.6 collective-permute-start.26
  67.8 2.6 collective-permute-start.27
  73.2 1.9 shard_map.248
  75.1 3.0 collective-permute-start.20
  78.0 24.4 %collective-permute-done.20.refs_1_ = bf16[96,896]{1,0:T(8,128)(2,1)S(1)} collective-permute-done((bf16[96,896]{1,0:T(8,128)(2,1)S(1)}, bf16[96,896]{1,0:T(8,128)(2,1)S(1)}, u32[]{:S(2)}, u32[]{:S(2)}) %collective-permute-start.20) | collective-permute-done | bytes 172064 | tf_op jit(solution)/shard_map/ppermute | solution.py:766
  103.9 2.1 collective-permute-done.21.refs_2_
  105.9 1.9 collective-permute-done.22.refs_3_
  109.8 1.6 collective-permute-done.24.g_b
  111.4 14.1 %shard_map.252 = (bf16[768,1024]{1,0:T(8,128)(2,1)S(1)}, bf16[768,1024]{1,0:T(8,128)(2,1)S(1)}, bf16[768,1024]{1,0:T(8,128)(2,1)S(1)}, bf16[768,768]{1,0:T(8,128...) custom-call(bf16[384,896]{1,0:T(8,128)(2,1)S(1)} %shard_map.249.rows, ...), custom_call_target="tpu_custom_call" | custom-call | tf_op jit(solution)/shard_map/pallas_call | solution.py:939
  126.0 2.5 collective-permute-start.32
  128.5 16.8 %collective-permute-done.32.rows_a = bf16[384,896]{1,0:T(8,128)(2,1)S(1)} collective-permute-done((bf16[384,896]{1,0:T(8,128)(2,1)S(1)}, bf16[384,896]{1,0:T(8,128)(2,1)S(1)}, u32[]{:S(2)}, u32[]{:S(2)}) %collective-permute-start.32) | collective-permute-done | bytes 688160 | tf_op jit(solution)/shard_map/ppermute | solution.py:769
  146.3 18.4 %collective-permute-start.31 = (bf16[2,96,768]{2,1,0:T(8,128)(2,1)S(1)}, bf16[2,96,768]{2,1,0:T(8,128)(2,1)S(1)}, u32[]{:S(2)}, u32[]{:S(2)}) collective-permute-start(bf16[2,96,768]{2,1,0:T(8,128)(2,1)S(1)} %get-tuple-element.215), channel_id=1, source_target_pairs={{0,8},{8,16},{16,24},{24,0},{1,9},{9,17},{17,25},{25,1},{2,10},{10... | collective-permute-start | bytes 884744 | tf_op jit(solution)/shard_map/ppermute | solution.py:766
  165.3 3.8 collective-permute-start.41
  169.1 2.0 collective-permute-done.31.refs_3_
  171.5 5.8 %collective-permute-done.30.refs_2_ = bf16[2,96,768]{2,1,0:T(8,128)(2,1)S(1)} collective-permute-done((bf16[2,96,768]{2,1,0:T(8,128)(2,1)S(1)}, bf16[2,96,768]{2,1,0:T(8,128)(2,1)S(1)}, u32[]{:S(2)}, u32[]{:S(2)}) %collective-permute-start.30) | collective-permute-done | bytes 294944 | tf_op jit(solution)/shard_map/ppermute | solution.py:766
  177.3 12.6 %collective-permute-start.29 = (bf16[2,96,768]{2,1,0:T(8,128)(2,1)S(1)}, bf16[2,96,768]{2,1,0:T(8,128)(2,1)S(1)}, u32[]{:S(2)}, u32[]{:S(2)}) collective-permute-start(bf16[2,96,768]{2,1,0:T(8,128)(2,1)S(1)} %get-tuple-element.217), channel_id=1, source_target_pairs={{0,24},{8,0},{16,8},{24,16},{1,25},{9,1},{17,9},{25,17},{2,26},{10... | collective-permute-start | bytes 884744 | tf_op jit(solution)/shard_map/ppermute | solution.py:766
  189.8 5.0 %collective-permute-done.29.refs_1_ = bf16[2,96,768]{2,1,0:T(8,128)(2,1)S(1)} collective-permute-done((bf16[2,96,768]{2,1,0:T(8,128)(2,1)S(1)}, bf16[2,96,768]{2,1,0:T(8,128)(2,1)S(1)}, u32[]{:S(2)}, u32[]{:S(2)}) %collective-permute-start.29) | collective-permute-done | bytes 294944 | tf_op jit(solution)/shard_map/ppermute | solution.py:766
  194.8 6.4 %shard_map.253 = (bf16[2,128,768]{2,1,0:T(8,128)(2,1)}, f32[256,768]{1,0:T(8,128)S(1)}, f32[2,8,128]{2,1,0:T(8,128)}, bf16[2,128,192]{2,1,0:T(8,128)(2,1)S(1)}, ...) custom-call(f32[256,768]{1,0:T(8,128)S(1)} %get-tuple-element.124.hi, ...), custom_call_target="tpu_custom_call" | custom-call | tf_op jit(solution)/shard_map/pallas_call | solution.py:789
  201.2 2.9 collective-permute-start.61
  204.4 5.9 %collective-permute-done.33.g_a = bf16[384,768]{1,0:T(8,128)(2,1)S(1)} collective-permute-done((bf16[384,768]{1,0:T(8,128)(2,1)S(1)}, bf16[384,768]{1,0:T(8,128)(2,1)S(1)}, u32[]{:S(2)}, u32[]{:S(2)}) %collective-permute-start.33) | collective-permute-done | bytes 589856 | tf_op jit(solution)/shard_map/ppermute | solution.py:769
  210.3 17.7 %collective-permute-start.63 = (bf16[208,768]{1,0:T(8,128)(2,1)S(1)}, bf16[208,768]{1,0:T(8,128)(2,1)S(1)}, u32[]{:S(2)}, u32[]{:S(2)}) collective-permute-start(bf16[208,768]{1,0:T(8,128)(2,1)S(1)} %get-tuple-element.201), channel_id=1, source_target_pairs={{0,24},{8,0},{16,8},{24,16},{1,25},{9,1},{17,9},{25,17},{2,26},{10... | collective-permute-start | bytes 958472 | tf_op jit(solution)/shard_map/ppermute | solution.py:766
  228.0 5.5 %collective-permute-done.37.g_a = bf16[384,768]{1,0:T(8,128)(2,1)S(1)} collective-permute-done((bf16[384,768]{1,0:T(8,128)(2,1)S(1)}, bf16[384,768]{1,0:T(8,128)(2,1)S(1)}, u32[]{:S(2)}, u32[]{:S(2)}) %collective-permute-start.37) | collective-permute-done | bytes 589856 | tf_op jit(solution)/shard_map/ppermute | solution.py:769
  234.4 6.2 %collective-permute-done.44.refs_1_ = bf16[2,128,192]{2,1,0:T(8,128)(2,1)S(1)} collective-permute-done((bf16[2,128,192]{2,1,0:T(8,128)(2,1)S(1)}, bf16[2,128,192]{2,1,0:T(8,128)(2,1)S(1)}, u32[]{:S(2)}, u32[]{:S(2)}) %collective-permute-start.44) | collective-permute-done | bytes 98336 | tf_op jit(solution)/shard_map/ppermute | solution.py:769
  241.3 2.0 collective-permute-done.45.refs_2_
  244.7 6.9 %collective-permute-done.46.refs_3_ = bf16[2,128,192]{2,1,0:T(8,128)(2,1)S(1)} collective-permute-done((bf16[2,128,192]{2,1,0:T(8,128)(2,1)S(1)}, bf16[2,128,192]{2,1,0:T(8,128)(2,1)S(1)}, u32[]{:S(2)}, u32[]{:S(2)}) %collective-permute-start.46) | collective-permute-done | bytes 98336 | tf_op jit(solution)/shard_map/ppermute | solution.py:769
  252.7 7.2 %shard_map.254 = (bf16[768,1024]{1,0:T(8,128)(2,1)S(1)}, bf16[768,1024]{1,0:T(8,128)(2,1)S(1)}, bf16[768,1024]{1,0:T(8,128)(2,1)S(1)}, bf16[768,768]{1,0:T(8,128)(2,1)S(1)}, bf16[768,768]{1,0:T(8,128)(2,1)S(1)}) custom-call(bf16[384,896]{1,0:T(8,128)(2,1)S(1)} %collective-permute-done.32.rows_a, bf16[384,896]{1,0:T(8,128)(2,1)S(1)} %collective-permute-done.34.rows_b, ...), custom_call_target="tpu_custom_call" | custom-call | tf_op jit(solution)/shard_map/pallas_call | solution.py:939
  259.9 7.2 %shard_map.256 = (bf16[768,1024]{1,0:T(8,128)(2,1)S(1)}, bf16[768,1024]{1,0:T(8,128)(2,1)S(1)}, bf16[768,1024]{1,0:T(8,128)(2,1)S(1)}, bf16[768,768]{1,0:T(8,128)(2,1)S(1)}, bf16[768,768]{1,0:T(8,128)(2,1)S(1)}) custom-call(bf16[384,896]{1,0:T(8,128)(2,1)S(1)} %collective-permute-done.40.rows_a, bf16[384,896]{1,0:T(8,128)(2,1)S(1)} %collective-permute-done.42.rows_b, ...), custom_call_target="tpu_custom_call" | custom-call | tf_op jit(solution)/shard_map/pallas_call | solution.py:939
  267.2 7.2 %shard_map.255 = (bf16[768,1024]{1,0:T(8,128)(2,1)S(1)}, bf16[768,1024]{1,0:T(8,128)(2,1)S(1)}, bf16[768,1024]{1,0:T(8,128)(2,1)S(1)}, bf16[768,768]{1,0:T(8,128)(2,1)S(1)}, bf16[768,768]{1,0:T(8,128)(2,1)S(1)}) custom-call(bf16[384,896]{1,0:T(8,128)(2,1)S(1)} %collective-permute-done.36.rows_a, bf16[384,896]{1,0:T(8,128)(2,1)S(1)} %collective-permute-done.38.rows_b, ...), custom_call_target="tpu_custom_call" | custom-call | tf_op jit(solution)/shard_map/pallas_call | solution.py:939
  274.4 4.0 shard_map.257
  278.5 15.1 %shard_map.258 = (bf16[208,576]{1,0:T(8,128)(2,1)S(1)}, bf16[208,576]{1,0:T(8,128)(2,1)S(1)}, bf16[208,576]{1,0:T(8,128)(2,1)S(1)}, bf16[208,576]{1,0:T(8,128)(2,1)S(1)}, bf16[1024,576]{1,0:T(8,128)(2,1)S(1)}) custom-call(s32[2]{0:T(128)S(1)} %and_select_fusion.blocks, s32[1,1024]{1,0:T(1,128)S(1)} %bitcast.74, f32[1024,64]{1,0:T(8,128)S(1)} %copy-done.19, ...), custom_call_target="tpu_custom_call" | custom-call | tf_op jit(solution)/shard_map/pallas_call | solution.py:789
  293.7 14.8 %collective-permute-start.55 = (bf16[208,576]{1,0:T(8,128)(2,1)S(1)}, bf16[208,576]{1,0:T(8,128)(2,1)S(1)}, u32[]{:S(2)}, u32[]{:S(2)}) collective-permute-start(bf16[208,576]{1,0:T(8,128)(2,1)S(1)} %get-tuple-element.193), channel_id=1, source_target_pairs={{0,8},{8,16},{16,24},{24,0},{1,9},{9,17},{17,25},{25,1},{2,10},{10... | collective-permute-start | bytes 718856 | tf_op jit(solution)/shard_map/ppermute | solution.py:766
  308.5 14.2 %shard_map.263 = (bf16[3,192,768]{2,1,0:T(8,128)(2,1)S(1)}, bf16[3,192,768]{2,1,0:T(8,128)(2,1)S(1)}, bf16[3,192,768]{2,1,0:T(8,128)(2,1)S(1)}, bf16[3,192,768]{2,1,0:T(8,128)(2,1)S(1)}) custom-call(bf16[768,1024]{1,0:T(8,128)(2,1)S(1)} %get-tuple-element.144.refs_0_, bf16[768,1024]{1,0:T(8,128)(2,1)S(1)} %get-tuple-element.145.refs_1_, ...), custom_call_target="tpu_custom_call" | custom-call | tf_op jit(solution)/shard_map/pallas_call | solution.py:1003
  322.7 4.3 shard_map.259
  327.0 2.1 collective-permute-start.56
  329.1 2.8 collective-permute-start.57
  332.1 3.1 collective-permute-done.56
  335.2 3.5 collective-permute-done.57
  338.8 11.3 %collective-permute-start.74 = (bf16[3,192,768]{2,1,0:T(8,128)(2,1)S(1)}, bf16[3,192,768]{2,1,0:T(8,128)(2,1)S(1)}, u32[]{:S(2)}, u32[]{:S(2)}) collective-permute-start(bf16[3,192,768]{2,1,0:T(8,128)(2,1)S(1)} %get-tuple-element.206), channel_id=1, source_target_pairs={{0,8},{8,16},{16,24},{24,0},{1,9},{9,17},{17,25},{25,1},{2,10},{10... | collective-permute-start | bytes 2654216 | tf_op jit(solution)/shard_map/ppermute | solution.py:766
  350.9 2.6 collective-permute-start.58
  353.5 25.4 %collective-permute-done.58 = bf16[208,576]{1,0:T(8,128)(2,1)S(1)} collective-permute-done((bf16[208,576]{1,0:T(8,128)(2,1)S(1)}, bf16[208,576]{1,0:T(8,128)(2,1)S(1)}, u32[]{:S(2)}, u32[]{:S(2)}) %collective-permute-start.58) | collective-permute-done | bytes 239648 | tf_op jit(solution)/shard_map/ppermute | solution.py:1084
  379.0 1.7 collective-permute-start.76
  381.4 7.7 %collective-permute-done.75.refs_2_ = bf16[3,192,768]{2,1,0:T(8,128)(2,1)S(1)} collective-permute-done((bf16[3,192,768]{2,1,0:T(8,128)(2,1)S(1)}, bf16[3,192,768]{2,1,0:T(8,128)(2,1)S(1)}, u32[]{:S(2)}, u32[]{:S(2)}) %collective-permute-start.75) | collective-permute-done | bytes 884768 | tf_op jit(solution)/shard_map/ppermute | solution.py:766
  389.4 2.1 collective-permute-start.52
  391.5 8.4 %collective-permute-done.76.refs_3_ = bf16[3,192,768]{2,1,0:T(8,128)(2,1)S(1)} collective-permute-done((bf16[3,192,768]{2,1,0:T(8,128)(2,1)S(1)}, bf16[3,192,768]{2,1,0:T(8,128)(2,1)S(1)}, u32[]{:S(2)}, u32[]{:S(2)}) %collective-permute-start.76) | collective-permute-done | bytes 884768 | tf_op jit(solution)/shard_map/ppermute | solution.py:766
  399.9 2.7 collective-permute-start.53
  402.7 11.5 %collective-permute-done.53.refs_2_ = bf16[128,768]{1,0:T(8,128)(2,1)S(1)} collective-permute-done((bf16[128,768]{1,0:T(8,128)(2,1)S(1)}, bf16[128,768]{1,0:T(8,128)(2,1)S(1)}, u32[]{:S(2)}, u32[]{:S(2)}) %collective-permute-start.53) | collective-permute-done | bytes 196640 | tf_op jit(solution)/shard_map/ppermute | solution.py:769
  414.2 3.7 collective-permute-start.54
  418.5 4.1 collective-permute-done.54.refs_3_
  427.7 1.6 shard_map.262
  429.2 5.3 %shard_map.264 = (f32[192,4,2048]{2,1,0:T(4,128)}, f32[192,4,2048]{2,1,0:T(4,128)}, f32[192,4,2048]{2,1,0:T(4,128)}) custom-call(bf16[3,192,768]{2,1,0:T(8,128)(2,1)S(1)} %get-tuple-element.205.refs_0_, bf16[3,192,768]{2,1,0:T(8,128)(2,1)S(1)} %collective-permute-done.74.refs_1_, bf16[3,192,768]{2,1,0:T(8,128)(2,1)S(1)} %collective-permute-done.75.refs_2_, ...), custom_call_target="tpu_custom_call" | custom-call | tf_op jit(solution)/shard_map/pallas_call | solution.py:1117
  434.6 2.6 shard_map.265
  (226 shorter events, 36.9 us)
Async XLA Ops:
  3.2 19.1 %collective-permute-start.2 = (bf16[128,768]{1,0:T(8,128)(2,1)}, bf16[128,768]{1,0:T(8,128)(2,1)}, u32[]{:S(2)}, u32[]{:S(2)}) collective-permute-start(bf16[128,768]{1,0:T(8,128)(2,1)} %get-tuple-element.219), channel_id=1, source_target_pairs={{0,6},{1,7},{2,0},{3,1},{4,2},{5,3},{6,4},{7,5},{8,14},{9,15},{10,... | collective-permute-start | bytes 589832 | tf_op jit(solution)/shard_map/ppermute | solution.py:769
  8.2 17.4 %collective-permute-start.1 = (bf16[128,768]{1,0:T(8,128)(2,1)}, bf16[128,768]{1,0:T(8,128)(2,1)}, u32[]{:S(2)}, u32[]{:S(2)}) collective-permute-start(bf16[128,768]{1,0:T(8,128)(2,1)} %get-tuple-element.220), channel_id=1, source_target_pairs={{0,4},{1,5},{2,6},{3,7},{4,0},{5,1},{6,2},{7,3},{8,12},{9,13},{10,... | collective-permute-start | bytes 589832 | tf_op jit(solution)/shard_map/ppermute | solution.py:769
  8.2 18.0 %collective-permute-start = (bf16[128,768]{1,0:T(8,128)(2,1)}, bf16[128,768]{1,0:T(8,128)(2,1)}, u32[]{:S(2)}, u32[]{:S(2)}) collective-permute-start(bf16[128,768]{1,0:T(8,128)(2,1)} %get-tuple-element.221), channel_id=1, source_target_pairs={{0,2},{1,3},{2,4},{3,5},{4,6},{5,7},{6,0},{7,1},{8,10},{9,11},{10,... | collective-permute-start | bytes 589832 | tf_op jit(solution)/shard_map/ppermute | solution.py:769
  12.6 18.8 %collective-permute-start.7 = (bf16[304,768]{1,0:T(8,128)(2,1)}, bf16[304,768]{1,0:T(8,128)(2,1)}, u32[]{:S(2)}, u32[]{:S(2)}) collective-permute-start(bf16[304,768]{1,0:T(8,128)(2,1)} %get-tuple-element.115), channel_id=1, source_target_pairs={{0,8},{8,16},{16,24},{24,0},{1,9},{9,17},{17,25},{25,1},{2,10},{10... | collective-permute-start | bytes 1400840 | tf_op jit(solution)/shard_map/ppermute | solution.py:766
  14.0 23.3 %collective-permute-start.8 = (bf16[304,768]{1,0:T(8,128)(2,1)}, bf16[304,768]{1,0:T(8,128)(2,1)}, u32[]{:S(2)}, u32[]{:S(2)}) collective-permute-start(bf16[304,768]{1,0:T(8,128)(2,1)} %get-tuple-element.116), channel_id=1, source_target_pairs={{0,16},{8,24},{16,0},{24,8},{1,17},{9,25},{17,1},{25,9},{2,18},{10... | collective-permute-start | bytes 1400840 | tf_op jit(solution)/shard_map/ppermute | solution.py:766
  22.3 15.0 %collective-permute-start.9 = (bf16[304,768]{1,0:T(8,128)(2,1)S(1)}, bf16[304,768]{1,0:T(8,128)(2,1)S(1)}, u32[]{:S(2)}, u32[]{:S(2)}) collective-permute-start(bf16[304,768]{1,0:T(8,128)(2,1)S(1)} %copy-done.29), channel_id=1, source_target_pairs={{0,24},{8,0},{16,8},{24,16},{1,25},{9,1},{17,9},{25,17},{2,26},{10... | collective-permute-start | bytes 1400840 | tf_op jit(solution)/shard_map/ppermute | solution.py:766
  29.3 36.9 %collective-permute-start.18 = (bf16[192,768]{1,0:T(8,128)(2,1)S(1)}, bf16[192,768]{1,0:T(8,128)(2,1)S(1)}, u32[]{:S(2)}, u32[]{:S(2)}) collective-permute-start(bf16[192,768]{1,0:T(8,128)(2,1)S(1)} %copy-done.22), channel_id=1, source_target_pairs={{0,16},{8,24},{16,0},{24,8},{1,17},{9,25},{17,1},{25,9},{2,18},{10... | collective-permute-start | bytes 884744 | tf_op jit(solution)/shard_map/ppermute | solution.py:766
  29.9 38.0 %collective-permute-start.17 = (bf16[192,768]{1,0:T(8,128)(2,1)S(1)}, bf16[192,768]{1,0:T(8,128)(2,1)S(1)}, u32[]{:S(2)}, u32[]{:S(2)}) collective-permute-start(bf16[192,768]{1,0:T(8,128)(2,1)S(1)} %copy-done.22), channel_id=1, source_target_pairs={{0,8},{8,16},{16,24},{24,0},{1,9},{9,17},{17,25},{25,1},{2,10},{10... | collective-permute-start | bytes 884744 | tf_op jit(solution)/shard_map/ppermute | solution.py:766
  31.4 39.1 %collective-permute-start.19 = (bf16[192,768]{1,0:T(8,128)(2,1)S(1)}, bf16[192,768]{1,0:T(8,128)(2,1)S(1)}, u32[]{:S(2)}, u32[]{:S(2)}) collective-permute-start(bf16[192,768]{1,0:T(8,128)(2,1)S(1)} %copy-done.22), channel_id=1, source_target_pairs={{0,24},{8,0},{16,8},{24,16},{1,25},{9,1},{17,9},{25,17},{2,26},{10... | collective-permute-start | bytes 884744 | tf_op jit(solution)/shard_map/ppermute | solution.py:766
  37.3 74.1 %collective-permute-start.25 = (bf16[3,192,1024]{2,1,0:T(8,128)(2,1)S(1)}, bf16[3,192,1024]{2,1,0:T(8,128)(2,1)S(1)}, u32[]{:S(2)}, u32[]{:S(2)}) collective-permute-start(bf16[3,192,1024]{2,1,0:T(8,128)(2,1)S(1)} %get-tuple-element.133), channel_id=1, source_target_pairs={{0,8},{8,16},{16,24},{24,0},{1,9},{9,17},{17,25},{25,1},{2,10},{10... | collective-permute-start | bytes 3538952 | tf_op jit(solution)/shard_map/ppermute | solution.py:766
  57.1 8.2 %collective-permute-start.11 = (bf16[2,128,192]{2,1,0:T(8,128)(2,1)S(1)}, bf16[2,128,192]{2,1,0:T(8,128)(2,1)S(1)}, u32[]{:S(2)}, u32[]{:S(2)}) collective-permute-start(bf16[2,128,192]{2,1,0:T(8,128)(2,1)S(1)} %get-tuple-element.122), channel_id=1, source_target_pairs={{0,4},{1,5},{2,6},{3,7},{4,0},{5,1},{6,2},{7,3},{8,12},{9,13},{10,... | collective-permute-start | bytes 294920 | tf_op jit(solution)/shard_map/ppermute | solution.py:769
  66.2 45.2 %collective-permute-start.26 = (bf16[3,192,1024]{2,1,0:T(8,128)(2,1)S(1)}, bf16[3,192,1024]{2,1,0:T(8,128)(2,1)S(1)}, u32[]{:S(2)}, u32[]{:S(2)}) collective-permute-start(bf16[3,192,1024]{2,1,0:T(8,128)(2,1)S(1)} %get-tuple-element.134), channel_id=1, source_target_pairs={{0,16},{8,24},{16,0},{24,8},{1,17},{9,25},{17,1},{25,9},{2,18},{10... | collective-permute-start | bytes 3538952 | tf_op jit(solution)/shard_map/ppermute | solution.py:766
  67.8 43.6 %collective-permute-start.27 = (bf16[3,192,1024]{2,1,0:T(8,128)(2,1)S(1)}, bf16[3,192,1024]{2,1,0:T(8,128)(2,1)S(1)}, u32[]{:S(2)}, u32[]{:S(2)}) collective-permute-start(bf16[3,192,1024]{2,1,0:T(8,128)(2,1)S(1)} %get-tuple-element.135), channel_id=1, source_target_pairs={{0,24},{8,0},{16,8},{24,16},{1,25},{9,1},{17,9},{25,17},{2,26},{10... | collective-permute-start | bytes 3538952 | tf_op jit(solution)/shard_map/ppermute | solution.py:766
  75.1 27.4 %collective-permute-start.20 = (bf16[96,896]{1,0:T(8,128)(2,1)S(1)}, bf16[96,896]{1,0:T(8,128)(2,1)S(1)}, u32[]{:S(2)}, u32[]{:S(2)}) collective-permute-start(bf16[96,896]{1,0:T(8,128)(2,1)S(1)} %get-tuple-element.126), channel_id=1, source_target_pairs={{0,8},{8,16},{16,24},{24,0},{1,9},{9,17},{17,25},{25,1},{2,10},{10... | collective-permute-start | bytes 516104 | tf_op jit(solution)/shard_map/ppermute | solution.py:766
  78.0 27.9 %collective-permute-start.21 = (bf16[96,896]{1,0:T(8,128)(2,1)S(1)}, bf16[96,896]{1,0:T(8,128)(2,1)S(1)}, u32[]{:S(2)}, u32[]{:S(2)}) collective-permute-start(bf16[96,896]{1,0:T(8,128)(2,1)S(1)} %get-tuple-element.127), channel_id=1, source_target_pairs={{0,16},{8,24},{16,0},{24,8},{1,17},{9,25},{17,1},{25,9},{2,18},{10... | collective-permute-start | bytes 516104 | tf_op jit(solution)/shard_map/ppermute | solution.py:766
  125.6 20.4 %collective-permute-start.28 = (bf16[2,384,768]{2,1,0:T(8,128)(2,1)S(1)}, bf16[2,384,768]{2,1,0:T(8,128)(2,1)S(1)}, u32[]{:S(2)}, u32[]{:S(2)}) collective-permute-start(bf16[2,384,768]{2,1,0:T(8,128)(2,1)S(1)} %get-tuple-element.137), channel_id=1, source_target_pairs={{0,1},{1,0},{2,3},{3,2},{4,5},{5,4},{6,7},{7,6},{8,9},{9,8},{10,11... | collective-permute-start | bytes 3538952 | tf_op jit(solution)/shard_map/ppermute | solution.py:774
  126.0 19.3 %collective-permute-start.32 = (bf16[384,896]{1,0:T(8,128)(2,1)S(1)}, bf16[384,896]{1,0:T(8,128)(2,1)S(1)}, u32[]{:S(2)}, u32[]{:S(2)}) collective-permute-start(bf16[384,896]{1,0:T(8,128)(2,1)S(1)} %shard_map.249.rows_a), channel_id=1, source_target_pairs={{0,2},{1,3},{2,4},{3,5},{4,6},{5,7},{6,0},{7,1},{8,10},{9,11},{10,... | collective-permute-start | bytes 2064392 | tf_op jit(solution)/shard_map/ppermute | solution.py:769
  145.3 19.5 %collective-permute-start.36 = (bf16[384,896]{1,0:T(8,128)(2,1)S(1)}, bf16[384,896]{1,0:T(8,128)(2,1)S(1)}, u32[]{:S(2)}, u32[]{:S(2)}) collective-permute-start(bf16[384,896]{1,0:T(8,128)(2,1)S(1)} %collective-permute-done.32.rows_a), channel_id=1, source_target_pairs={{0,2},{1,3},{2,4},{3,5},{4,6},{5,7},{6,0},{7,1},{8,10},{9,11},{10,... | collective-permute-start | bytes 2064392 | tf_op jit(solution)/shard_map/ppermute | solution.py:769
  146.3 24.7 %collective-permute-start.31 = (bf16[2,96,768]{2,1,0:T(8,128)(2,1)S(1)}, bf16[2,96,768]{2,1,0:T(8,128)(2,1)S(1)}, u32[]{:S(2)}, u32[]{:S(2)}) collective-permute-start(bf16[2,96,768]{2,1,0:T(8,128)(2,1)S(1)} %get-tuple-element.215), channel_id=1, source_target_pairs={{0,8},{8,16},{16,24},{24,0},{1,9},{9,17},{17,25},{25,1},{2,10},{10... | collective-permute-start | bytes 884744 | tf_op jit(solution)/shard_map/ppermute | solution.py:766
  164.8 68.7 %collective-permute-start.40 = (bf16[384,896]{1,0:T(8,128)(2,1)S(1)}, bf16[384,896]{1,0:T(8,128)(2,1)S(1)}, u32[]{:S(2)}, u32[]{:S(2)}) collective-permute-start(bf16[384,896]{1,0:T(8,128)(2,1)S(1)} %collective-permute-done.36.rows_a), channel_id=1, source_target_pairs={{0,2},{1,3},{2,4},{3,5},{4,6},{5,7},{6,0},{7,1},{8,10},{9,11},{10,... | collective-permute-start | bytes 2064392 | tf_op jit(solution)/shard_map/ppermute | solution.py:769
  165.0 12.3 %collective-permute-start.30 = (bf16[2,96,768]{2,1,0:T(8,128)(2,1)S(1)}, bf16[2,96,768]{2,1,0:T(8,128)(2,1)S(1)}, u32[]{:S(2)}, u32[]{:S(2)}) collective-permute-start(bf16[2,96,768]{2,1,0:T(8,128)(2,1)S(1)} %get-tuple-element.216), channel_id=1, source_target_pairs={{0,16},{8,24},{16,0},{24,8},{1,17},{9,25},{17,1},{25,9},{2,18},{10... | collective-permute-start | bytes 884744 | tf_op jit(solution)/shard_map/ppermute | solution.py:766
  165.3 38.8 %collective-permute-start.41 = (bf16[384,768]{1,0:T(8,128)(2,1)S(1)}, bf16[384,768]{1,0:T(8,128)(2,1)S(1)}, u32[]{:S(2)}, u32[]{:S(2)}) collective-permute-start(bf16[384,768]{1,0:T(8,128)(2,1)S(1)} %shard_map.250.g_a), channel_id=1, source_target_pairs={{0,6},{1,7},{2,0},{3,1},{4,2},{5,3},{6,4},{7,5},{8,14},{9,15},{10,... | collective-permute-start | bytes 1769480 | tf_op jit(solution)/shard_map/ppermute | solution.py:769
  169.0 41.2 %collective-permute-start.33 = (bf16[384,768]{1,0:T(8,128)(2,1)S(1)}, bf16[384,768]{1,0:T(8,128)(2,1)S(1)}, u32[]{:S(2)}, u32[]{:S(2)}) collective-permute-start(bf16[384,768]{1,0:T(8,128)(2,1)S(1)} %shard_map.250.g_a), channel_id=1, source_target_pairs={{0,2},{1,3},{2,4},{3,5},{4,6},{5,7},{6,0},{7,1},{8,10},{9,11},{10,... | collective-permute-start | bytes 1769480 | tf_op jit(solution)/shard_map/ppermute | solution.py:769
  171.1 62.4 %collective-permute-start.37 = (bf16[384,768]{1,0:T(8,128)(2,1)S(1)}, bf16[384,768]{1,0:T(8,128)(2,1)S(1)}, u32[]{:S(2)}, u32[]{:S(2)}) collective-permute-start(bf16[384,768]{1,0:T(8,128)(2,1)S(1)} %shard_map.250.g_a), channel_id=1, source_target_pairs={{0,4},{1,5},{2,6},{3,7},{4,0},{5,1},{6,2},{7,3},{8,12},{9,13},{10,... | collective-permute-start | bytes 1769480 | tf_op jit(solution)/shard_map/ppermute | solution.py:769
  177.3 17.5 %collective-permute-start.29 = (bf16[2,96,768]{2,1,0:T(8,128)(2,1)S(1)}, bf16[2,96,768]{2,1,0:T(8,128)(2,1)S(1)}, u32[]{:S(2)}, u32[]{:S(2)}) collective-permute-start(bf16[2,96,768]{2,1,0:T(8,128)(2,1)S(1)} %get-tuple-element.217), channel_id=1, source_target_pairs={{0,24},{8,0},{16,8},{24,16},{1,25},{9,1},{17,9},{25,17},{2,26},{10... | collective-permute-start | bytes 884744 | tf_op jit(solution)/shard_map/ppermute | solution.py:766
  201.2 32.8 %collective-permute-start.61 = (bf16[208,768]{1,0:T(8,128)(2,1)S(1)}, bf16[208,768]{1,0:T(8,128)(2,1)S(1)}, u32[]{:S(2)}, u32[]{:S(2)}) collective-permute-start(bf16[208,768]{1,0:T(8,128)(2,1)S(1)} %get-tuple-element.199), channel_id=1, source_target_pairs={{0,8},{8,16},{16,24},{24,0},{1,9},{9,17},{17,25},{25,1},{2,10},{10... | collective-permute-start | bytes 958472 | tf_op jit(solution)/shard_map/ppermute | solution.py:766
  204.1 30.0 %collective-permute-start.62 = (bf16[208,768]{1,0:T(8,128)(2,1)S(1)}, bf16[208,768]{1,0:T(8,128)(2,1)S(1)}, u32[]{:S(2)}, u32[]{:S(2)}) collective-permute-start(bf16[208,768]{1,0:T(8,128)(2,1)S(1)} %get-tuple-element.200), channel_id=1, source_target_pairs={{0,16},{8,24},{16,0},{24,8},{1,17},{9,25},{17,1},{25,9},{2,18},{10... | collective-permute-start | bytes 958472 | tf_op jit(solution)/shard_map/ppermute | solution.py:766
  210.3 23.9 %collective-permute-start.63 = (bf16[208,768]{1,0:T(8,128)(2,1)S(1)}, bf16[208,768]{1,0:T(8,128)(2,1)S(1)}, u32[]{:S(2)}, u32[]{:S(2)}) collective-permute-start(bf16[208,768]{1,0:T(8,128)(2,1)S(1)} %get-tuple-element.201), channel_id=1, source_target_pairs={{0,24},{8,0},{16,8},{24,16},{1,25},{9,1},{17,9},{25,17},{2,26},{10... | collective-permute-start | bytes 958472 | tf_op jit(solution)/shard_map/ppermute | solution.py:766
  234.1 9.2 %collective-permute-start.45 = (bf16[2,128,192]{2,1,0:T(8,128)(2,1)S(1)}, bf16[2,128,192]{2,1,0:T(8,128)(2,1)S(1)}, u32[]{:S(2)}, u32[]{:S(2)}) collective-permute-start(bf16[2,128,192]{2,1,0:T(8,128)(2,1)S(1)} %get-tuple-element.174), channel_id=1, source_target_pairs={{0,4},{1,5},{2,6},{3,7},{4,0},{5,1},{6,2},{7,3},{8,12},{9,13},{10,... | collective-permute-start | bytes 294920 | tf_op jit(solution)/shard_map/ppermute | solution.py:769
  234.2 17.4 %collective-permute-start.39 = (bf16[384,768]{1,0:T(8,128)(2,1)S(1)}, bf16[384,768]{1,0:T(8,128)(2,1)S(1)}, u32[]{:S(2)}, u32[]{:S(2)}) collective-permute-start(bf16[384,768]{1,0:T(8,128)(2,1)S(1)} %collective-permute-done.37.g_a), channel_id=1, source_target_pairs={{0,1},{1,0},{2,3},{3,2},{4,5},{5,4},{6,7},{7,6},{8,9},{9,8},{10,11... | collective-permute-start | bytes 1769480 | tf_op jit(solution)/shard_map/ppermute | solution.py:774
  240.7 11.0 %collective-permute-start.43 = (bf16[384,768]{1,0:T(8,128)(2,1)S(1)}, bf16[384,768]{1,0:T(8,128)(2,1)S(1)}, u32[]{:S(2)}, u32[]{:S(2)}) collective-permute-start(bf16[384,768]{1,0:T(8,128)(2,1)S(1)} %collective-permute-done.41.g_a), channel_id=1, source_target_pairs={{0,1},{1,0},{2,3},{3,2},{4,5},{5,4},{6,7},{7,6},{8,9},{9,8},{10,11... | collective-permute-start | bytes 1769480 | tf_op jit(solution)/shard_map/ppermute | solution.py:774
  241.2 11.0 %collective-permute-start.38 = (bf16[384,896]{1,0:T(8,128)(2,1)S(1)}, bf16[384,896]{1,0:T(8,128)(2,1)S(1)}, u32[]{:S(2)}, u32[]{:S(2)}) collective-permute-start(bf16[384,896]{1,0:T(8,128)(2,1)S(1)} %collective-permute-done.36.rows_a), channel_id=1, source_target_pairs={{0,1},{1,0},{2,3},{3,2},{4,5},{5,4},{6,7},{7,6},{8,9},{9,8},{10,11... | collective-permute-start | bytes 2064392 | tf_op jit(solution)/shard_map/ppermute | solution.py:774
  243.3 9.0 %collective-permute-start.42 = (bf16[384,896]{1,0:T(8,128)(2,1)S(1)}, bf16[384,896]{1,0:T(8,128)(2,1)S(1)}, u32[]{:S(2)}, u32[]{:S(2)}) collective-permute-start(bf16[384,896]{1,0:T(8,128)(2,1)S(1)} %collective-permute-done.40.rows_a), channel_id=1, source_target_pairs={{0,1},{1,0},{2,3},{3,2},{4,5},{5,4},{6,7},{7,6},{8,9},{9,8},{10,11... | collective-permute-start | bytes 2064392 | tf_op jit(solution)/shard_map/ppermute | solution.py:774
  243.4 8.2 %collective-permute-start.46 = (bf16[2,128,192]{2,1,0:T(8,128)(2,1)S(1)}, bf16[2,128,192]{2,1,0:T(8,128)(2,1)S(1)}, u32[]{:S(2)}, u32[]{:S(2)}) collective-permute-start(bf16[2,128,192]{2,1,0:T(8,128)(2,1)S(1)} %get-tuple-element.175), channel_id=1, source_target_pairs={{0,2},{1,3},{2,4},{3,5},{4,6},{5,7},{6,0},{7,1},{8,10},{9,11},{10,... | collective-permute-start | bytes 294920 | tf_op jit(solution)/shard_map/ppermute | solution.py:769
  251.6 80.4 %collective-permute-start.65 = (bf16[208,768]{1,0:T(8,128)(2,1)S(1)}, bf16[208,768]{1,0:T(8,128)(2,1)S(1)}, u32[]{:S(2)}, u32[]{:S(2)}) collective-permute-start(bf16[208,768]{1,0:T(8,128)(2,1)S(1)} %add_convert_fusion.3), channel_id=1, source_target_pairs={{0,2},{1,3},{2,0},{3,1},{4,6},{5,7},{6,4},{7,5},{8,10},{9,11},{10,... | collective-permute-start | bytes 958472 | tf_op jit(solution)/shard_map/ppermute | solution.py:1076
  251.6 26.8 %collective-permute-start.47 = (bf16[128,192]{1,0:T(8,128)(2,1)S(1)}, bf16[128,192]{1,0:T(8,128)(2,1)S(1)}, u32[]{:S(2)}, u32[]{:S(2)}) collective-permute-start(bf16[128,192]{1,0:T(8,128)(2,1)S(1)} %slice_bitcast_fusion.10), channel_id=1, source_target_pairs={{0,1},{1,0},{2,3},{3,2},{4,5},{5,4},{6,7},{7,6},{8,9},{9,8},{10,11... | collective-permute-start | bytes 147464 | tf_op jit(solution)/shard_map/ppermute | solution.py:774
  251.7 26.7 %collective-permute-start.48 = (bf16[128,192]{1,0:T(8,128)(2,1)S(1)}, bf16[128,192]{1,0:T(8,128)(2,1)S(1)}, u32[]{:S(2)}, u32[]{:S(2)}) collective-permute-start(bf16[128,192]{1,0:T(8,128)(2,1)S(1)} %slice_bitcast_fusion.6), channel_id=1, source_target_pairs={{0,1},{1,0},{2,3},{3,2},{4,5},{5,4},{6,7},{7,6},{8,9},{9,8},{10,11... | collective-permute-start | bytes 147464 | tf_op jit(solution)/shard_map/ppermute | solution.py:774
  252.2 26.3 %collective-permute-start.49 = (bf16[128,192]{1,0:T(8,128)(2,1)S(1)}, bf16[128,192]{1,0:T(8,128)(2,1)S(1)}, u32[]{:S(2)}, u32[]{:S(2)}) collective-permute-start(bf16[128,192]{1,0:T(8,128)(2,1)S(1)} %slice_bitcast_fusion.5), channel_id=1, source_target_pairs={{0,1},{1,0},{2,3},{3,2},{4,5},{5,4},{6,7},{7,6},{8,9},{9,8},{10,11... | collective-permute-start | bytes 147464 | tf_op jit(solution)/shard_map/ppermute | solution.py:774
  252.3 26.2 %collective-permute-start.50 = (bf16[128,192]{1,0:T(8,128)(2,1)S(1)}, bf16[128,192]{1,0:T(8,128)(2,1)S(1)}, u32[]{:S(2)}, u32[]{:S(2)}) collective-permute-start(bf16[128,192]{1,0:T(8,128)(2,1)S(1)} %slice_bitcast_fusion.4), channel_id=1, source_target_pairs={{0,1},{1,0},{2,3},{3,2},{4,5},{5,4},{6,7},{7,6},{8,9},{9,8},{10,11... | collective-permute-start | bytes 147464 | tf_op jit(solution)/shard_map/ppermute | solution.py:774
  293.7 35.4 %collective-permute-start.55 = (bf16[208,576]{1,0:T(8,128)(2,1)S(1)}, bf16[208,576]{1,0:T(8,128)(2,1)S(1)}, u32[]{:S(2)}, u32[]{:S(2)}) collective-permute-start(bf16[208,576]{1,0:T(8,128)(2,1)S(1)} %get-tuple-element.193), channel_id=1, source_target_pairs={{0,8},{8,16},{16,24},{24,0},{1,9},{9,17},{17,25},{25,1},{2,10},{10... | collective-permute-start | bytes 718856 | tf_op jit(solution)/shard_map/ppermute | solution.py:766
  308.5 41.6 %collective-permute-start.67 = (bf16[3,192,256]{2,1,0:T(8,128)(2,1)S(1)}, bf16[3,192,256]{2,1,0:T(8,128)(2,1)S(1)}, u32[]{:S(2)}, u32[]{:S(2)}) collective-permute-start(bf16[3,192,256]{2,1,0:T(8,128)(2,1)S(1)} %get-tuple-element.202), channel_id=1, source_target_pairs={{0,8},{8,16},{16,24},{24,0},{1,9},{9,17},{17,25},{25,1},{2,10},{10... | collective-permute-start | bytes 884744 | tf_op jit(solution)/shard_map/ppermute | solution.py:766
  308.5 41.9 %collective-permute-start.68 = (bf16[3,192,256]{2,1,0:T(8,128)(2,1)S(1)}, bf16[3,192,256]{2,1,0:T(8,128)(2,1)S(1)}, u32[]{:S(2)}, u32[]{:S(2)}) collective-permute-start(bf16[3,192,256]{2,1,0:T(8,128)(2,1)S(1)} %get-tuple-element.203), channel_id=1, source_target_pairs={{0,16},{8,24},{16,0},{24,8},{1,17},{9,25},{17,1},{25,9},{2,18},{10... | collective-permute-start | bytes 884744 | tf_op jit(solution)/shard_map/ppermute | solution.py:766
  327.0 8.2 %collective-permute-start.56 = (bf16[208,576]{1,0:T(8,128)(2,1)S(1)}, bf16[208,576]{1,0:T(8,128)(2,1)S(1)}, u32[]{:S(2)}, u32[]{:S(2)}) collective-permute-start(bf16[208,576]{1,0:T(8,128)(2,1)S(1)} %get-tuple-element.194), channel_id=1, source_target_pairs={{0,16},{8,24},{16,0},{24,8},{1,17},{9,25},{17,1},{25,9},{2,18},{10... | collective-permute-start | bytes 718856 | tf_op jit(solution)/shard_map/ppermute | solution.py:766
  329.1 9.6 %collective-permute-start.57 = (bf16[208,576]{1,0:T(8,128)(2,1)S(1)}, bf16[208,576]{1,0:T(8,128)(2,1)S(1)}, u32[]{:S(2)}, u32[]{:S(2)}) collective-permute-start(bf16[208,576]{1,0:T(8,128)(2,1)S(1)} %get-tuple-element.195), channel_id=1, source_target_pairs={{0,24},{8,0},{16,8},{24,16},{1,25},{9,1},{17,9},{25,17},{2,26},{10... | collective-permute-start | bytes 718856 | tf_op jit(solution)/shard_map/ppermute | solution.py:766
  332.0 18.9 %collective-permute-start.69 = (bf16[3,192,256]{2,1,0:T(8,128)(2,1)S(1)}, bf16[3,192,256]{2,1,0:T(8,128)(2,1)S(1)}, u32[]{:S(2)}, u32[]{:S(2)}) collective-permute-start(bf16[3,192,256]{2,1,0:T(8,128)(2,1)S(1)} %get-tuple-element.204), channel_id=1, source_target_pairs={{0,24},{8,0},{16,8},{24,16},{1,25},{9,1},{17,9},{25,17},{2,26},{10... | collective-permute-start | bytes 884744 | tf_op jit(solution)/shard_map/ppermute | solution.py:766
  335.2 45.6 %collective-permute-start.51 = (bf16[4,128,768]{2,1,0:T(8,128)(2,1)S(1)}, bf16[4,128,768]{2,1,0:T(8,128)(2,1)S(1)}, u32[]{:S(2)}, u32[]{:S(2)}) collective-permute-start(bf16[4,128,768]{2,1,0:T(8,128)(2,1)S(1)} %get-tuple-element.186), channel_id=1, source_target_pairs={{0,1},{1,0},{2,3},{3,2},{4,5},{5,4},{6,7},{7,6},{8,9},{9,8},{10,11... | collective-permute-start | bytes 2359304 | tf_op jit(solution)/shard_map/ppermute | solution.py:774
  338.8 42.6 %collective-permute-start.74 = (bf16[3,192,768]{2,1,0:T(8,128)(2,1)S(1)}, bf16[3,192,768]{2,1,0:T(8,128)(2,1)S(1)}, u32[]{:S(2)}, u32[]{:S(2)}) collective-permute-start(bf16[3,192,768]{2,1,0:T(8,128)(2,1)S(1)} %get-tuple-element.206), channel_id=1, source_target_pairs={{0,8},{8,16},{16,24},{24,0},{1,9},{9,17},{17,25},{25,1},{2,10},{10... | collective-permute-start | bytes 2654216 | tf_op jit(solution)/shard_map/ppermute | solution.py:766
  350.1 39.0 %collective-permute-start.75 = (bf16[3,192,768]{2,1,0:T(8,128)(2,1)S(1)}, bf16[3,192,768]{2,1,0:T(8,128)(2,1)S(1)}, u32[]{:S(2)}, u32[]{:S(2)}) collective-permute-start(bf16[3,192,768]{2,1,0:T(8,128)(2,1)S(1)} %get-tuple-element.207), channel_id=1, source_target_pairs={{0,16},{8,24},{16,0},{24,8},{1,17},{9,25},{17,1},{25,9},{2,18},{10... | collective-permute-start | bytes 2654216 | tf_op jit(solution)/shard_map/ppermute | solution.py:766
  350.4 30.3 %collective-permute-start.66 = (bf16[208,768]{1,0:T(8,128)(2,1)S(1)}, bf16[208,768]{1,0:T(8,128)(2,1)S(1)}, u32[]{:S(2)}, u32[]{:S(2)}) collective-permute-start(bf16[208,768]{1,0:T(8,128)(2,1)S(1)} %add_convert_fusion.2), channel_id=1, source_target_pairs={{0,4},{1,5},{2,6},{3,7},{4,0},{5,1},{6,2},{7,3},{8,12},{9,13},{10,... | collective-permute-start | bytes 958472 | tf_op jit(solution)/shard_map/ppermute | solution.py:1076
  350.9 28.1 %collective-permute-start.58 = (bf16[208,576]{1,0:T(8,128)(2,1)S(1)}, bf16[208,576]{1,0:T(8,128)(2,1)S(1)}, u32[]{:S(2)}, u32[]{:S(2)}) collective-permute-start(bf16[208,576]{1,0:T(8,128)(2,1)S(1)} %add_convert_fusion.6), channel_id=1, source_target_pairs={{0,4},{1,5},{2,6},{3,7},{4,0},{5,1},{6,2},{7,3},{8,12},{9,13},{10,... | collective-permute-start | bytes 718856 | tf_op jit(solution)/shard_map/ppermute | solution.py:1084
  379.0 20.9 %collective-permute-start.76 = (bf16[3,192,768]{2,1,0:T(8,128)(2,1)S(1)}, bf16[3,192,768]{2,1,0:T(8,128)(2,1)S(1)}, u32[]{:S(2)}, u32[]{:S(2)}) collective-permute-start(bf16[3,192,768]{2,1,0:T(8,128)(2,1)S(1)} %get-tuple-element.208), channel_id=1, source_target_pairs={{0,24},{8,0},{16,8},{24,16},{1,25},{9,1},{17,9},{25,17},{2,26},{10... | collective-permute-start | bytes 2654216 | tf_op jit(solution)/shard_map/ppermute | solution.py:766
  380.7 19.2 %collective-permute-start.77 = (bf16[3,192,768]{2,1,0:T(8,128)(2,1)S(1)}, bf16[3,192,768]{2,1,0:T(8,128)(2,1)S(1)}, u32[]{:S(2)}, u32[]{:S(2)}) collective-permute-start(bf16[3,192,768]{2,1,0:T(8,128)(2,1)S(1)} %get-tuple-element.205.refs_0_), channel_id=1, source_target_pairs={{0,1},{1,0},{2,3},{3,2},{4,5},{5,4},{6,7},{7,6},{8,9},{9,8},{10,11... | collective-permute-start | bytes 2654216 | tf_op jit(solution)/shard_map/ppermute | solution.py:774
  380.8 8.6 %collective-permute-start.59 = (bf16[1,208,576]{2,1,0:T(8,128)(2,1)S(1)}, bf16[1,208,576]{2,1,0:T(8,128)(2,1)S(1)}, u32[]{:S(2)}, u32[]{:S(2)}) collective-permute-start(bf16[1,208,576]{2,1,0:T(8,128)(2,1)S(1)} %fusion.1.refs_0_), channel_id=1, source_target_pairs={{0,1},{1,0},{2,3},{3,2},{4,5},{5,4},{6,7},{7,6},{8,9},{9,8},{10,11... | collective-permute-start | bytes 718856 | tf_op jit(solution)/shard_map/ppermute | solution.py:1090
  381.4 41.8 %collective-permute-start.78 = (bf16[3,192,768]{2,1,0:T(8,128)(2,1)S(1)}, bf16[3,192,768]{2,1,0:T(8,128)(2,1)S(1)}, u32[]{:S(2)}, u32[]{:S(2)}) collective-permute-start(bf16[3,192,768]{2,1,0:T(8,128)(2,1)S(1)} %collective-permute-done.74.refs_1_), channel_id=1, source_target_pairs={{0,1},{1,0},{2,3},{3,2},{4,5},{5,4},{6,7},{7,6},{8,9},{9,8},{10,11... | collective-permute-start | bytes 2654216 | tf_op jit(solution)/shard_map/ppermute | solution.py:774
  389.1 34.1 %collective-permute-start.79 = (bf16[3,192,768]{2,1,0:T(8,128)(2,1)S(1)}, bf16[3,192,768]{2,1,0:T(8,128)(2,1)S(1)}, u32[]{:S(2)}, u32[]{:S(2)}) collective-permute-start(bf16[3,192,768]{2,1,0:T(8,128)(2,1)S(1)} %collective-permute-done.75.refs_2_), channel_id=1, source_target_pairs={{0,1},{1,0},{2,3},{3,2},{4,5},{5,4},{6,7},{7,6},{8,9},{9,8},{10,11... | collective-permute-start | bytes 2654216 | tf_op jit(solution)/shard_map/ppermute | solution.py:774
  389.4 13.2 %collective-permute-start.52 = (bf16[128,768]{1,0:T(8,128)(2,1)S(1)}, bf16[128,768]{1,0:T(8,128)(2,1)S(1)}, u32[]{:S(2)}, u32[]{:S(2)}) collective-permute-start(bf16[128,768]{1,0:T(8,128)(2,1)S(1)} %get-tuple-element.188), channel_id=1, source_target_pairs={{0,2},{1,3},{2,4},{3,5},{4,6},{5,7},{6,0},{7,1},{8,10},{9,11},{10,... | collective-permute-start | bytes 589832 | tf_op jit(solution)/shard_map/ppermute | solution.py:769
  399.9 22.7 %collective-permute-start.60 = (bf16[2,208,576]{2,1,0:T(8,128)(2,1)S(1)}, bf16[2,208,576]{2,1,0:T(8,128)(2,1)S(1)}, u32[]{:S(2)}, u32[]{:S(2)}) collective-permute-start(bf16[2,208,576]{2,1,0:T(8,128)(2,1)S(1)} %pad_maximum_fusion), channel_id=1, source_target_pairs={{0,2},{1,3},{2,0},{3,1},{4,6},{5,7},{6,4},{7,5},{8,10},{9,11},{10,... | collective-permute-start | bytes 1437704 | tf_op jit(solution)/shard_map/ppermute | solution.py:1090
  399.9 14.3 %collective-permute-start.53 = (bf16[128,768]{1,0:T(8,128)(2,1)S(1)}, bf16[128,768]{1,0:T(8,128)(2,1)S(1)}, u32[]{:S(2)}, u32[]{:S(2)}) collective-permute-start(bf16[128,768]{1,0:T(8,128)(2,1)S(1)} %get-tuple-element.189), channel_id=1, source_target_pairs={{0,4},{1,5},{2,6},{3,7},{4,0},{5,1},{6,2},{7,3},{8,12},{9,13},{10,... | collective-permute-start | bytes 589832 | tf_op jit(solution)/shard_map/ppermute | solution.py:769
  402.6 26.6 %collective-permute-start.80 = (bf16[3,192,768]{2,1,0:T(8,128)(2,1)S(1)}, bf16[3,192,768]{2,1,0:T(8,128)(2,1)S(1)}, u32[]{:S(2)}, u32[]{:S(2)}) collective-permute-start(bf16[3,192,768]{2,1,0:T(8,128)(2,1)S(1)} %collective-permute-done.76.refs_3_), channel_id=1, source_target_pairs={{0,1},{1,0},{2,3},{3,2},{4,5},{5,4},{6,7},{7,6},{8,9},{9,8},{10,11... | collective-permute-start | bytes 2654216 | tf_op jit(solution)/shard_map/ppermute | solution.py:774
  414.2 8.4 %collective-permute-start.54 = (bf16[128,768]{1,0:T(8,128)(2,1)S(1)}, bf16[128,768]{1,0:T(8,128)(2,1)S(1)}, u32[]{:S(2)}, u32[]{:S(2)}) collective-permute-start(bf16[128,768]{1,0:T(8,128)(2,1)S(1)} %get-tuple-element.190), channel_id=1, source_target_pairs={{0,6},{1,7},{2,0},{3,1},{4,2},{5,3},{6,4},{7,5},{8,14},{9,15},{10,... | collective-permute-start | bytes 589832 | tf_op jit(solution)/shard_map/ppermute | solution.py:769
  422.6 11.9 %collective-permute-start.70 = (bf16[3,192,256]{2,1,0:T(8,128)(2,1)S(1)}, bf16[3,192,256]{2,1,0:T(8,128)(2,1)S(1)}, u32[]{:S(2)}, u32[]{:S(2)}) collective-permute-start(bf16[3,192,256]{2,1,0:T(8,128)(2,1)S(1)} %get-tuple-element.171.refs_0_), channel_id=1, source_target_pairs={{0,1},{1,0},{2,3},{3,2},{4,5},{5,4},{6,7},{7,6},{8,9},{9,8},{10,11... | collective-permute-start | bytes 884744 | tf_op jit(solution)/shard_map/ppermute | solution.py:774
  422.6 11.9 %collective-permute-start.71 = (bf16[3,192,256]{2,1,0:T(8,128)(2,1)S(1)}, bf16[3,192,256]{2,1,0:T(8,128)(2,1)S(1)}, u32[]{:S(2)}, u32[]{:S(2)}) collective-permute-start(bf16[3,192,256]{2,1,0:T(8,128)(2,1)S(1)} %collective-permute-done.67.refs_1_), channel_id=1, source_target_pairs={{0,1},{1,0},{2,3},{3,2},{4,5},{5,4},{6,7},{7,6},{8,9},{9,8},{10,11... | collective-permute-start | bytes 884744 | tf_op jit(solution)/shard_map/ppermute | solution.py:774
  423.1 11.4 %collective-permute-start.72 = (bf16[3,192,256]{2,1,0:T(8,128)(2,1)S(1)}, bf16[3,192,256]{2,1,0:T(8,128)(2,1)S(1)}, u32[]{:S(2)}, u32[]{:S(2)}) collective-permute-start(bf16[3,192,256]{2,1,0:T(8,128)(2,1)S(1)} %collective-permute-done.68.refs_2_), channel_id=1, source_target_pairs={{0,1},{1,0},{2,3},{3,2},{4,5},{5,4},{6,7},{7,6},{8,9},{9,8},{10,11... | collective-permute-start | bytes 884744 | tf_op jit(solution)/shard_map/ppermute | solution.py:774
  423.2 11.4 %collective-permute-start.73 = (bf16[3,192,256]{2,1,0:T(8,128)(2,1)S(1)}, bf16[3,192,256]{2,1,0:T(8,128)(2,1)S(1)}, u32[]{:S(2)}, u32[]{:S(2)}) collective-permute-start(bf16[3,192,256]{2,1,0:T(8,128)(2,1)S(1)} %collective-permute-done.69.refs_3_), channel_id=1, source_target_pairs={{0,1},{1,0},{2,3},{3,2},{4,5},{5,4},{6,7},{7,6},{8,9},{9,8},{10,11... | collective-permute-start | bytes 884744 | tf_op jit(solution)/shard_map/ppermute | solution.py:774
  (51 other events, 706.7 us)
